TPU v7x, 256 devices: a whole 4x4x8 slice. The times are simulated.
256 devices in a mesh: section: 8 (over y_hi, x), seq: 32 (over z, y_lo, core).
Axes of the slice: x: 4, y: 4 (y_hi: 2, y_lo: 2; y = y_hi * 2 + y_lo), z: 8, core: 2. Of those that a mesh axis runs over, the one named last changes fastest.
Arguments:
- features: bfloat16 [4096, 8192], P('seq', 'section'), may hold values from -600 to 600
- norm_gain: float32 [8192], P('section'), may hold values from 0.1 to 1.9
- kv_weight: bfloat16 [8192, 2048], P('section'), may hold values from -0.09375 to 0.09375
- queries: bfloat16 [3, 64, 4096, 128], P(None, 'section', 'seq'), may hold values from -64 to 64
- step_kv: bfloat16 [3, 8, 4096, 256], P(None, 'section', 'seq'), may hold values from -6 to 6
- doc_ids: int32 [4096], replicated, may hold values from 0 to 7, never falling along the last dimension, each value on 1 to 3072 neighbouring positions
- block_lists: int32 [3, 64, 16], replicated, may hold values from 0 to 63, as said below
Outputs:
- attended: bfloat16 [3, 64, 4096, 128], P(None, 'section', 'seq')
- kv_cache: bfloat16 [8, 4096, 256], P('section', 'seq')
Inputs may be any that keep to these rules, and one draw needn't show every extreme that they name: `doc_ids`: document numbers never fall along the tokens; a document holds 1 to 3072 tokens, and one holds exactly 3072. `block_lists`: entry [k, b, 0] is b itself; every entry of row b is at most b; entries may repeat.
All inputs are finite; a program needn't handle non-finite values.
Results may differ from a plain program's by a relative error of at most 0.0084.
Values may be sent and summed in bfloat16 or wider, within the bound.
No kernel may reach another device: no remote copies, remote signals or barrier semaphores. Data moves between devices by JAX's collectives and lax.ppermute only.
A program may use at most 128 MiB of HBM per device.

v0:
```python
import functools
import math

import jax
import jax.numpy as jnp
from jax import lax
from jax.experimental import pallas as pl
from jax.experimental.pallas import tpu as pltpu
from jax.sharding import PartitionSpec as P

HEAD = 128
BLK = 64
LIST = 16
DOCS = 8
HIDDEN = -1e30
FAR = 1 << 24
EXTRA = 8
CHUNK = 128
NEAR_ROWS = 512
FAR_ROWS = 640
LINE = 128
COUNTS = 64
NEAR_SIZES = (4, 8, 12, 16)
FAR_SIZES = (0, 2, 4, 6, 8, 16)

VMEM_ALL = 60 << 20


def project_kernel(feat, gain, weight, out, scaled, tail):
    tokens = feat.shape[0]

    @pl.when(pl.program_id(0) == 0)
    def _():
        x = feat[...].astype(jnp.float32)
        g = x * gain[...]
        high = g.astype(jnp.bfloat16)
        scaled[:tokens] = high
        scaled[tokens:] = (g - high.astype(jnp.float32)).astype(jnp.bfloat16)
        total = jnp.sum(x * x, axis=1, keepdims=True)
        row = jnp.broadcast_to(total, (tokens, 128)).T[:EXTRA]
        top = row.astype(jnp.bfloat16).astype(jnp.float32)
        which = lax.broadcasted_iota(jnp.int32, (EXTRA, 128), 0)
        tail[...] = jnp.where(which == 0, top, jnp.where(which == 1, row - top, 0.0)).astype(jnp.bfloat16)

    product = jnp.dot(scaled[...], weight[...], preferred_element_type=jnp.float32)
    product = (product[:tokens] + product[tokens:]).astype(jnp.bfloat16)
    cols = out.shape[2]
    for j in range(out.shape[0]):
        out[j, :tokens, :] = product[:, j * cols : (j + 1) * cols]
        out[j, tokens:, :128] = tail[...]
        out[j, tokens:, 128:] = jnp.zeros_like(tail)


def project(features, norm_gain, kv_weight, heads):
    tokens, width = features.shape
    cols = kv_weight.shape[1] // heads
    grid = 2
    return pl.pallas_call(
        project_kernel,
        grid=(grid,),
        in_specs=[
            pl.BlockSpec((tokens, width), lambda i: (0, 0)),
            pl.BlockSpec((1, width), lambda i: (0, 0)),
            pl.BlockSpec((width, kv_weight.shape[1] // grid), lambda i: (0, i)),
        ],
        out_specs=pl.BlockSpec((heads // grid, tokens + EXTRA, cols), lambda i: (i, 0, 0)),
        out_shape=jax.ShapeDtypeStruct((heads, tokens + EXTRA, cols), jnp.bfloat16),
        scratch_shapes=[
            pltpu.VMEM((2 * tokens, width), jnp.bfloat16),
            pltpu.VMEM((EXTRA, 128), jnp.bfloat16),
        ],
        compiler_params=pltpu.CompilerParams(vmem_limit_bytes=VMEM_ALL),
        name="project",
    )(features, norm_gain.reshape(1, width), kv_weight)


def reduce_kernel(width, parts, out, work):
    tokens = out.shape[0]
    total = jnp.sum(parts[:, tokens:, :128].astype(jnp.float32), axis=0)
    squares = jnp.broadcast_to(total[0:1] + total[1:2], (128, tokens)).T
    inverse = lax.rsqrt(squares / width + 1e-05)
    for half in range(2):
        cols = slice(half * 128, half * 128 + 128)
        kept = parts[0, :tokens, cols].astype(jnp.float32)
        for s in range(1, parts.shape[0]):
            kept = kept + parts[s, :tokens, cols].astype(jnp.float32)
        kept = (kept * inverse).astype(jnp.bfloat16)
        out[:, cols] = kept
        work[:, cols] = kept


def prepare_kernel(blocks_dev, place, lists, docs, table, seen):
    t = place[0]
    z = t // 4
    low = lax.rem(t, 4)
    units = lists.shape[0]
    d = docs[...]
    starts = [0] + [jnp.sum((d < doc).astype(jnp.int32)) for doc in range(1, DOCS)]
    for doc in range(DOCS):
        table[units * LINE + doc] = starts[doc]
    for c in range(seen.shape[0]):
        seen[c] = -1

    def unit_lists(u, carry):
        block = t * blocks_dev + lax.rem(u, blocks_dev)
        first = block * BLK
        begin = 0
        for doc in range(1, DOCS):
            begin = jnp.where(starts[doc] <= first, starts[doc], begin)
        least = begin // BLK
        base = u * LINE
        for e in range(LIST):
            table[base + e] = 0
            table[base + LIST + e] = FAR
            table[base + 2 * LIST + e] = 0
            table[base + 3 * LIST + e] = FAR
        near = 0
        far = 0
        for e in range(LIST):
            c = lists[u, e]
            keep = (c >= least) & (seen[c] != u)
            seen[c] = u
            away = z - c // 8
            x = lax.rem(c // 2, 4) ^ low
            inner = lax.rem(c, 2) * BLK
            y = x >> 1
            core = x & 1
            is_near = (away <= 1) | (y == 0)
            slot = jnp.where(away <= 3, away - 2, 8 - away)
            far_row = core * FAR_ROWS + slot * CHUNK + inner
            near_row = core * (NEAR_ROWS + FAR_ROWS) + inner
            near_row += jnp.where(away <= 1, away * (2 * CHUNK) + y * CHUNK, NEAR_ROWS + slot * CHUNK)
            at = base + jnp.where(is_near, near, 2 * LIST + far)
            row = jnp.where(is_near, near_row, far_row)
            table[at] = jnp.where(keep, row, 0)
            table[at + LIST] = jnp.where(keep, c * BLK, FAR)
            near = near + (keep & is_near).astype(jnp.int32)
            far = far + (keep & ~is_near).astype(jnp.int32)
        counts = units * LINE + COUNTS + u
        table[counts] = near
        table[counts + units] = far
        return carry

    lax.fori_loop(0, units, unit_lists, 0)


def scores(blocks, base, block, extra, begins, table, queries, held):
    pieces = [held[pl.ds(pl.multiple_of(table[base + e], BLK), BLK), :] for e in range(blocks)]
    pieces += [rows for rows, _ in extra]
    kv = jnp.concatenate(pieces, axis=0)
    lane = lax.rem(lax.broadcasted_iota(jnp.int32, (1, 128), 1), BLK)
    sub = lax.broadcasted_iota(jnp.int32, (BLK, 128), 0)
    pos_i = block * BLK + lane
    masks = []
    for e in range(blocks):
        pos_j = table[base + LIST + e] + sub
        masks.append((pos_j >= begins) & (pos_j <= pos_i))
    masks += [(sub == lane) & allowed for _, allowed in extra]
    mask = jnp.concatenate(masks, axis=0)
    mask = jnp.concatenate([mask] * (queries.shape[0] // 128), axis=1)
    s = lax.dot_general(kv[:, :HEAD], queries, (((1,), (1,)), ((), ())), preferred_element_type=jnp.float32)
    return jnp.where(mask, s, HIDDEN), kv[:, HEAD:]


def weigh(p, values):
    return lax.dot_general(
        values, p.astype(jnp.bfloat16), (((0,), (0,)), ((), ())), preferred_element_type=jnp.float32
    )


def unit_state(blocks_dev, u, t, table, q):
    steps, heads, tokens, head_dim = q.shape
    units = steps * blocks_dev
    k = u // blocks_dev
    half = lax.rem(u, blocks_dev)
    block = t * blocks_dev + half
    rows = pl.ds(pl.multiple_of(half * BLK, BLK), BLK)
    queries = q[k, :, rows, :].reshape(heads * BLK, head_dim)
    pos_i = block * BLK + lax.rem(lax.broadcasted_iota(jnp.int32, (1, 128), 1), BLK)
    begins = jnp.zeros((1, 128), jnp.int32)
    for doc in range(1, DOCS):
        start = table[units * LINE + doc]
        begins = jnp.where(start <= pos_i, start, begins)
    return k, block, rows, queries, begins


def per_size(sizes, n, run):
    least = -1
    for size in sizes:
        pl.when((n > least) & (n <= size))(functools.partial(run, size))
        least = size


SCALE = math.log2(math.e) / math.sqrt(HEAD)


def hold(held, parts):
    row = 0
    for part in parts:
        held[row : row + part.shape[0]] = part[...]
        row += part.shape[0]


def near_kernel(blocks_dev, place, table, q, own, mine, theirs, state, sums, held):
    t = place[0]
    units = q.shape[0] * blocks_dev
    hold(held, (mine, theirs))

    def body(u, carry):
        k, block, rows, queries, begins = unit_state(blocks_dev, u, t, table, q)

        def run(size):
            extra = [(own[m, 0, rows, :], m <= k) for m in range(own.shape[0])]
            s, values = scores(size, u * LINE, block, extra, begins, table, queries, held)
            top = jnp.max(s, axis=0, keepdims=True)
            p = jnp.exp2((s - top) * SCALE)
            sums[u, 0:1] = top
            sums[u, 1:2] = jnp.sum(p, axis=0, keepdims=True)
            state[u] = weigh(p, values)

        per_size(NEAR_SIZES, table[units * LINE + COUNTS + u], run)
        return carry

    lax.fori_loop(0, units, body, 0)


def far_kernel(blocks_dev, place, table, q, state, sums, mine, theirs, out, held, result, sems):
    t = place[0]
    steps, heads, tokens, head_dim = q.shape
    units = steps * blocks_dev
    hold(held, (mine, theirs))

    def copy(u):
        rows = pl.ds(pl.multiple_of(lax.rem(u, blocks_dev) * BLK, BLK), BLK)
        return pltpu.make_async_copy(result.at[u], out.at[u // blocks_dev, :, rows, :], sems.at[u])

    def body(u, carry):
        k, block, rows, queries, begins = unit_state(blocks_dev, u, t, table, q)

        def run(size):
            top, total, summed = sums[u, 0:1], sums[u, 1:2], state[u]
            if size:
                s, values = scores(size, u * LINE + 2 * LIST, block, [], begins, table, queries, held)
                new_top = jnp.maximum(top, jnp.max(s, axis=0, keepdims=True))
                p = jnp.exp2((s - new_top) * SCALE)
                factor = jnp.exp2((top - new_top) * SCALE)
                total = total * factor + jnp.sum(p, axis=0, keepdims=True)
                summed = summed * factor + weigh(p, values)
            result[u] = (summed / total).T.astype(jnp.bfloat16).reshape(heads, BLK, head_dim)

        per_size(FAR_SIZES, table[units * LINE + COUNTS + units + u], run)
        copy(u).start()
        return carry

    lax.fori_loop(0, units, body, 0)
    lax.fori_loop(0, units, lambda u, c: (copy(u).wait(), c)[1], 0)


SMEM_ALL = pl.BlockSpec(memory_space=pltpu.SMEM)
VMEM_WHOLE = pl.BlockSpec(memory_space=pltpu.VMEM)


def limit(mib):
    return pltpu.CompilerParams(vmem_limit_bytes=mib << 20)


def attend_near(place, table, queries, step_kv, parts, blocks_dev):
    steps, heads, tokens, head_dim = queries.shape
    units = steps * blocks_dev
    return pl.pallas_call(
        functools.partial(near_kernel, blocks_dev),
        in_specs=[SMEM_ALL, SMEM_ALL] + [VMEM_WHOLE] * (2 + len(parts)),
        out_specs=[VMEM_WHOLE, VMEM_WHOLE],
        out_shape=[
            jax.ShapeDtypeStruct((units, head_dim, heads * BLK), jnp.float32),
            jax.ShapeDtypeStruct((units, 8, heads * BLK), jnp.float32),
        ],
        scratch_shapes=[pltpu.VMEM((2 * (NEAR_ROWS + FAR_ROWS), 2 * head_dim), jnp.bfloat16)],
        compiler_params=limit(24),
        name="attend_near",
    )(place, table, queries, step_kv, *parts)


def attend_far(place, table, queries, state, sums, mine, theirs, blocks_dev):
    steps, heads, tokens, head_dim = queries.shape
    units = steps * blocks_dev
    return pl.pallas_call(
        functools.partial(far_kernel, blocks_dev),
        in_specs=[SMEM_ALL, SMEM_ALL] + [VMEM_WHOLE] * 5,
        out_specs=pl.BlockSpec(memory_space=pl.ANY),
        out_shape=jax.ShapeDtypeStruct(queries.shape, jnp.bfloat16),
        scratch_shapes=[
            pltpu.VMEM((2 * FAR_ROWS, 2 * head_dim), jnp.bfloat16),
            pltpu.VMEM((units, heads, BLK, head_dim), jnp.bfloat16),
            pltpu.SemaphoreType.DMA((units,)),
        ],
        compiler_params=limit(24),
        name="attend_far",
    )(place, table, queries, state, sums, mine, theirs)


def per_device(features, norm_gain, kv_weight, queries, step_kv, doc_ids, block_lists):
    sections = lax.axis_size("section")
    seqs = lax.axis_size("seq")
    step_total, local_heads, tok_dev, head_dim = queries.shape
    blocks_dev = tok_dev // BLK
    units = step_total * blocks_dev
    place = lax.axis_index("seq").reshape(1).astype(jnp.int32)

    partial = project(features, norm_gain, kv_weight, sections)
    parts = lax.all_to_all(partial, "section", 0, 0, tiled=True)
    lists = lax.dynamic_slice_in_dim(block_lists, place[0] * blocks_dev, blocks_dev, 1).reshape(units, LIST)
    table = pl.pallas_call(
        functools.partial(prepare_kernel, blocks_dev),
        in_specs=[SMEM_ALL, SMEM_ALL, VMEM_WHOLE],
        out_specs=SMEM_ALL,
        out_shape=jax.ShapeDtypeStruct(((units + 1) * LINE,), jnp.int32),
        scratch_shapes=[pltpu.SMEM((block_lists.shape[1],), jnp.int32)],
        compiler_params=limit(4),
        name="prepare",
    )(place, lists, doc_ids.reshape(-1, 128))

    parts, table = lax.optimization_barrier((parts, table))
    kv_cache, kv = pl.pallas_call(
        functools.partial(reduce_kernel, float(features.shape[1] * sections)),
        out_shape=[jax.ShapeDtypeStruct((tok_dev, 2 * head_dim), jnp.bfloat16)] * 2,
        compiler_params=limit(8),
        name="reduce",
    )(parts)

    every = range(seqs)

    def along_z(x, levels):
        return lax.ppermute(x, "seq", [(i, (i + 4 * levels) % seqs) for i in every])

    def along_y(x):
        return lax.ppermute(x, "seq", [(i, i ^ 2) for i in every])

    def along_core(x):
        return lax.ppermute(x, "seq", [(i, i ^ 1) for i in every])

    def join(*arrays):
        return jnp.concatenate(arrays, axis=0)

    up1 = along_z(kv, 1)
    down1 = along_z(kv, -1)
    own_y = along_y(kv)
    low, high = join(kv, up1), join(kv, down1)
    low, high = lax.optimization_barrier((low, high))
    up23 = along_z(low, 2)
    down23 = along_z(high, -2)
    kept, _, _, _ = lax.optimization_barrier((kv, low, high, own_y))
    up4 = along_z(kept, 4)
    up1_y = along_y(up1)
    column = join(up23, down23, up4)
    far = along_y(column)
    near = join(kv, own_y, up1, up1_y, column)
    state, sums = attend_near(place, table, queries, step_kv, (near, along_core(near)), blocks_dev)
    far, state, sums = lax.optimization_barrier((far, state, sums))
    attended = attend_far(place, table, queries, state, sums, far, along_core(far), blocks_dev)
    return attended, kv_cache[None]


def solution(mesh):
    in_specs = (
        P("seq", "section"),
        P("section"),
        P("section", None),
        P(None, "section", "seq", None),
        P(None, "section", "seq", None),
        P(),
        P(),
    )
    out_specs = (P(None, "section", "seq", None), P("section", "seq", None))
    return jax.shard_map(per_device, mesh=mesh, in_specs=in_specs, out_specs=out_specs, check_vma=False)
```

profile of v0, /device:TPU:1, one launch (start us, length us, event | category | flops | bytes accessed | tf_op | source)
XLA Modules:
  0.0 64.5 jit_solution(17411803981560832448)
XLA Ops:
  0.7 4.1 %project.1 = bf16[8,136,256]{2,1,0:T(8,128)(2,1)} custom-call(bf16[128,1024]{1,0:T(8,128)(2,1)} %feat.1, f32[1,1024]{1,0:T(1,128)} %bitcast.5, bf16[1024,2048]{1,0:T(8,128)(2,1)} %weight.1), custom_call_target="tpu_custom_call" | custom-call | tf_op jit(solution)/shard_map/project/pallas_call | solution.py:58
  4.8 7.5 %all-to-all-start = ((bf16[8,136,256]{2,1,0:T(8,128)(2,1)}), bf16[8,136,256]{2,1,0:T(8,128)(2,1)S(1)}, u32[]{:S(2)}, u32[]{:S(2)}) async-start(bf16[8,136,256]{2,1,0:T(8,128)(2,1)} %project.1), calls=%async_computation | async-start | bytes 1114112 | tf_op jit(solution)/shard_map/all_to_all | solution.py:311
  12.3 0.1 copy.9
  12.4 3.9 %prepare.1.table = s32[896]{0:T(1024)S(1)} custom-call(s32[1]{0:T(128)} %bitcast.place, s32[6,16]{1,0:T(8,128)S(1)} %reshape.18.lists, s32[32,128]{1,0:T(8,128)S(1)} %bitcast.4), custom_call_target="tpu_custom_call" | custom-call | tf_op jit(solution)/shard_map/prepare/pallas_call | solution.py:313
  16.3 8.0 %all-to-all-done.parts = bf16[8,136,256]{2,1,0:T(8,128)(2,1)S(1)} async-done(((bf16[8,136,256]{2,1,0:T(8,128)(2,1)}), bf16[8,136,256]{2,1,0:T(8,128)(2,1)S(1)}, u32[]{:S(2)}, u32[]{:S(2)}) %all-to-all-start) | async-done | bytes 557088 | tf_op jit(solution)/shard_map/all_to_all | solution.py:311
  24.3 0.8 %reduce.1 = (bf16[128,256]{1,0:T(8,128)(2,1)}, bf16[128,256]{1,0:T(8,128)(2,1)S(1)}) custom-call(bf16[8,136,256]{2,1,0:T(8,128)(2,1)S(1)} %all-to-all-done.parts), custom_call_target="tpu_custom_call" | custom-call | tf_op jit(solution)/shard_map/reduce/pallas_call | solution.py:324
  25.1 0.4 collective-permute-start.4
  25.5 5.6 %collective-permute-start.1 = (bf16[128,256]{1,0:T(8,128)(2,1)S(1)}, bf16[128,256]{1,0:T(8,128)(2,1)S(1)}, u32[]{:S(2)}, u32[]{:S(2)}) collective-permute-start(bf16[128,256]{1,0:T(8,128)(2,1)S(1)} %get-tuple-element.19), channel_id=1, source_target_pairs={{0,28},{1,29},{2,30},{3,31},{4,0},{5,1},{6,2},{7,3},{8,4},{9,5},{1... | collective-permute-start | bytes 196616 | tf_op jit(solution)/shard_map/ppermute | solution.py:334
  31.0 1.3 %collective-permute-done.1 = bf16[128,256]{1,0:T(8,128)(2,1)S(1)} collective-permute-done((bf16[128,256]{1,0:T(8,128)(2,1)S(1)}, bf16[128,256]{1,0:T(8,128)(2,1)S(1)}, u32[]{:S(2)}, u32[]{:S(2)}) %collective-permute-start.1) | collective-permute-done | bytes 65568 | tf_op jit(solution)/shard_map/ppermute | solution.py:334
  32.4 3.0 %collective-permute-done = bf16[128,256]{1,0:T(8,128)(2,1)S(1)} collective-permute-done((bf16[128,256]{1,0:T(8,128)(2,1)S(1)}, bf16[128,256]{1,0:T(8,128)(2,1)S(1)}, u32[]{:S(2)}, u32[]{:S(2)}) %collective-permute-start) | collective-permute-done | bytes 65568 | tf_op jit(solution)/shard_map/ppermute | solution.py:334
  35.4 0.1 collective-permute-start.2
  35.5 3.6 %collective-permute-start.3 = (bf16[256,256]{1,0:T(8,128)(2,1)S(1)}, bf16[256,256]{1,0:T(8,128)(2,1)S(1)}, u32[]{:S(2)}, u32[]{:S(2)}) collective-permute-start(bf16[256,256]{1,0:T(8,128)(2,1)S(1)} %get-tuple-element.18), channel_id=1, source_target_pairs={{0,24},{1,25},{2,26},{3,27},{4,28},{5,29},{6,30},{7,31},{8,0},{9,1... | collective-permute-start | bytes 393224 | tf_op jit(solution)/shard_map/ppermute | solution.py:334
  39.0 1.3 %collective-permute-start.5 = (bf16[128,256]{1,0:T(8,128)(2,1)S(1)}, bf16[128,256]{1,0:T(8,128)(2,1)S(1)}, u32[]{:S(2)}, u32[]{:S(2)}) collective-permute-start(bf16[128,256]{1,0:T(8,128)(2,1)S(1)} %get-tuple-element.19), channel_id=1, source_target_pairs={{0,16},{1,17},{2,18},{3,19},{4,20},{5,21},{6,22},{7,23},{8,24},{9,... | collective-permute-start | bytes 196616 | tf_op jit(solution)/shard_map/ppermute | solution.py:334
  40.4 1.1 %collective-permute-start.7 = (bf16[128,256]{1,0:T(8,128)(2,1)S(1)}, bf16[128,256]{1,0:T(8,128)(2,1)S(1)}, u32[]{:S(2)}, u32[]{:S(2)}) collective-permute-start(bf16[128,256]{1,0:T(8,128)(2,1)S(1)} %collective-permute-done), channel_id=1, source_target_pairs={{0,2},{1,3},{2,0},{3,1},{4,6},{5,7},{6,4},{7,5},{8,10},{9,11},{10,... | collective-permute-start | bytes 196616 | tf_op jit(solution)/shard_map/ppermute | solution.py:337
  41.5 2.3 %collective-permute-done.7 = bf16[128,256]{1,0:T(8,128)(2,1)S(1)} collective-permute-done((bf16[128,256]{1,0:T(8,128)(2,1)S(1)}, bf16[128,256]{1,0:T(8,128)(2,1)S(1)}, u32[]{:S(2)}, u32[]{:S(2)}) %collective-permute-start.7) | collective-permute-done | bytes 65568 | tf_op jit(solution)/shard_map/ppermute | solution.py:337
  43.8 3.5 %collective-permute-done.5 = bf16[128,256]{1,0:T(8,128)(2,1)S(1)} collective-permute-done((bf16[128,256]{1,0:T(8,128)(2,1)S(1)}, bf16[128,256]{1,0:T(8,128)(2,1)S(1)}, u32[]{:S(2)}, u32[]{:S(2)}) %collective-permute-start.5) | collective-permute-done | bytes 65568 | tf_op jit(solution)/shard_map/ppermute | solution.py:334
  47.4 3.1 %collective-permute-start.8 = (bf16[1152,256]{1,0:T(8,128)(2,1)S(1)}, bf16[1152,256]{1,0:T(8,128)(2,1)S(1)}, u32[]{:S(2)}, u32[]{:S(2)}) collective-permute-start(bf16[1152,256]{1,0:T(8,128)(2,1)S(1)} %constant_dynamic-update-slice_fusion.mine), channel_id=1, source_target_pairs={{0,1},{1,0},{2,3},{3,2},{4,5},{5,4},{6,7},{7,6},{8,9},{9,8},{10,11... | collective-permute-start | bytes 1769480 | tf_op jit(solution)/shard_map/ppermute | solution.py:340
  50.5 1.2 %collective-permute-start.6 = (bf16[640,256]{1,0:T(8,128)(2,1)S(1)}, bf16[640,256]{1,0:T(8,128)(2,1)S(1)}, u32[]{:S(2)}, u32[]{:S(2)}) collective-permute-start(bf16[640,256]{1,0:T(8,128)(2,1)S(1)} %pad_maximum_fusion), channel_id=1, source_target_pairs={{0,2},{1,3},{2,0},{3,1},{4,6},{5,7},{6,4},{7,5},{8,10},{9,11},{10,... | collective-permute-start | bytes 983048 | tf_op jit(solution)/shard_map/ppermute | solution.py:337
  51.7 0.4 collective-permute-done.8.theirs
  52.1 4.8 %attend_near.1 = (f32[6,128,512]{2,1,0:T(8,128)S(1)}, f32[6,8,512]{2,1,0:T(8,128)S(1)}) custom-call(s32[1]{0:T(128)} %bitcast.place, s32[896]{0:T(1024)S(1)} %prepare.1.table, bf16[3,8,128,128]{3,2,1,0:T(8,128)(2,1)S(1)} %copy-done.1, bf16[3,1,128,256]{3,2,1,0:T(8,128)(2,1)S(1)} %copy-done.2, bf16[1152,256]{1,0:T(8,128)(2,1)S(1)} %constant_dynamic-update-slice_fusion.mine, ...), custom_call_target="tpu_custom_call" | custom-call | tf_op jit(solution)/shard_map/attend_near/pallas_call | solution.py:270
  56.9 3.0 %collective-permute-done.6.mine = bf16[640,256]{1,0:T(8,128)(2,1)S(1)} collective-permute-done((bf16[640,256]{1,0:T(8,128)(2,1)S(1)}, bf16[640,256]{1,0:T(8,128)(2,1)S(1)}, u32[]{:S(2)}, u32[]{:S(2)}) %collective-permute-start.6) | collective-permute-done | bytes 327712 | tf_op jit(solution)/shard_map/ppermute | solution.py:337
  59.9 0.8 %collective-permute-start.9 = (bf16[640,256]{1,0:T(8,128)(2,1)S(1)}, bf16[640,256]{1,0:T(8,128)(2,1)S(1)}, u32[]{:S(2)}, u32[]{:S(2)}) collective-permute-start(bf16[640,256]{1,0:T(8,128)(2,1)S(1)} %collective-permute-done.6.mine), channel_id=1, source_target_pairs={{0,1},{1,0},{2,3},{3,2},{4,5},{5,4},{6,7},{7,6},{8,9},{9,8},{10,11... | collective-permute-start | bytes 983048 | tf_op jit(solution)/shard_map/ppermute | solution.py:340
  60.7 1.3 %collective-permute-done.9.theirs = bf16[640,256]{1,0:T(8,128)(2,1)S(1)} collective-permute-done((bf16[640,256]{1,0:T(8,128)(2,1)S(1)}, bf16[640,256]{1,0:T(8,128)(2,1)S(1)}, u32[]{:S(2)}, u32[]{:S(2)}) %collective-permute-start.9) | collective-permute-done | bytes 327712 | tf_op jit(solution)/shard_map/ppermute | solution.py:340
  62.0 2.4 %attend_far.1 = bf16[3,8,128,128]{3,2,1,0:T(8,128)(2,1)} custom-call(s32[1]{0:T(128)} %bitcast.place, s32[896]{0:T(1024)S(1)} %prepare.1.table, bf16[3,8,128,128]{3,2,1,0:T(8,128)(2,1)S(1)} %copy-done.1, f32[6,128,512]{2,1,0:T(8,128)S(1)} %get-tuple-element.22.state, f32[6,8,512]{2,1,0:T(8,128)S(1)} %get-tuple-element.23.sums, ...), custom_call_target="tpu_custom_call" | custom-call | tf_op jit(solution)/shard_map/attend_far/pallas_call | solution.py:287
  (23 shorter events, 0.2 us)
Async XLA Ops:
  0.6 11.6 %copy-start = (s32[3,64,16]{1,2,0:T(8,128)S(1)}, s32[3,64,16]{1,2,0:T(8,128)}, u32[]{:S(2)}) copy-start(s32[3,64,16]{1,2,0:T(8,128)} %param.13) | copy-start | bytes 36868
  0.6 11.8 %copy-start.3 = (s32[4096]{0:T(1024)S(1)}, s32[4096]{0:T(1024)}, u32[]{:S(2)}) copy-start(s32[4096]{0:T(1024)} %param.12) | copy-start | bytes 49156
  0.7 51.4 %copy-start.1 = (bf16[3,8,128,128]{3,2,1,0:T(8,128)(2,1)S(1)}, bf16[3,8,128,128]{3,2,1,0:T(8,128)(2,1)}, u32[]{:S(2)}) copy-start(bf16[3,8,128,128]{3,2,1,0:T(8,128)(2,1)} %q.3) | copy-start | bytes 2359300
  0.7 51.4 %copy-start.2 = (bf16[3,1,128,256]{3,2,1,0:T(8,128)(2,1)S(1)}, bf16[3,1,128,256]{3,2,1,0:T(8,128)(2,1)}, u32[]{:S(2)}) copy-start(bf16[3,1,128,256]{3,2,1,0:T(8,128)(2,1)} %own.1) | copy-start | bytes 589828
  4.8 19.5 %all-to-all-start = ((bf16[8,136,256]{2,1,0:T(8,128)(2,1)}), bf16[8,136,256]{2,1,0:T(8,128)(2,1)S(1)}, u32[]{:S(2)}, u32[]{:S(2)}) async-start(bf16[8,136,256]{2,1,0:T(8,128)(2,1)} %project.1), calls=%async_computation | async-start | bytes 1114112 | tf_op jit(solution)/shard_map/all_to_all | solution.py:311
  25.1 14.0 %collective-permute-start.4 = (bf16[128,256]{1,0:T(8,128)(2,1)S(1)}, bf16[128,256]{1,0:T(8,128)(2,1)S(1)}, u32[]{:S(2)}, u32[]{:S(2)}) collective-permute-start(bf16[128,256]{1,0:T(8,128)(2,1)S(1)} %get-tuple-element.19), channel_id=1, source_target_pairs={{0,2},{1,3},{2,0},{3,1},{4,6},{5,7},{6,4},{7,5},{8,10},{9,11},{10,... | collective-permute-start | bytes 196616 | tf_op jit(solution)/shard_map/ppermute | solution.py:337
  25.5 6.9 %collective-permute-start.1 = (bf16[128,256]{1,0:T(8,128)(2,1)S(1)}, bf16[128,256]{1,0:T(8,128)(2,1)S(1)}, u32[]{:S(2)}, u32[]{:S(2)}) collective-permute-start(bf16[128,256]{1,0:T(8,128)(2,1)S(1)} %get-tuple-element.19), channel_id=1, source_target_pairs={{0,28},{1,29},{2,30},{3,31},{4,0},{5,1},{6,2},{7,3},{8,4},{9,5},{1... | collective-permute-start | bytes 196616 | tf_op jit(solution)/shard_map/ppermute | solution.py:334
  31.0 4.3 %collective-permute-start = (bf16[128,256]{1,0:T(8,128)(2,1)S(1)}, bf16[128,256]{1,0:T(8,128)(2,1)S(1)}, u32[]{:S(2)}, u32[]{:S(2)}) collective-permute-start(bf16[128,256]{1,0:T(8,128)(2,1)S(1)} %get-tuple-element.19), channel_id=1, source_target_pairs={{0,4},{1,5},{2,6},{3,7},{4,8},{5,9},{6,10},{7,11},{8,12},{9,13},{1... | collective-permute-start | bytes 196616 | tf_op jit(solution)/shard_map/ppermute | solution.py:334
  35.4 8.4 %collective-permute-start.2 = (bf16[256,256]{1,0:T(8,128)(2,1)S(1)}, bf16[256,256]{1,0:T(8,128)(2,1)S(1)}, u32[]{:S(2)}, u32[]{:S(2)}) collective-permute-start(bf16[256,256]{1,0:T(8,128)(2,1)S(1)} %get-tuple-element.17), channel_id=1, source_target_pairs={{0,8},{1,9},{2,10},{3,11},{4,12},{5,13},{6,14},{7,15},{8,16},{9,17... | collective-permute-start | bytes 393224 | tf_op jit(solution)/shard_map/ppermute | solution.py:334
  35.5 8.3 %collective-permute-start.3 = (bf16[256,256]{1,0:T(8,128)(2,1)S(1)}, bf16[256,256]{1,0:T(8,128)(2,1)S(1)}, u32[]{:S(2)}, u32[]{:S(2)}) collective-permute-start(bf16[256,256]{1,0:T(8,128)(2,1)S(1)} %get-tuple-element.18), channel_id=1, source_target_pairs={{0,24},{1,25},{2,26},{3,27},{4,28},{5,29},{6,30},{7,31},{8,0},{9,1... | collective-permute-start | bytes 393224 | tf_op jit(solution)/shard_map/ppermute | solution.py:334
  39.0 8.3 %collective-permute-start.5 = (bf16[128,256]{1,0:T(8,128)(2,1)S(1)}, bf16[128,256]{1,0:T(8,128)(2,1)S(1)}, u32[]{:S(2)}, u32[]{:S(2)}) collective-permute-start(bf16[128,256]{1,0:T(8,128)(2,1)S(1)} %get-tuple-element.19), channel_id=1, source_target_pairs={{0,16},{1,17},{2,18},{3,19},{4,20},{5,21},{6,22},{7,23},{8,24},{9,... | collective-permute-start | bytes 196616 | tf_op jit(solution)/shard_map/ppermute | solution.py:334
  40.4 3.4 %collective-permute-start.7 = (bf16[128,256]{1,0:T(8,128)(2,1)S(1)}, bf16[128,256]{1,0:T(8,128)(2,1)S(1)}, u32[]{:S(2)}, u32[]{:S(2)}) collective-permute-start(bf16[128,256]{1,0:T(8,128)(2,1)S(1)} %collective-permute-done), channel_id=1, source_target_pairs={{0,2},{1,3},{2,0},{3,1},{4,6},{5,7},{6,4},{7,5},{8,10},{9,11},{10,... | collective-permute-start | bytes 196616 | tf_op jit(solution)/shard_map/ppermute | solution.py:337
  47.4 4.7 %collective-permute-start.8 = (bf16[1152,256]{1,0:T(8,128)(2,1)S(1)}, bf16[1152,256]{1,0:T(8,128)(2,1)S(1)}, u32[]{:S(2)}, u32[]{:S(2)}) collective-permute-start(bf16[1152,256]{1,0:T(8,128)(2,1)S(1)} %constant_dynamic-update-slice_fusion.mine), channel_id=1, source_target_pairs={{0,1},{1,0},{2,3},{3,2},{4,5},{5,4},{6,7},{7,6},{8,9},{9,8},{10,11... | collective-permute-start | bytes 1769480 | tf_op jit(solution)/shard_map/ppermute | solution.py:340
  50.5 9.4 %collective-permute-start.6 = (bf16[640,256]{1,0:T(8,128)(2,1)S(1)}, bf16[640,256]{1,0:T(8,128)(2,1)S(1)}, u32[]{:S(2)}, u32[]{:S(2)}) collective-permute-start(bf16[640,256]{1,0:T(8,128)(2,1)S(1)} %pad_maximum_fusion), channel_id=1, source_target_pairs={{0,2},{1,3},{2,0},{3,1},{4,6},{5,7},{6,4},{7,5},{8,10},{9,11},{10,... | collective-permute-start | bytes 983048 | tf_op jit(solution)/shard_map/ppermute | solution.py:337
  59.9 2.1 %collective-permute-start.9 = (bf16[640,256]{1,0:T(8,128)(2,1)S(1)}, bf16[640,256]{1,0:T(8,128)(2,1)S(1)}, u32[]{:S(2)}, u32[]{:S(2)}) collective-permute-start(bf16[640,256]{1,0:T(8,128)(2,1)S(1)} %collective-permute-done.6.mine), channel_id=1, source_target_pairs={{0,1},{1,0},{2,3},{3,2},{4,5},{5,4},{6,7},{7,6},{8,9},{9,8},{10,11... | collective-permute-start | bytes 983048 | tf_op jit(solution)/shard_map/ppermute | solution.py:340
where the time goes:
time: 64.6 us; the launch traced here: 64.5 us
  starting transfers between devices  24.6 us (38%)
  waiting for transfers between devices  22.9 us (35%)
  Pallas kernels  15.8 us (24%)
  between operations  0.91 us (1%)
    ppermute x5, starting transfers between devices, along_z(): return lax.ppermute(x, 'seq', [(i, (i + 4 * levels) % seqs) for i in every])  10.6 us
    all_to_all x1, waiting for transfers between devices, per_device(): parts = lax.all_to_all(partial, 'section', 0, 0, tiled=True)  7.97 us
    ppermute x5, waiting for transfers between devices, along_z(): return lax.ppermute(x, 'seq', [(i, (i + 4 * levels) % seqs) for i in every])  7.84 us
    all_to_all x1, starting transfers between devices, per_device(): parts = lax.all_to_all(partial, 'section', 0, 0, tiled=True)  7.48 us
    ppermute x3, waiting for transfers between devices, along_y(): return lax.ppermute(x, 'seq', [(i, i ^ 2) for i in every])  5.37 us
    pallas_call x1, Pallas kernels, attend_near(): pl.pallas_call(functools.partial(near_kernel, blocks_dev), in_specs=[SMEM...  4.76 us
    pallas_call x1, Pallas kernels, project(): pl.pallas_call(project_kernel, grid=(grid,), in_specs=[pl.BlockSpec((toke...  4.1 us
    ppermute x2, starting transfers between devices, along_core(): return lax.ppermute(x, 'seq', [(i, i ^ 1) for i in every])  3.89 us
  transfers between devices with their start and end apart: 11, of which 8 were waited for; matrix products, arithmetic and copies ran while one was open for 0% of the time, Pallas kernels for 13%

commit v1 on v0

--- a/solution.py
+++ b/solution.py
@@ -129,7 +129,7 @@
             slot = jnp.where(away <= 3, away - 2, 8 - away)
             far_row = core * FAR_ROWS + slot * CHUNK + inner
             near_row = core * (NEAR_ROWS + FAR_ROWS) + inner
-            near_row += jnp.where(away <= 1, away * (2 * CHUNK) + y * CHUNK, NEAR_ROWS + slot * CHUNK)
+            near_row += jnp.where(away <= 1, y * (2 * CHUNK) + away * CHUNK, NEAR_ROWS + slot * CHUNK)
             at = base + jnp.where(is_near, near, 2 * LIST + far)
             row = jnp.where(is_near, near_row, far_row)
             table[at] = jnp.where(keep, row, 0)
@@ -246,7 +246,7 @@
                 factor = jnp.exp2((top - new_top) * SCALE)
                 total = total * factor + jnp.sum(p, axis=0, keepdims=True)
                 summed = summed * factor + weigh(p, values)
-            result[u] = (summed / total).T.astype(jnp.bfloat16).reshape(heads, BLK, head_dim)
+            result[u] = (summed * (1.0 / total)).T.astype(jnp.bfloat16).reshape(heads, BLK, head_dim)
 
         per_size(FAR_SIZES, table[units * LINE + COUNTS + units + u], run)
         copy(u).start()
@@ -344,17 +344,14 @@
 
     up1 = along_z(kv, 1)
     down1 = along_z(kv, -1)
-    own_y = along_y(kv)
-    low, high = join(kv, up1), join(kv, down1)
-    low, high = lax.optimization_barrier((low, high))
+    low, high = lax.optimization_barrier((join(kv, up1), join(kv, down1)))
     up23 = along_z(low, 2)
     down23 = along_z(high, -2)
-    kept, _, _, _ = lax.optimization_barrier((kv, low, high, own_y))
-    up4 = along_z(kept, 4)
-    up1_y = along_y(up1)
-    column = join(up23, down23, up4)
+    low_y = along_y(low)
+    up4 = along_z(low[:tok_dev], 4)
+    column = lax.optimization_barrier(join(up23, down23, up4))
     far = along_y(column)
-    near = join(kv, own_y, up1, up1_y, column)
+    near = join(low, low_y, column)
     state, sums = attend_near(place, table, queries, step_kv, (near, along_core(near)), blocks_dev)
     far, state, sums = lax.optimization_barrier((far, state, sums))
     attended = attend_far(place, table, queries, state, sums, far, along_core(far), blocks_dev)

time: 64.6 us -> 63.3 us (0.980)
  starting transfers between devices: 24.6 us -> 22.3 us
  waiting for transfers between devices: 22.9 us -> 23.9 us
    ppermute x5, waiting for transfers between devices: 7.84 us -> 10.5 us  [along_z(): return lax.ppermute(x, 'seq', [(i, (i + 4 * levels) % seqs) for i in every])]
    ppermute x3 -> x2, waiting for transfers between devices: 5.37 us -> 2.9 us  [along_y(): return lax.ppermute(x, 'seq', [(i, i ^ 2) for i in every])]
    ppermute x3 -> x2, starting transfers between devices: 2.62 us -> 0.81 us  [along_y(): return lax.ppermute(x, 'seq', [(i, i ^ 2) for i in every])]
    ppermute x5, starting transfers between devices: 10.6 us -> 9.36 us  [along_z(): return lax.ppermute(x, 'seq', [(i, (i + 4 * levels) % seqs) for i in every])]
    ppermute x2, waiting for transfers between devices: 1.71 us -> 2.47 us  [along_core(): return lax.ppermute(x, 'seq', [(i, i ^ 1) for i in every])]
    ppermute x2, starting transfers between devices: 3.89 us -> 4.54 us  [along_core(): return lax.ppermute(x, 'seq', [(i, i ^ 1) for i in every])]
  transfers between devices with their start and end apart: 11 -> 10, of which waited for: 8 -> 7; matrix products, arithmetic and copies ran while one was open for 0% -> 0% of each run, Pallas kernels for 13% -> 14%
where the time goes in v1:
time: 63.3 us; the launch traced here: 63.1 us
  waiting for transfers between devices  23.9 us (38%)
  starting transfers between devices  22.3 us (35%)
  Pallas kernels  15.7 us (25%)
  between operations  0.86 us (1%)
    ppermute x5, waiting for transfers between devices, along_z(): return lax.ppermute(x, 'seq', [(i, (i + 4 * levels) % seqs) for i in every])  10.5 us
    ppermute x5, starting transfers between devices, along_z(): return lax.ppermute(x, 'seq', [(i, (i + 4 * levels) % seqs) for i in every])  9.36 us
    all_to_all x1, waiting for transfers between devices, per_device(): parts = lax.all_to_all(partial, 'section', 0, 0, tiled=True)  7.97 us
    all_to_all x1, starting transfers between devices, per_device(): parts = lax.all_to_all(partial, 'section', 0, 0, tiled=True)  7.61 us
    pallas_call x1, Pallas kernels, attend_near(): pl.pallas_call(functools.partial(near_kernel, blocks_dev), in_specs=[SMEM...  4.73 us
    ppermute x2, starting transfers between devices, along_core(): return lax.ppermute(x, 'seq', [(i, i ^ 1) for i in every])  4.54 us
    pallas_call x1, Pallas kernels, project(): pl.pallas_call(project_kernel, grid=(grid,), in_specs=[pl.BlockSpec((toke...  4.02 us
    pallas_call x1, Pallas kernels, per_device(): pl.pallas_call(functools.partial(prepare_kernel, blocks_dev), in_specs=[S...  3.89 us
  transfers between devices with their start and end apart: 10, of which 7 were waited for; matrix products, arithmetic and copies ran while one was open for 0% of the time, Pallas kernels for 14%

profile of v1, /device:TPU:1, one launch (start us, length us, event | category | flops | bytes accessed | tf_op | source)
XLA Modules:
  0.0 63.1 jit_solution(7641666730628138137)
XLA Ops:
  0.6 0.0 copy-start
  0.6 4.0 %project.1 = bf16[8,136,256]{2,1,0:T(8,128)(2,1)} custom-call(bf16[128,1024]{1,0:T(8,128)(2,1)} %feat.1, f32[1,1024]{1,0:T(1,128)} %bitcast.5, bf16[1024,2048]{1,0:T(8,128)(2,1)} %weight.1), custom_call_target="tpu_custom_call" | custom-call | tf_op jit(solution)/shard_map/project/pallas_call | solution.py:58
  4.7 7.6 %all-to-all-start = ((bf16[8,136,256]{2,1,0:T(8,128)(2,1)}), bf16[8,136,256]{2,1,0:T(8,128)(2,1)S(1)}, u32[]{:S(2)}, u32[]{:S(2)}) async-start(bf16[8,136,256]{2,1,0:T(8,128)(2,1)} %project.1), calls=%async_computation | async-start | bytes 1114112 | tf_op jit(solution)/shard_map/all_to_all | solution.py:311
  12.3 0.1 constant_dynamic-slice_fusion
  12.4 0.1 copy.9
  12.5 3.9 %prepare.1.table = s32[896]{0:T(1024)S(1)} custom-call(s32[1]{0:T(128)} %bitcast.place, s32[6,16]{1,0:T(8,128)S(1)} %reshape.18.lists, s32[32,128]{1,0:T(8,128)S(1)} %bitcast.4), custom_call_target="tpu_custom_call" | custom-call | tf_op jit(solution)/shard_map/prepare/pallas_call | solution.py:313
  16.4 8.0 %all-to-all-done.parts = bf16[8,136,256]{2,1,0:T(8,128)(2,1)S(1)} async-done(((bf16[8,136,256]{2,1,0:T(8,128)(2,1)}), bf16[8,136,256]{2,1,0:T(8,128)(2,1)S(1)}, u32[]{:S(2)}, u32[]{:S(2)}) %all-to-all-start) | async-done | bytes 557088 | tf_op jit(solution)/shard_map/all_to_all | solution.py:311
  24.3 0.8 %reduce.1 = (bf16[128,256]{1,0:T(8,128)(2,1)}, bf16[128,256]{1,0:T(8,128)(2,1)S(1)}) custom-call(bf16[8,136,256]{2,1,0:T(8,128)(2,1)S(1)} %all-to-all-done.parts), custom_call_target="tpu_custom_call" | custom-call | tf_op jit(solution)/shard_map/reduce/pallas_call | solution.py:324
  25.1 5.6 %collective-permute-start.1 = (bf16[128,256]{1,0:T(8,128)(2,1)S(1)}, bf16[128,256]{1,0:T(8,128)(2,1)S(1)}, u32[]{:S(2)}, u32[]{:S(2)}) collective-permute-start(bf16[128,256]{1,0:T(8,128)(2,1)S(1)} %get-tuple-element.15), channel_id=1, source_target_pairs={{0,28},{1,29},{2,30},{3,31},{4,0},{5,1},{6,2},{7,3},{8,4},{9,5},{1... | collective-permute-start | bytes 196616 | tf_op jit(solution)/shard_map/ppermute | solution.py:334
  30.7 1.3 %collective-permute-done.1 = bf16[128,256]{1,0:T(8,128)(2,1)S(1)} collective-permute-done((bf16[128,256]{1,0:T(8,128)(2,1)S(1)}, bf16[128,256]{1,0:T(8,128)(2,1)S(1)}, u32[]{:S(2)}, u32[]{:S(2)}) %collective-permute-start.1) | collective-permute-done | bytes 65568 | tf_op jit(solution)/shard_map/ppermute | solution.py:334
  32.0 3.0 %collective-permute-done = bf16[128,256]{1,0:T(8,128)(2,1)S(1)} collective-permute-done((bf16[128,256]{1,0:T(8,128)(2,1)S(1)}, bf16[128,256]{1,0:T(8,128)(2,1)S(1)}, u32[]{:S(2)}, u32[]{:S(2)}) %collective-permute-start) | collective-permute-done | bytes 65568 | tf_op jit(solution)/shard_map/ppermute | solution.py:334
  35.0 0.3 collective-permute-start.3
  35.3 2.1 %collective-permute-start.2 = (bf16[256,256]{1,0:T(8,128)(2,1)S(1)}, bf16[256,256]{1,0:T(8,128)(2,1)S(1)}, u32[]{:S(2)}, u32[]{:S(2)}) collective-permute-start(bf16[256,256]{1,0:T(8,128)(2,1)S(1)} %get-tuple-element.16), channel_id=1, source_target_pairs={{0,8},{1,9},{2,10},{3,11},{4,12},{5,13},{6,14},{7,15},{8,16},{9,17... | collective-permute-start | bytes 393224 | tf_op jit(solution)/shard_map/ppermute | solution.py:334
  37.5 1.3 %collective-permute-start.4 = (bf16[128,256]{1,0:T(8,128)(2,1)S(1)}, bf16[128,256]{1,0:T(8,128)(2,1)S(1)}, u32[]{:S(2)}, u32[]{:S(2)}) collective-permute-start(bf16[128,256]{1,0:T(8,128)(2,1)S(1)} %slice.3), channel_id=1, source_target_pairs={{0,16},{1,17},{2,18},{3,19},{4,20},{5,21},{6,22},{7,23},{8,24},{9,... | collective-permute-start | bytes 196616 | tf_op jit(solution)/shard_map/ppermute | solution.py:334
  38.8 0.4 collective-permute-start.6
  39.2 6.2 %collective-permute-done.4 = bf16[128,256]{1,0:T(8,128)(2,1)S(1)} collective-permute-done((bf16[128,256]{1,0:T(8,128)(2,1)S(1)}, bf16[128,256]{1,0:T(8,128)(2,1)S(1)}, u32[]{:S(2)}, u32[]{:S(2)}) %collective-permute-start.4) | collective-permute-done | bytes 65568 | tf_op jit(solution)/shard_map/ppermute | solution.py:334
  45.5 3.7 %collective-permute-start.7 = (bf16[1152,256]{1,0:T(8,128)(2,1)S(1)}, bf16[1152,256]{1,0:T(8,128)(2,1)S(1)}, u32[]{:S(2)}, u32[]{:S(2)}) collective-permute-start(bf16[1152,256]{1,0:T(8,128)(2,1)S(1)} %pad_maximum_fusion.mine), channel_id=1, source_target_pairs={{0,1},{1,0},{2,3},{3,2},{4,5},{5,4},{6,7},{7,6},{8,9},{9,8},{10,11... | collective-permute-start | bytes 1769480 | tf_op jit(solution)/shard_map/ppermute | solution.py:340
  49.1 0.4 collective-permute-start.5
  49.6 1.2 %collective-permute-done.7.theirs = bf16[1152,256]{1,0:T(8,128)(2,1)S(1)} collective-permute-done((bf16[1152,256]{1,0:T(8,128)(2,1)S(1)}, bf16[1152,256]{1,0:T(8,128)(2,1)S(1)}, u32[]{:S(2)}, u32[]{:S(2)}) %collective-permute-start.7) | collective-permute-done | bytes 589856 | tf_op jit(solution)/shard_map/ppermute | solution.py:340
  50.8 4.7 %attend_near.1 = (f32[6,128,512]{2,1,0:T(8,128)S(1)}, f32[6,8,512]{2,1,0:T(8,128)S(1)}) custom-call(s32[1]{0:T(128)} %bitcast.place, s32[896]{0:T(1024)S(1)} %prepare.1.table, bf16[3,8,128,128]{3,2,1,0:T(8,128)(2,1)S(1)} %copy-done.1, bf16[3,1,128,256]{3,2,1,0:T(8,128)(2,1)S(1)} %copy-done.2, bf16[1152,256]{1,0:T(8,128)(2,1)S(1)} %pad_maximum_fusion.mine, ...), custom_call_target="tpu_custom_call" | custom-call | tf_op jit(solution)/shard_map/attend_near/pallas_call | solution.py:270
  55.5 2.9 %collective-permute-done.5.mine = bf16[640,256]{1,0:T(8,128)(2,1)S(1)} collective-permute-done((bf16[640,256]{1,0:T(8,128)(2,1)S(1)}, bf16[640,256]{1,0:T(8,128)(2,1)S(1)}, u32[]{:S(2)}, u32[]{:S(2)}) %collective-permute-start.5) | collective-permute-done | bytes 327712 | tf_op jit(solution)/shard_map/ppermute | solution.py:337
  58.4 0.9 %collective-permute-start.8 = (bf16[640,256]{1,0:T(8,128)(2,1)S(1)}, bf16[640,256]{1,0:T(8,128)(2,1)S(1)}, u32[]{:S(2)}, u32[]{:S(2)}) collective-permute-start(bf16[640,256]{1,0:T(8,128)(2,1)S(1)} %collective-permute-done.5.mine), channel_id=1, source_target_pairs={{0,1},{1,0},{2,3},{3,2},{4,5},{5,4},{6,7},{7,6},{8,9},{9,8},{10,11... | collective-permute-start | bytes 983048 | tf_op jit(solution)/shard_map/ppermute | solution.py:340
  59.3 1.3 %collective-permute-done.8.theirs = bf16[640,256]{1,0:T(8,128)(2,1)S(1)} collective-permute-done((bf16[640,256]{1,0:T(8,128)(2,1)S(1)}, bf16[640,256]{1,0:T(8,128)(2,1)S(1)}, u32[]{:S(2)}, u32[]{:S(2)}) %collective-permute-start.8) | collective-permute-done | bytes 327712 | tf_op jit(solution)/shard_map/ppermute | solution.py:340
  60.6 2.4 %attend_far.1 = bf16[3,8,128,128]{3,2,1,0:T(8,128)(2,1)} custom-call(s32[1]{0:T(128)} %bitcast.place, s32[896]{0:T(1024)S(1)} %prepare.1.table, bf16[3,8,128,128]{3,2,1,0:T(8,128)(2,1)S(1)} %copy-done.1, f32[6,128,512]{2,1,0:T(8,128)S(1)} %get-tuple-element.20.state, f32[6,8,512]{2,1,0:T(8,128)S(1)} %get-tuple-element.21.sums, ...), custom_call_target="tpu_custom_call" | custom-call | tf_op jit(solution)/shard_map/attend_far/pallas_call | solution.py:287
  (16 shorter events, 0.1 us)
Async XLA Ops:
  0.6 11.6 %copy-start = (s32[3,64,16]{1,2,0:T(8,128)S(1)}, s32[3,64,16]{1,2,0:T(8,128)}, u32[]{:S(2)}) copy-start(s32[3,64,16]{1,2,0:T(8,128)} %param.13) | copy-start | bytes 36868
  4.7 7.8 %copy-start.3 = (s32[4096]{0:T(1024)S(1)}, s32[4096]{0:T(1024)}, u32[]{:S(2)}) copy-start(s32[4096]{0:T(1024)} %param.12) | copy-start | bytes 49156
  4.7 19.7 %all-to-all-start = ((bf16[8,136,256]{2,1,0:T(8,128)(2,1)}), bf16[8,136,256]{2,1,0:T(8,128)(2,1)S(1)}, u32[]{:S(2)}, u32[]{:S(2)}) async-start(bf16[8,136,256]{2,1,0:T(8,128)(2,1)} %project.1), calls=%async_computation | async-start | bytes 1114112 | tf_op jit(solution)/shard_map/all_to_all | solution.py:311
  25.1 25.7 %copy-start.1 = (bf16[3,8,128,128]{3,2,1,0:T(8,128)(2,1)S(1)}, bf16[3,8,128,128]{3,2,1,0:T(8,128)(2,1)}, u32[]{:S(2)}) copy-start(bf16[3,8,128,128]{3,2,1,0:T(8,128)(2,1)} %q.3) | copy-start | bytes 2359300
  25.1 25.7 %copy-start.2 = (bf16[3,1,128,256]{3,2,1,0:T(8,128)(2,1)S(1)}, bf16[3,1,128,256]{3,2,1,0:T(8,128)(2,1)}, u32[]{:S(2)}) copy-start(bf16[3,1,128,256]{3,2,1,0:T(8,128)(2,1)} %own.1) | copy-start | bytes 589828
  25.1 6.9 %collective-permute-start.1 = (bf16[128,256]{1,0:T(8,128)(2,1)S(1)}, bf16[128,256]{1,0:T(8,128)(2,1)S(1)}, u32[]{:S(2)}, u32[]{:S(2)}) collective-permute-start(bf16[128,256]{1,0:T(8,128)(2,1)S(1)} %get-tuple-element.15), channel_id=1, source_target_pairs={{0,28},{1,29},{2,30},{3,31},{4,0},{5,1},{6,2},{7,3},{8,4},{9,5},{1... | collective-permute-start | bytes 196616 | tf_op jit(solution)/shard_map/ppermute | solution.py:334
  30.7 4.3 %collective-permute-start = (bf16[128,256]{1,0:T(8,128)(2,1)S(1)}, bf16[128,256]{1,0:T(8,128)(2,1)S(1)}, u32[]{:S(2)}, u32[]{:S(2)}) collective-permute-start(bf16[128,256]{1,0:T(8,128)(2,1)S(1)} %get-tuple-element.15), channel_id=1, source_target_pairs={{0,4},{1,5},{2,6},{3,7},{4,8},{5,9},{6,10},{7,11},{8,12},{9,13},{1... | collective-permute-start | bytes 196616 | tf_op jit(solution)/shard_map/ppermute | solution.py:334
  35.0 10.4 %collective-permute-start.3 = (bf16[256,256]{1,0:T(8,128)(2,1)S(1)}, bf16[256,256]{1,0:T(8,128)(2,1)S(1)}, u32[]{:S(2)}, u32[]{:S(2)}) collective-permute-start(bf16[256,256]{1,0:T(8,128)(2,1)S(1)} %get-tuple-element.17), channel_id=1, source_target_pairs={{0,24},{1,25},{2,26},{3,27},{4,28},{5,29},{6,30},{7,31},{8,0},{9,1... | collective-permute-start | bytes 393224 | tf_op jit(solution)/shard_map/ppermute | solution.py:334
  35.3 10.1 %collective-permute-start.2 = (bf16[256,256]{1,0:T(8,128)(2,1)S(1)}, bf16[256,256]{1,0:T(8,128)(2,1)S(1)}, u32[]{:S(2)}, u32[]{:S(2)}) collective-permute-start(bf16[256,256]{1,0:T(8,128)(2,1)S(1)} %get-tuple-element.16), channel_id=1, source_target_pairs={{0,8},{1,9},{2,10},{3,11},{4,12},{5,13},{6,14},{7,15},{8,16},{9,17... | collective-permute-start | bytes 393224 | tf_op jit(solution)/shard_map/ppermute | solution.py:334
  37.5 7.9 %collective-permute-start.4 = (bf16[128,256]{1,0:T(8,128)(2,1)S(1)}, bf16[128,256]{1,0:T(8,128)(2,1)S(1)}, u32[]{:S(2)}, u32[]{:S(2)}) collective-permute-start(bf16[128,256]{1,0:T(8,128)(2,1)S(1)} %slice.3), channel_id=1, source_target_pairs={{0,16},{1,17},{2,18},{3,19},{4,20},{5,21},{6,22},{7,23},{8,24},{9,... | collective-permute-start | bytes 196616 | tf_op jit(solution)/shard_map/ppermute | solution.py:334
  38.8 6.6 %collective-permute-start.6 = (bf16[256,256]{1,0:T(8,128)(2,1)S(1)}, bf16[256,256]{1,0:T(8,128)(2,1)S(1)}, u32[]{:S(2)}, u32[]{:S(2)}) collective-permute-start(bf16[256,256]{1,0:T(8,128)(2,1)S(1)} %get-tuple-element.16), channel_id=1, source_target_pairs={{0,2},{1,3},{2,0},{3,1},{4,6},{5,7},{6,4},{7,5},{8,10},{9,11},{10,... | collective-permute-start | bytes 393224 | tf_op jit(solution)/shard_map/ppermute | solution.py:337
  45.5 5.3 %collective-permute-start.7 = (bf16[1152,256]{1,0:T(8,128)(2,1)S(1)}, bf16[1152,256]{1,0:T(8,128)(2,1)S(1)}, u32[]{:S(2)}, u32[]{:S(2)}) collective-permute-start(bf16[1152,256]{1,0:T(8,128)(2,1)S(1)} %pad_maximum_fusion.mine), channel_id=1, source_target_pairs={{0,1},{1,0},{2,3},{3,2},{4,5},{5,4},{6,7},{7,6},{8,9},{9,8},{10,11... | collective-permute-start | bytes 1769480 | tf_op jit(solution)/shard_map/ppermute | solution.py:340
  49.1 9.3 %collective-permute-start.5 = (bf16[640,256]{1,0:T(8,128)(2,1)S(1)}, bf16[640,256]{1,0:T(8,128)(2,1)S(1)}, u32[]{:S(2)}, u32[]{:S(2)}) collective-permute-start(bf16[640,256]{1,0:T(8,128)(2,1)S(1)} %pad_maximum_fusion.1), channel_id=1, source_target_pairs={{0,2},{1,3},{2,0},{3,1},{4,6},{5,7},{6,4},{7,5},{8,10},{9,11},{10,... | collective-permute-start | bytes 983048 | tf_op jit(solution)/shard_map/ppermute | solution.py:337
  58.4 2.1 %collective-permute-start.8 = (bf16[640,256]{1,0:T(8,128)(2,1)S(1)}, bf16[640,256]{1,0:T(8,128)(2,1)S(1)}, u32[]{:S(2)}, u32[]{:S(2)}) collective-permute-start(bf16[640,256]{1,0:T(8,128)(2,1)S(1)} %collective-permute-done.5.mine), channel_id=1, source_target_pairs={{0,1},{1,0},{2,3},{3,2},{4,5},{5,4},{6,7},{7,6},{8,9},{9,8},{10,11... | collective-permute-start | bytes 983048 | tf_op jit(solution)/shard_map/ppermute | solution.py:340

commit v2 on v1

--- a/solution.py
+++ b/solution.py
@@ -16,8 +16,11 @@
 FAR = 1 << 24
 EXTRA = 8
 CHUNK = 128
-NEAR_ROWS = 512
-FAR_ROWS = 640
+CLOSE = 512
+RISING = 384
+FALLING = 256
+NEAR_ROWS = CLOSE + RISING + 2 * FALLING
+FAR_ROWS = RISING
 LINE = 128
 COUNTS = 64
 NEAR_SIZES = (4, 8, 12, 16)
@@ -26,48 +29,56 @@
 VMEM_ALL = 60 << 20
 
 
-def project_kernel(feat, gain, weight, out, scaled, tail):
+def project_kernel(feat_hbm, gain_hbm, weight_hbm, out, feat, gain, weight, sems):
     tokens = feat.shape[0]
-
-    @pl.when(pl.program_id(0) == 0)
-    def _():
-        x = feat[...].astype(jnp.float32)
-        g = x * gain[...]
-        high = g.astype(jnp.bfloat16)
-        scaled[:tokens] = high
-        scaled[tokens:] = (g - high.astype(jnp.float32)).astype(jnp.bfloat16)
-        total = jnp.sum(x * x, axis=1, keepdims=True)
-        row = jnp.broadcast_to(total, (tokens, 128)).T[:EXTRA]
-        top = row.astype(jnp.bfloat16).astype(jnp.float32)
-        which = lax.broadcasted_iota(jnp.int32, (EXTRA, 128), 0)
-        tail[...] = jnp.where(which == 0, top, jnp.where(which == 1, row - top, 0.0)).astype(jnp.bfloat16)
-
-    product = jnp.dot(scaled[...], weight[...], preferred_element_type=jnp.float32)
-    product = (product[:tokens] + product[tokens:]).astype(jnp.bfloat16)
+    blocks, _, width = weight.shape
+    small = [
+        pltpu.make_async_copy(feat_hbm, feat, sems.at[blocks]),
+        pltpu.make_async_copy(gain_hbm, gain, sems.at[blocks + 1]),
+    ]
+    copies = [
+        pltpu.make_async_copy(weight_hbm.at[:, pl.ds(j * width, width)], weight.at[j], sems.at[j]) for j in range(blocks)
+    ]
+    for copy in small + copies:
+        copy.start()
+    for copy in small:
+        copy.wait()
+    x = feat[...].astype(jnp.float32)
+    g = x * gain[...]
+    high = g.astype(jnp.bfloat16)
+    both = jnp.concatenate([high, (g - high.astype(jnp.float32)).astype(jnp.bfloat16)], axis=0)
+    total = jnp.sum(x * x, axis=1, keepdims=True)
+    row = jnp.broadcast_to(total, (tokens, 128)).T[:EXTRA]
+    top = row.astype(jnp.bfloat16).astype(jnp.float32)
+    which = lax.broadcasted_iota(jnp.int32, (EXTRA, 128), 0)
+    tail = jnp.where(which == 0, top, jnp.where(which == 1, row - top, 0.0)).astype(jnp.bfloat16)
     cols = out.shape[2]
-    for j in range(out.shape[0]):
-        out[j, :tokens, :] = product[:, j * cols : (j + 1) * cols]
-        out[j, tokens:, :128] = tail[...]
-        out[j, tokens:, 128:] = jnp.zeros_like(tail)
+    for h in range(out.shape[0]):
+        out[h, tokens:, :128] = tail
+        out[h, tokens:, 128:] = jnp.zeros_like(tail)
+    for j, copy in enumerate(copies):
+        copy.wait()
+        product = jnp.dot(both, weight[j], preferred_element_type=jnp.float32)
+        product = (product[:tokens] + product[tokens:]).astype(jnp.bfloat16)
+        for i in range(width // cols):
+            out[j * (width // cols) + i, :tokens, :] = product[:, i * cols : (i + 1) * cols]
 
 
 def project(features, norm_gain, kv_weight, heads):
     tokens, width = features.shape
     cols = kv_weight.shape[1] // heads
-    grid = 2
+    blocks = 4
+    anywhere = pl.BlockSpec(memory_space=pl.ANY)
     return pl.pallas_call(
         project_kernel,
-        grid=(grid,),
-        in_specs=[
-            pl.BlockSpec((tokens, width), lambda i: (0, 0)),
-            pl.BlockSpec((1, width), lambda i: (0, 0)),
-            pl.BlockSpec((width, kv_weight.shape[1] // grid), lambda i: (0, i)),
-        ],
-        out_specs=pl.BlockSpec((heads // grid, tokens + EXTRA, cols), lambda i: (i, 0, 0)),
+        in_specs=[anywhere] * 3,
+        out_specs=pl.BlockSpec(memory_space=pltpu.VMEM),
         out_shape=jax.ShapeDtypeStruct((heads, tokens + EXTRA, cols), jnp.bfloat16),
         scratch_shapes=[
-            pltpu.VMEM((2 * tokens, width), jnp.bfloat16),
-            pltpu.VMEM((EXTRA, 128), jnp.bfloat16),
+            pltpu.VMEM((tokens, width), features.dtype),
+            pltpu.VMEM((1, width), norm_gain.dtype),
+            pltpu.VMEM((blocks, width, kv_weight.shape[1] // blocks), kv_weight.dtype),
+            pltpu.SemaphoreType.DMA((blocks + 2,)),
         ],
         compiler_params=pltpu.CompilerParams(vmem_limit_bytes=VMEM_ALL),
         name="project",
@@ -125,11 +136,14 @@
             inner = lax.rem(c, 2) * BLK
             y = x >> 1
             core = x & 1
-            is_near = (away <= 1) | (y == 0)
-            slot = jnp.where(away <= 3, away - 2, 8 - away)
-            far_row = core * FAR_ROWS + slot * CHUNK + inner
-            near_row = core * (NEAR_ROWS + FAR_ROWS) + inner
-            near_row += jnp.where(away <= 1, y * (2 * CHUNK) + away * CHUNK, NEAR_ROWS + slot * CHUNK)
+            is_near = (away <= 1) | (y == 0) | (away >= 5)
+            near_row = jnp.where(
+                away <= 1,
+                y * (CLOSE // 2) + away * CHUNK,
+                jnp.where(away <= 4, CLOSE + (away - 2) * CHUNK, CLOSE + RISING + y * FALLING + (6 - away) * CHUNK),
+            )
+            near_row += core * NEAR_ROWS + inner
+            far_row = core * FAR_ROWS + (away - 2) * CHUNK + inner
             at = base + jnp.where(is_near, near, 2 * LIST + far)
             row = jnp.where(is_near, near_row, far_row)
             table[at] = jnp.where(keep, row, 0)
@@ -275,7 +289,7 @@
             jax.ShapeDtypeStruct((units, head_dim, heads * BLK), jnp.float32),
             jax.ShapeDtypeStruct((units, 8, heads * BLK), jnp.float32),
         ],
-        scratch_shapes=[pltpu.VMEM((2 * (NEAR_ROWS + FAR_ROWS), 2 * head_dim), jnp.bfloat16)],
+        scratch_shapes=[pltpu.VMEM((2 * NEAR_ROWS, 2 * head_dim), jnp.bfloat16)],
         compiler_params=limit(24),
         name="attend_near",
     )(place, table, queries, step_kv, *parts)
@@ -345,13 +359,14 @@
     up1 = along_z(kv, 1)
     down1 = along_z(kv, -1)
     low, high = lax.optimization_barrier((join(kv, up1), join(kv, down1)))
+    down23 = along_z(high, -2)
     up23 = along_z(low, 2)
-    down23 = along_z(high, -2)
     low_y = along_y(low)
     up4 = along_z(low[:tok_dev], 4)
-    column = lax.optimization_barrier(join(up23, down23, up4))
-    far = along_y(column)
-    near = join(low, low_y, column)
+    falling = join(down23, along_y(down23))
+    rising = join(up23, up4)
+    far = along_y(rising)
+    near = join(low, low_y, rising, falling)
     state, sums = attend_near(place, table, queries, step_kv, (near, along_core(near)), blocks_dev)
     far, state, sums = lax.optimization_barrier((far, state, sums))
     attended = attend_far(place, table, queries, state, sums, far, along_core(far), blocks_dev)

time: 63.3 us -> 61.8 us (0.976)
  waiting for transfers between devices: 23.9 us -> 21.5 us
    ppermute x2 -> x3, waiting for transfers between devices: 2.9 us -> 0.29 us  [along_y(): return lax.ppermute(x, 'seq', [(i, i ^ 2) for i in every])]
  transfers between devices with their start and end apart: 10 -> 11, of which waited for: 7 -> 8; matrix products, arithmetic and copies ran while one was open for 0% -> 0% of each run, Pallas kernels for 14% -> 14%
where the time goes in v2:
time: 61.8 us; the launch traced here: 61.5 us
  starting transfers between devices  22.9 us (37%)
  waiting for transfers between devices  21.5 us (35%)
  Pallas kernels  15.9 us (26%)
  between operations  0.91 us (1%)
    ppermute x5, waiting for transfers between devices, along_z(): return lax.ppermute(x, 'seq', [(i, (i + 4 * levels) % seqs) for i in every])  10.9 us
    ppermute x5, starting transfers between devices, along_z(): return lax.ppermute(x, 'seq', [(i, (i + 4 * levels) % seqs) for i in every])  9.44 us
    all_to_all x1, waiting for transfers between devices, per_device(): parts = lax.all_to_all(partial, 'section', 0, 0, tiled=True)  7.83 us
    all_to_all x1, starting transfers between devices, per_device(): parts = lax.all_to_all(partial, 'section', 0, 0, tiled=True)  7.49 us
    ppermute x2, starting transfers between devices, along_core(): return lax.ppermute(x, 'seq', [(i, i ^ 1) for i in every])  4.8 us
    pallas_call x1, Pallas kernels, attend_near(): pl.pallas_call(functools.partial(near_kernel, blocks_dev), in_specs=[SMEM...  4.76 us
    pallas_call x1, Pallas kernels, per_device(): pl.pallas_call(functools.partial(prepare_kernel, blocks_dev), in_specs=[S...  4.02 us
    pallas_call x1, Pallas kernels, project(): pl.pallas_call(project_kernel, in_specs=[anywhere] * 3, out_specs=pl.Bloc...  4.01 us
  transfers between devices with their start and end apart: 11, of which 8 were waited for; matrix products, arithmetic and copies ran while one was open for 0% of the time, Pallas kernels for 14%

profile of v2, /device:TPU:1, one launch (start us, length us, event | category | flops | bytes accessed | tf_op | source)
XLA Modules:
  0.0 61.5 jit_solution(16452024053446424365)
XLA Ops:
  0.7 4.0 %project.1 = bf16[8,136,256]{2,1,0:T(8,128)(2,1)} custom-call(bf16[128,1024]{1,0:T(8,128)(2,1)} %feat_hbm.1, f32[1,1024]{1,0:T(1,128)} %bitcast.5, bf16[1024,2048]{1,0:T(8,128)(2,1)} %weight_hbm.1), custom_call_target="tpu_custom_call" | custom-call | tf_op jit(solution)/shard_map/project/pallas_call | solution.py:72
  4.7 7.5 %all-to-all-start = ((bf16[8,136,256]{2,1,0:T(8,128)(2,1)}), bf16[8,136,256]{2,1,0:T(8,128)(2,1)S(1)}, u32[]{:S(2)}, u32[]{:S(2)}) async-start(bf16[8,136,256]{2,1,0:T(8,128)(2,1)} %project.1), calls=%async_computation | async-start | bytes 1114112 | tf_op jit(solution)/shard_map/all_to_all | solution.py:325
  12.3 0.1 copy.9
  12.4 4.0 %prepare.1.table = s32[896]{0:T(1024)S(1)} custom-call(s32[1]{0:T(128)} %bitcast.place, s32[6,16]{1,0:T(8,128)S(1)} %reshape.18.lists, s32[32,128]{1,0:T(8,128)S(1)} %bitcast.4), custom_call_target="tpu_custom_call" | custom-call | tf_op jit(solution)/shard_map/prepare/pallas_call | solution.py:327
  16.4 7.8 %all-to-all-done.parts = bf16[8,136,256]{2,1,0:T(8,128)(2,1)S(1)} async-done(((bf16[8,136,256]{2,1,0:T(8,128)(2,1)}), bf16[8,136,256]{2,1,0:T(8,128)(2,1)S(1)}, u32[]{:S(2)}, u32[]{:S(2)}) %all-to-all-start) | async-done | bytes 557088 | tf_op jit(solution)/shard_map/all_to_all | solution.py:325
  24.2 0.8 %reduce.1 = (bf16[128,256]{1,0:T(8,128)(2,1)}, bf16[128,256]{1,0:T(8,128)(2,1)S(1)}) custom-call(bf16[8,136,256]{2,1,0:T(8,128)(2,1)S(1)} %all-to-all-done.parts), custom_call_target="tpu_custom_call" | custom-call | tf_op jit(solution)/shard_map/reduce/pallas_call | solution.py:338
  25.0 5.6 %collective-permute-start.1 = (bf16[128,256]{1,0:T(8,128)(2,1)S(1)}, bf16[128,256]{1,0:T(8,128)(2,1)S(1)}, u32[]{:S(2)}, u32[]{:S(2)}) collective-permute-start(bf16[128,256]{1,0:T(8,128)(2,1)S(1)} %get-tuple-element.15), channel_id=1, source_target_pairs={{0,28},{1,29},{2,30},{3,31},{4,0},{5,1},{6,2},{7,3},{8,4},{9,5},{1... | collective-permute-start | bytes 196616 | tf_op jit(solution)/shard_map/ppermute | solution.py:348
  30.6 1.3 %collective-permute-done.1 = bf16[128,256]{1,0:T(8,128)(2,1)S(1)} collective-permute-done((bf16[128,256]{1,0:T(8,128)(2,1)S(1)}, bf16[128,256]{1,0:T(8,128)(2,1)S(1)}, u32[]{:S(2)}, u32[]{:S(2)}) %collective-permute-start.1) | collective-permute-done | bytes 65568 | tf_op jit(solution)/shard_map/ppermute | solution.py:348
  31.9 3.0 %collective-permute-done = bf16[128,256]{1,0:T(8,128)(2,1)S(1)} collective-permute-done((bf16[128,256]{1,0:T(8,128)(2,1)S(1)}, bf16[128,256]{1,0:T(8,128)(2,1)S(1)}, u32[]{:S(2)}, u32[]{:S(2)}) %collective-permute-start) | collective-permute-done | bytes 65568 | tf_op jit(solution)/shard_map/ppermute | solution.py:348
  34.9 0.3 collective-permute-start.6
  35.2 0.4 collective-permute-start.5
  35.6 2.1 %collective-permute-start.2 = (bf16[256,256]{1,0:T(8,128)(2,1)S(1)}, bf16[256,256]{1,0:T(8,128)(2,1)S(1)}, u32[]{:S(2)}, u32[]{:S(2)}) collective-permute-start(bf16[256,256]{1,0:T(8,128)(2,1)S(1)} %get-tuple-element.16), channel_id=1, source_target_pairs={{0,8},{1,9},{2,10},{3,11},{4,12},{5,13},{6,14},{7,15},{8,16},{9,17... | collective-permute-start | bytes 393224 | tf_op jit(solution)/shard_map/ppermute | solution.py:348
  37.8 1.4 %collective-permute-start.3 = (bf16[128,256]{1,0:T(8,128)(2,1)S(1)}, bf16[128,256]{1,0:T(8,128)(2,1)S(1)}, u32[]{:S(2)}, u32[]{:S(2)}) collective-permute-start(bf16[128,256]{1,0:T(8,128)(2,1)S(1)} %slice.3), channel_id=1, source_target_pairs={{0,16},{1,17},{2,18},{3,19},{4,20},{5,21},{6,22},{7,23},{8,24},{9,... | collective-permute-start | bytes 196616 | tf_op jit(solution)/shard_map/ppermute | solution.py:348
  39.2 3.2 %collective-permute-done.6 = bf16[256,256]{1,0:T(8,128)(2,1)S(1)} collective-permute-done((bf16[256,256]{1,0:T(8,128)(2,1)S(1)}, bf16[256,256]{1,0:T(8,128)(2,1)S(1)}, u32[]{:S(2)}, u32[]{:S(2)}) %collective-permute-start.6) | collective-permute-done | bytes 131104 | tf_op jit(solution)/shard_map/ppermute | solution.py:348
  42.4 0.4 collective-permute-start.7
  42.8 3.4 %collective-permute-done.3 = bf16[128,256]{1,0:T(8,128)(2,1)S(1)} collective-permute-done((bf16[128,256]{1,0:T(8,128)(2,1)S(1)}, bf16[128,256]{1,0:T(8,128)(2,1)S(1)}, u32[]{:S(2)}, u32[]{:S(2)}) %collective-permute-start.3) | collective-permute-done | bytes 65568 | tf_op jit(solution)/shard_map/ppermute | solution.py:348
  46.2 0.3 collective-permute-done.7
  46.5 4.0 %collective-permute-start.8 = (bf16[1408,256]{1,0:T(8,128)(2,1)S(1)}, bf16[1408,256]{1,0:T(8,128)(2,1)S(1)}, u32[]{:S(2)}, u32[]{:S(2)}) collective-permute-start(bf16[1408,256]{1,0:T(8,128)(2,1)S(1)} %constant_dynamic-update-slice_fusion.mine), channel_id=1, source_target_pairs={{0,1},{1,0},{2,3},{3,2},{4,5},{5,4},{6,7},{7,6},{8,9},{9,8},{10,11... | collective-permute-start | bytes 2162696 | tf_op jit(solution)/shard_map/ppermute | solution.py:354
  50.5 0.3 collective-permute-start.4
  50.8 1.5 %collective-permute-done.8.theirs = bf16[1408,256]{1,0:T(8,128)(2,1)S(1)} collective-permute-done((bf16[1408,256]{1,0:T(8,128)(2,1)S(1)}, bf16[1408,256]{1,0:T(8,128)(2,1)S(1)}, u32[]{:S(2)}, u32[]{:S(2)}) %collective-permute-start.8) | collective-permute-done | bytes 720928 | tf_op jit(solution)/shard_map/ppermute | solution.py:354
  52.3 4.8 %attend_near.1 = (f32[6,128,512]{2,1,0:T(8,128)S(1)}, f32[6,8,512]{2,1,0:T(8,128)S(1)}) custom-call(s32[1]{0:T(128)} %bitcast.place, s32[896]{0:T(1024)S(1)} %prepare.1.table, bf16[3,8,128,128]{3,2,1,0:T(8,128)(2,1)S(1)} %copy-done.1, bf16[3,1,128,256]{3,2,1,0:T(8,128)(2,1)S(1)} %copy-done.2, bf16[1408,256]{1,0:T(8,128)(2,1)S(1)} %constant_dynamic-update-slice_fusion.mine, ...), custom_call_target="tpu_custom_call" | custom-call | tf_op jit(solution)/shard_map/attend_near/pallas_call | solution.py:284
  57.1 0.8 %collective-permute-start.9 = (bf16[384,256]{1,0:T(8,128)(2,1)S(1)}, bf16[384,256]{1,0:T(8,128)(2,1)S(1)}, u32[]{:S(2)}, u32[]{:S(2)}) collective-permute-start(bf16[384,256]{1,0:T(8,128)(2,1)S(1)} %collective-permute-done.4.mine), channel_id=1, source_target_pairs={{0,1},{1,0},{2,3},{3,2},{4,5},{5,4},{6,7},{7,6},{8,9},{9,8},{10,11... | collective-permute-start | bytes 589832 | tf_op jit(solution)/shard_map/ppermute | solution.py:354
  57.9 1.1 %collective-permute-done.9.theirs = bf16[384,256]{1,0:T(8,128)(2,1)S(1)} collective-permute-done((bf16[384,256]{1,0:T(8,128)(2,1)S(1)}, bf16[384,256]{1,0:T(8,128)(2,1)S(1)}, u32[]{:S(2)}, u32[]{:S(2)}) %collective-permute-start.9) | collective-permute-done | bytes 196640 | tf_op jit(solution)/shard_map/ppermute | solution.py:354
  59.0 2.3 %attend_far.1 = bf16[3,8,128,128]{3,2,1,0:T(8,128)(2,1)} custom-call(s32[1]{0:T(128)} %bitcast.place, s32[896]{0:T(1024)S(1)} %prepare.1.table, bf16[3,8,128,128]{3,2,1,0:T(8,128)(2,1)S(1)} %copy-done.1, f32[6,128,512]{2,1,0:T(8,128)S(1)} %get-tuple-element.20.state, f32[6,8,512]{2,1,0:T(8,128)S(1)} %get-tuple-element.21.sums, ...), custom_call_target="tpu_custom_call" | custom-call | tf_op jit(solution)/shard_map/attend_far/pallas_call | solution.py:301
  (23 shorter events, 0.2 us)
Async XLA Ops:
  0.6 11.6 %copy-start = (s32[3,64,16]{1,2,0:T(8,128)S(1)}, s32[3,64,16]{1,2,0:T(8,128)}, u32[]{:S(2)}) copy-start(s32[3,64,16]{1,2,0:T(8,128)} %param.13) | copy-start | bytes 36868
  0.6 11.7 %copy-start.3 = (s32[4096]{0:T(1024)S(1)}, s32[4096]{0:T(1024)}, u32[]{:S(2)}) copy-start(s32[4096]{0:T(1024)} %param.12) | copy-start | bytes 49156
  0.7 51.6 %copy-start.1 = (bf16[3,8,128,128]{3,2,1,0:T(8,128)(2,1)S(1)}, bf16[3,8,128,128]{3,2,1,0:T(8,128)(2,1)}, u32[]{:S(2)}) copy-start(bf16[3,8,128,128]{3,2,1,0:T(8,128)(2,1)} %q.3) | copy-start | bytes 2359300
  0.7 51.6 %copy-start.2 = (bf16[3,1,128,256]{3,2,1,0:T(8,128)(2,1)S(1)}, bf16[3,1,128,256]{3,2,1,0:T(8,128)(2,1)}, u32[]{:S(2)}) copy-start(bf16[3,1,128,256]{3,2,1,0:T(8,128)(2,1)} %own.1) | copy-start | bytes 589828
  4.7 19.5 %all-to-all-start = ((bf16[8,136,256]{2,1,0:T(8,128)(2,1)}), bf16[8,136,256]{2,1,0:T(8,128)(2,1)S(1)}, u32[]{:S(2)}, u32[]{:S(2)}) async-start(bf16[8,136,256]{2,1,0:T(8,128)(2,1)} %project.1), calls=%async_computation | async-start | bytes 1114112 | tf_op jit(solution)/shard_map/all_to_all | solution.py:325
  25.0 6.9 %collective-permute-start.1 = (bf16[128,256]{1,0:T(8,128)(2,1)S(1)}, bf16[128,256]{1,0:T(8,128)(2,1)S(1)}, u32[]{:S(2)}, u32[]{:S(2)}) collective-permute-start(bf16[128,256]{1,0:T(8,128)(2,1)S(1)} %get-tuple-element.15), channel_id=1, source_target_pairs={{0,28},{1,29},{2,30},{3,31},{4,0},{5,1},{6,2},{7,3},{8,4},{9,5},{1... | collective-permute-start | bytes 196616 | tf_op jit(solution)/shard_map/ppermute | solution.py:348
  30.6 4.3 %collective-permute-start = (bf16[128,256]{1,0:T(8,128)(2,1)S(1)}, bf16[128,256]{1,0:T(8,128)(2,1)S(1)}, u32[]{:S(2)}, u32[]{:S(2)}) collective-permute-start(bf16[128,256]{1,0:T(8,128)(2,1)S(1)} %get-tuple-element.15), channel_id=1, source_target_pairs={{0,4},{1,5},{2,6},{3,7},{4,8},{5,9},{6,10},{7,11},{8,12},{9,13},{1... | collective-permute-start | bytes 196616 | tf_op jit(solution)/shard_map/ppermute | solution.py:348
  34.9 7.4 %collective-permute-start.6 = (bf16[256,256]{1,0:T(8,128)(2,1)S(1)}, bf16[256,256]{1,0:T(8,128)(2,1)S(1)}, u32[]{:S(2)}, u32[]{:S(2)}) collective-permute-start(bf16[256,256]{1,0:T(8,128)(2,1)S(1)} %get-tuple-element.17), channel_id=1, source_target_pairs={{0,24},{1,25},{2,26},{3,27},{4,28},{5,29},{6,30},{7,31},{8,0},{9,1... | collective-permute-start | bytes 393224 | tf_op jit(solution)/shard_map/ppermute | solution.py:348
  35.2 7.5 %collective-permute-start.5 = (bf16[256,256]{1,0:T(8,128)(2,1)S(1)}, bf16[256,256]{1,0:T(8,128)(2,1)S(1)}, u32[]{:S(2)}, u32[]{:S(2)}) collective-permute-start(bf16[256,256]{1,0:T(8,128)(2,1)S(1)} %get-tuple-element.16), channel_id=1, source_target_pairs={{0,2},{1,3},{2,0},{3,1},{4,6},{5,7},{6,4},{7,5},{8,10},{9,11},{10,... | collective-permute-start | bytes 393224 | tf_op jit(solution)/shard_map/ppermute | solution.py:351
  35.6 7.1 %collective-permute-start.2 = (bf16[256,256]{1,0:T(8,128)(2,1)S(1)}, bf16[256,256]{1,0:T(8,128)(2,1)S(1)}, u32[]{:S(2)}, u32[]{:S(2)}) collective-permute-start(bf16[256,256]{1,0:T(8,128)(2,1)S(1)} %get-tuple-element.16), channel_id=1, source_target_pairs={{0,8},{1,9},{2,10},{3,11},{4,12},{5,13},{6,14},{7,15},{8,16},{9,17... | collective-permute-start | bytes 393224 | tf_op jit(solution)/shard_map/ppermute | solution.py:348
  37.8 8.4 %collective-permute-start.3 = (bf16[128,256]{1,0:T(8,128)(2,1)S(1)}, bf16[128,256]{1,0:T(8,128)(2,1)S(1)}, u32[]{:S(2)}, u32[]{:S(2)}) collective-permute-start(bf16[128,256]{1,0:T(8,128)(2,1)S(1)} %slice.3), channel_id=1, source_target_pairs={{0,16},{1,17},{2,18},{3,19},{4,20},{5,21},{6,22},{7,23},{8,24},{9,... | collective-permute-start | bytes 196616 | tf_op jit(solution)/shard_map/ppermute | solution.py:348
  42.4 4.1 %collective-permute-start.7 = (bf16[256,256]{1,0:T(8,128)(2,1)S(1)}, bf16[256,256]{1,0:T(8,128)(2,1)S(1)}, u32[]{:S(2)}, u32[]{:S(2)}) collective-permute-start(bf16[256,256]{1,0:T(8,128)(2,1)S(1)} %collective-permute-done.6), channel_id=1, source_target_pairs={{0,2},{1,3},{2,0},{3,1},{4,6},{5,7},{6,4},{7,5},{8,10},{9,11},{10,... | collective-permute-start | bytes 393224 | tf_op jit(solution)/shard_map/ppermute | solution.py:351
  46.5 5.8 %collective-permute-start.8 = (bf16[1408,256]{1,0:T(8,128)(2,1)S(1)}, bf16[1408,256]{1,0:T(8,128)(2,1)S(1)}, u32[]{:S(2)}, u32[]{:S(2)}) collective-permute-start(bf16[1408,256]{1,0:T(8,128)(2,1)S(1)} %constant_dynamic-update-slice_fusion.mine), channel_id=1, source_target_pairs={{0,1},{1,0},{2,3},{3,2},{4,5},{5,4},{6,7},{7,6},{8,9},{9,8},{10,11... | collective-permute-start | bytes 2162696 | tf_op jit(solution)/shard_map/ppermute | solution.py:354
  50.5 6.6 %collective-permute-start.4 = (bf16[384,256]{1,0:T(8,128)(2,1)S(1)}, bf16[384,256]{1,0:T(8,128)(2,1)S(1)}, u32[]{:S(2)}, u32[]{:S(2)}) collective-permute-start(bf16[384,256]{1,0:T(8,128)(2,1)S(1)} %pad_maximum_fusion), channel_id=1, source_target_pairs={{0,2},{1,3},{2,0},{3,1},{4,6},{5,7},{6,4},{7,5},{8,10},{9,11},{10,... | collective-permute-start | bytes 589832 | tf_op jit(solution)/shard_map/ppermute | solution.py:351
  57.1 1.9 %collective-permute-start.9 = (bf16[384,256]{1,0:T(8,128)(2,1)S(1)}, bf16[384,256]{1,0:T(8,128)(2,1)S(1)}, u32[]{:S(2)}, u32[]{:S(2)}) collective-permute-start(bf16[384,256]{1,0:T(8,128)(2,1)S(1)} %collective-permute-done.4.mine), channel_id=1, source_target_pairs={{0,1},{1,0},{2,3},{3,2},{4,5},{5,4},{6,7},{7,6},{8,9},{9,8},{10,11... | collective-permute-start | bytes 589832 | tf_op jit(solution)/shard_map/ppermute | solution.py:354

commit v3 on v2

--- a/solution.py
+++ b/solution.py
@@ -23,7 +23,7 @@
 FAR_ROWS = RISING
 LINE = 128
 COUNTS = 64
-NEAR_SIZES = (4, 8, 12, 16)
+NEAR_SIZES = (2, 4, 6, 8, 10, 12, 16)
 FAR_SIZES = (0, 2, 4, 6, 8, 16)
 
 VMEM_ALL = 60 << 20
@@ -67,7 +67,7 @@
 def project(features, norm_gain, kv_weight, heads):
     tokens, width = features.shape
     cols = kv_weight.shape[1] // heads
-    blocks = 4
+    blocks = 8
     anywhere = pl.BlockSpec(memory_space=pl.ANY)
     return pl.pallas_call(
         project_kernel,
@@ -215,7 +215,39 @@
         row += part.shape[0]
 
 
-def near_kernel(blocks_dev, place, table, q, own, mine, theirs, state, sums, held):
+def own_kernel(blocks_dev, q, own, state, sums):
+    steps, heads, tokens, head_dim = q.shape
+
+    def body(u, carry):
+        k = u // blocks_dev
+        rows = pl.ds(pl.multiple_of(lax.rem(u, blocks_dev) * BLK, BLK), BLK)
+        queries = q[k, :, rows, :].reshape(heads * BLK, head_dim)
+        extra = [(own[m, 0, rows, :], m <= k) for m in range(steps)]
+        s, values = scores(0, 0, 0, extra, None, None, queries, None)
+        top = jnp.max(s, axis=0, keepdims=True)
+        p = jnp.exp2((s - top) * SCALE)
+        sums[u, 0:1] = top
+        sums[u, 1:2] = jnp.sum(p, axis=0, keepdims=True)
+        state[u] = weigh(p, values)
+        return carry
+
+    lax.fori_loop(0, steps * blocks_dev, body, 0)
+
+
+def add_blocks(size, u, base, block, begins, table, queries, held, state, sums):
+    top, total, summed = sums[u, 0:1], sums[u, 1:2], state[u]
+    if size:
+        s, values = scores(size, base, block, [], begins, table, queries, held)
+        new_top = jnp.maximum(top, jnp.max(s, axis=0, keepdims=True))
+        p = jnp.exp2((s - new_top) * SCALE)
+        factor = jnp.exp2((top - new_top) * SCALE)
+        total = total * factor + jnp.sum(p, axis=0, keepdims=True)
+        summed = summed * factor + weigh(p, values)
+        top = new_top
+    return top, total, summed
+
+
+def near_kernel(blocks_dev, place, table, q, old_state, old_sums, mine, theirs, state, sums, held):
     t = place[0]
     units = q.shape[0] * blocks_dev
     hold(held, (mine, theirs))
@@ -224,13 +256,12 @@
         k, block, rows, queries, begins = unit_state(blocks_dev, u, t, table, q)
 
         def run(size):
-            extra = [(own[m, 0, rows, :], m <= k) for m in range(own.shape[0])]
-            s, values = scores(size, u * LINE, block, extra, begins, table, queries, held)
-            top = jnp.max(s, axis=0, keepdims=True)
-            p = jnp.exp2((s - top) * SCALE)
+            top, total, summed = add_blocks(
+                size, u, u * LINE, block, begins, table, queries, held, old_state, old_sums
+            )
             sums[u, 0:1] = top
-            sums[u, 1:2] = jnp.sum(p, axis=0, keepdims=True)
-            state[u] = weigh(p, values)
+            sums[u, 1:2] = total
+            state[u] = summed
 
         per_size(NEAR_SIZES, table[units * LINE + COUNTS + u], run)
         return carry
@@ -252,14 +283,9 @@
         k, block, rows, queries, begins = unit_state(blocks_dev, u, t, table, q)
 
         def run(size):
-            top, total, summed = sums[u, 0:1], sums[u, 1:2], state[u]
-            if size:
-                s, values = scores(size, u * LINE + 2 * LIST, block, [], begins, table, queries, held)
-                new_top = jnp.maximum(top, jnp.max(s, axis=0, keepdims=True))
-                p = jnp.exp2((s - new_top) * SCALE)
-                factor = jnp.exp2((top - new_top) * SCALE)
-                total = total * factor + jnp.sum(p, axis=0, keepdims=True)
-                summed = summed * factor + weigh(p, values)
+            top, total, summed = add_blocks(
+                size, u, u * LINE + 2 * LIST, block, begins, table, queries, held, state, sums
+            )
             result[u] = (summed * (1.0 / total)).T.astype(jnp.bfloat16).reshape(heads, BLK, head_dim)
 
         per_size(FAR_SIZES, table[units * LINE + COUNTS + units + u], run)
@@ -278,21 +304,37 @@
     return pltpu.CompilerParams(vmem_limit_bytes=mib << 20)
 
 
-def attend_near(place, table, queries, step_kv, parts, blocks_dev):
+def state_shapes(queries, blocks_dev):
     steps, heads, tokens, head_dim = queries.shape
     units = steps * blocks_dev
+    return [
+        jax.ShapeDtypeStruct((units, head_dim, heads * BLK), jnp.float32),
+        jax.ShapeDtypeStruct((units, 8, heads * BLK), jnp.float32),
+    ]
+
+
+def attend_own(queries, step_kv, blocks_dev):
+    return pl.pallas_call(
+        functools.partial(own_kernel, blocks_dev),
+        in_specs=[VMEM_WHOLE] * 2,
+        out_specs=[VMEM_WHOLE] * 2,
+        out_shape=state_shapes(queries, blocks_dev),
+        compiler_params=limit(16),
+        name="attend_own",
+    )(queries, step_kv)
+
+
+def attend_near(place, table, queries, state, sums, mine, theirs, blocks_dev):
     return pl.pallas_call(
         functools.partial(near_kernel, blocks_dev),
-        in_specs=[SMEM_ALL, SMEM_ALL] + [VMEM_WHOLE] * (2 + len(parts)),
-        out_specs=[VMEM_WHOLE, VMEM_WHOLE],
-        out_shape=[
-            jax.ShapeDtypeStruct((units, head_dim, heads * BLK), jnp.float32),
-            jax.ShapeDtypeStruct((units, 8, heads * BLK), jnp.float32),
-        ],
-        scratch_shapes=[pltpu.VMEM((2 * NEAR_ROWS, 2 * head_dim), jnp.bfloat16)],
+        in_specs=[SMEM_ALL] * 2 + [VMEM_WHOLE] * 5,
+        out_specs=[VMEM_WHOLE] * 2,
+        out_shape=state_shapes(queries, blocks_dev),
+        input_output_aliases={3: 0, 4: 1},
+        scratch_shapes=[pltpu.VMEM((2 * NEAR_ROWS, mine.shape[1]), jnp.bfloat16)],
         compiler_params=limit(24),
         name="attend_near",
-    )(place, table, queries, step_kv, *parts)
+    )(place, table, queries, state, sums, mine, theirs)
 
 
 def attend_far(place, table, queries, state, sums, mine, theirs, blocks_dev):
@@ -334,7 +376,8 @@
         name="prepare",
     )(place, lists, doc_ids.reshape(-1, 128))
 
-    parts, table = lax.optimization_barrier((parts, table))
+    state, sums = attend_own(queries, step_kv, blocks_dev)
+    parts, table, state, sums = lax.optimization_barrier((parts, table, state, sums))
     kv_cache, kv = pl.pallas_call(
         functools.partial(reduce_kernel, float(features.shape[1] * sections)),
         out_shape=[jax.ShapeDtypeStruct((tok_dev, 2 * head_dim), jnp.bfloat16)] * 2,
@@ -367,7 +410,7 @@
     rising = join(up23, up4)
     far = along_y(rising)
     near = join(low, low_y, rising, falling)
-    state, sums = attend_near(place, table, queries, step_kv, (near, along_core(near)), blocks_dev)
+    state, sums = attend_near(place, table, queries, state, sums, near, along_core(near), blocks_dev)
     far, state, sums = lax.optimization_barrier((far, state, sums))
     attended = attend_far(place, table, queries, state, sums, far, along_core(far), blocks_dev)
     return attended, kv_cache[None]

time: 61.8 us -> 63.4 us (1.026)
  Pallas kernels: 15.9 us -> 19.1 us
  waiting for transfers between devices: 21.5 us -> 19.7 us
    all_to_all x1, waiting for transfers between devices: 7.83 us -> 5.03 us  [per_device(): parts = lax.all_to_all(partial, 'section', 0, 0, tiled=True)]
    pallas_call x0 -> x1, Pallas kernels: none -> 2.78 us  [attend_own(): pl.pallas_call(functools.partial(own_kernel, blocks_dev), in_specs=[VMEM_...]
    pallas_call x1, Pallas kernels: 4.01 us -> 5.49 us  [project(): pl.pallas_call(project_kernel, in_specs=[anywhere] * 3, out_specs=pl.Bloc...]
    ppermute x3, waiting for transfers between devices: 0.29 us -> 1.48 us  [along_y(): return lax.ppermute(x, 'seq', [(i, i ^ 2) for i in every])]
    pallas_call x1, Pallas kernels: 4.76 us -> 3.76 us  [attend_near(): pl.pallas_call(functools.partial(near_kernel, blocks_dev), in_specs=[SMEM...]
  transfers between devices with their start and end apart: 11 -> 11, of which waited for: 8 -> 9; matrix products, arithmetic and copies ran while one was open for 0% -> 0% of each run, Pallas kernels for 14% -> 17%
where the time goes in v3:
time: 63.4 us; the launch traced here: 63.3 us
  starting transfers between devices  23.2 us (37%)
  waiting for transfers between devices  19.7 us (31%)
  Pallas kernels  19.1 us (30%)
  between operations  0.93 us (1%)
    ppermute x5, waiting for transfers between devices, along_z(): return lax.ppermute(x, 'seq', [(i, (i + 4 * levels) % seqs) for i in every])  10.9 us
    ppermute x5, starting transfers between devices, along_z(): return lax.ppermute(x, 'seq', [(i, (i + 4 * levels) % seqs) for i in every])  9.44 us
    all_to_all x1, starting transfers between devices, per_device(): parts = lax.all_to_all(partial, 'section', 0, 0, tiled=True)  7.62 us
    pallas_call x1, Pallas kernels, project(): pl.pallas_call(project_kernel, in_specs=[anywhere] * 3, out_specs=pl.Bloc...  5.49 us
    all_to_all x1, waiting for transfers between devices, per_device(): parts = lax.all_to_all(partial, 'section', 0, 0, tiled=True)  5.03 us
    ppermute x2, starting transfers between devices, along_core(): return lax.ppermute(x, 'seq', [(i, i ^ 1) for i in every])  4.79 us
    pallas_call x1, Pallas kernels, per_device(): pl.pallas_call(functools.partial(prepare_kernel, blocks_dev), in_specs=[S...  4.02 us
    pallas_call x1, Pallas kernels, attend_near(): pl.pallas_call(functools.partial(near_kernel, blocks_dev), in_specs=[SMEM...  3.76 us
  transfers between devices with their start and end apart: 11, of which 9 were waited for; matrix products, arithmetic and copies ran while one was open for 0% of the time, Pallas kernels for 17%

profile of v3, /device:TPU:1, one launch (start us, length us, event | category | flops | bytes accessed | tf_op | source)
XLA Modules:
  0.0 63.3 jit_solution(1453749888004989517)
XLA Ops:
  0.7 5.5 %project.1 = bf16[8,136,256]{2,1,0:T(8,128)(2,1)} custom-call(bf16[128,1024]{1,0:T(8,128)(2,1)} %feat_hbm.1, f32[1,1024]{1,0:T(1,128)} %bitcast.5, bf16[1024,2048]{1,0:T(8,128)(2,1)} %weight_hbm.1), custom_call_target="tpu_custom_call" | custom-call | tf_op jit(solution)/shard_map/project/pallas_call | solution.py:72
  6.2 7.6 %all-to-all-start = ((bf16[8,136,256]{2,1,0:T(8,128)(2,1)}), bf16[8,136,256]{2,1,0:T(8,128)(2,1)S(1)}, u32[]{:S(2)}, u32[]{:S(2)}) async-start(bf16[8,136,256]{2,1,0:T(8,128)(2,1)} %project.1), calls=%async_computation | async-start | bytes 1114112 | tf_op jit(solution)/shard_map/all_to_all | solution.py:367
  14.0 2.8 %attend_own.1 = (f32[6,128,512]{2,1,0:T(8,128)S(1)}, f32[6,8,512]{2,1,0:T(8,128)S(1)}) custom-call(bf16[3,8,128,128]{3,2,1,0:T(8,128)(2,1)S(1)} %copy-done.1, bf16[3,1,128,256]{3,2,1,0:T(8,128)(2,1)S(1)} %copy-done.2), custom_call_target="tpu_custom_call" | custom-call | tf_op jit(solution)/shard_map/attend_own/pallas_call | solution.py:317
  16.8 4.0 %prepare.1.table = s32[896]{0:T(1024)S(1)} custom-call(s32[1]{0:T(128)} %bitcast.place, s32[6,16]{1,0:T(8,128)S(1)} %reshape.18.lists, s32[32,128]{1,0:T(8,128)S(1)} %bitcast.4), custom_call_target="tpu_custom_call" | custom-call | tf_op jit(solution)/shard_map/prepare/pallas_call | solution.py:369
  20.8 5.0 %all-to-all-done.parts = bf16[8,136,256]{2,1,0:T(8,128)(2,1)S(1)} async-done(((bf16[8,136,256]{2,1,0:T(8,128)(2,1)}), bf16[8,136,256]{2,1,0:T(8,128)(2,1)S(1)}, u32[]{:S(2)}, u32[]{:S(2)}) %all-to-all-start) | async-done | bytes 557088 | tf_op jit(solution)/shard_map/all_to_all | solution.py:367
  25.8 0.8 %reduce.1 = (bf16[128,256]{1,0:T(8,128)(2,1)}, bf16[128,256]{1,0:T(8,128)(2,1)S(1)}) custom-call(bf16[8,136,256]{2,1,0:T(8,128)(2,1)S(1)} %all-to-all-done.parts), custom_call_target="tpu_custom_call" | custom-call | tf_op jit(solution)/shard_map/reduce/pallas_call | solution.py:381
  26.6 5.6 %collective-permute-start.1 = (bf16[128,256]{1,0:T(8,128)(2,1)S(1)}, bf16[128,256]{1,0:T(8,128)(2,1)S(1)}, u32[]{:S(2)}, u32[]{:S(2)}) collective-permute-start(bf16[128,256]{1,0:T(8,128)(2,1)S(1)} %get-tuple-element.21), channel_id=1, source_target_pairs={{0,28},{1,29},{2,30},{3,31},{4,0},{5,1},{6,2},{7,3},{8,4},{9,5},{1... | collective-permute-start | bytes 196616 | tf_op jit(solution)/shard_map/ppermute | solution.py:391
  32.2 1.3 %collective-permute-done.1 = bf16[128,256]{1,0:T(8,128)(2,1)S(1)} collective-permute-done((bf16[128,256]{1,0:T(8,128)(2,1)S(1)}, bf16[128,256]{1,0:T(8,128)(2,1)S(1)}, u32[]{:S(2)}, u32[]{:S(2)}) %collective-permute-start.1) | collective-permute-done | bytes 65568 | tf_op jit(solution)/shard_map/ppermute | solution.py:391
  33.5 3.0 %collective-permute-done = bf16[128,256]{1,0:T(8,128)(2,1)S(1)} collective-permute-done((bf16[128,256]{1,0:T(8,128)(2,1)S(1)}, bf16[128,256]{1,0:T(8,128)(2,1)S(1)}, u32[]{:S(2)}, u32[]{:S(2)}) %collective-permute-start) | collective-permute-done | bytes 65568 | tf_op jit(solution)/shard_map/ppermute | solution.py:391
  36.5 0.3 collective-permute-start.6
  36.9 0.4 collective-permute-start.5
  37.3 2.1 %collective-permute-start.2 = (bf16[256,256]{1,0:T(8,128)(2,1)S(1)}, bf16[256,256]{1,0:T(8,128)(2,1)S(1)}, u32[]{:S(2)}, u32[]{:S(2)}) collective-permute-start(bf16[256,256]{1,0:T(8,128)(2,1)S(1)} %get-tuple-element.22), channel_id=1, source_target_pairs={{0,8},{1,9},{2,10},{3,11},{4,12},{5,13},{6,14},{7,15},{8,16},{9,17... | collective-permute-start | bytes 393224 | tf_op jit(solution)/shard_map/ppermute | solution.py:391
  39.4 1.4 %collective-permute-start.3 = (bf16[128,256]{1,0:T(8,128)(2,1)S(1)}, bf16[128,256]{1,0:T(8,128)(2,1)S(1)}, u32[]{:S(2)}, u32[]{:S(2)}) collective-permute-start(bf16[128,256]{1,0:T(8,128)(2,1)S(1)} %slice.3), channel_id=1, source_target_pairs={{0,16},{1,17},{2,18},{3,19},{4,20},{5,21},{6,22},{7,23},{8,24},{9,... | collective-permute-start | bytes 196616 | tf_op jit(solution)/shard_map/ppermute | solution.py:391
  40.8 3.2 %collective-permute-done.6 = bf16[256,256]{1,0:T(8,128)(2,1)S(1)} collective-permute-done((bf16[256,256]{1,0:T(8,128)(2,1)S(1)}, bf16[256,256]{1,0:T(8,128)(2,1)S(1)}, u32[]{:S(2)}, u32[]{:S(2)}) %collective-permute-start.6) | collective-permute-done | bytes 131104 | tf_op jit(solution)/shard_map/ppermute | solution.py:391
  44.0 0.4 collective-permute-start.7
  44.4 3.4 %collective-permute-done.3 = bf16[128,256]{1,0:T(8,128)(2,1)S(1)} collective-permute-done((bf16[128,256]{1,0:T(8,128)(2,1)S(1)}, bf16[128,256]{1,0:T(8,128)(2,1)S(1)}, u32[]{:S(2)}, u32[]{:S(2)}) %collective-permute-start.3) | collective-permute-done | bytes 65568 | tf_op jit(solution)/shard_map/ppermute | solution.py:391
  48.1 4.0 %collective-permute-start.8 = (bf16[1408,256]{1,0:T(8,128)(2,1)S(1)}, bf16[1408,256]{1,0:T(8,128)(2,1)S(1)}, u32[]{:S(2)}, u32[]{:S(2)}) collective-permute-start(bf16[1408,256]{1,0:T(8,128)(2,1)S(1)} %constant_dynamic-update-slice_fusion.mine), channel_id=1, source_target_pairs={{0,1},{1,0},{2,3},{3,2},{4,5},{5,4},{6,7},{7,6},{8,9},{9,8},{10,11... | collective-permute-start | bytes 2162696 | tf_op jit(solution)/shard_map/ppermute | solution.py:397
  52.1 0.5 collective-permute-start.4
  52.6 1.3 %collective-permute-done.8.theirs = bf16[1408,256]{1,0:T(8,128)(2,1)S(1)} collective-permute-done((bf16[1408,256]{1,0:T(8,128)(2,1)S(1)}, bf16[1408,256]{1,0:T(8,128)(2,1)S(1)}, u32[]{:S(2)}, u32[]{:S(2)}) %collective-permute-start.8) | collective-permute-done | bytes 720928 | tf_op jit(solution)/shard_map/ppermute | solution.py:397
  53.9 3.8 %attend_near.1 = (f32[6,128,512]{2,1,0:T(8,128)S(1)}, f32[6,8,512]{2,1,0:T(8,128)S(1)}) custom-call(s32[1]{0:T(128)} %bitcast.place, s32[896]{0:T(1024)S(1)} %prepare.1.table, bf16[3,8,128,128]{3,2,1,0:T(8,128)(2,1)S(1)} %copy-done.1, f32[6,128,512]{2,1,0:T(8,128)S(1)} %get-tuple-element.23.old_state, ...), custom_call_target="tpu_custom_call", output_to_operand_aliasing={{0}: (3, {}), {1}: (4, {})} | custom-call | tf_op jit(solution)/shard_map/attend_near/pallas_call | solution.py:328
  57.7 1.2 %collective-permute-done.4.mine = bf16[384,256]{1,0:T(8,128)(2,1)S(1)} collective-permute-done((bf16[384,256]{1,0:T(8,128)(2,1)S(1)}, bf16[384,256]{1,0:T(8,128)(2,1)S(1)}, u32[]{:S(2)}, u32[]{:S(2)}) %collective-permute-start.4) | collective-permute-done | bytes 196640 | tf_op jit(solution)/shard_map/ppermute | solution.py:394
  58.9 0.8 %collective-permute-start.9 = (bf16[384,256]{1,0:T(8,128)(2,1)S(1)}, bf16[384,256]{1,0:T(8,128)(2,1)S(1)}, u32[]{:S(2)}, u32[]{:S(2)}) collective-permute-start(bf16[384,256]{1,0:T(8,128)(2,1)S(1)} %collective-permute-done.4.mine), channel_id=1, source_target_pairs={{0,1},{1,0},{2,3},{3,2},{4,5},{5,4},{6,7},{7,6},{8,9},{9,8},{10,11... | collective-permute-start | bytes 589832 | tf_op jit(solution)/shard_map/ppermute | solution.py:397
  59.7 1.1 %collective-permute-done.9.theirs = bf16[384,256]{1,0:T(8,128)(2,1)S(1)} collective-permute-done((bf16[384,256]{1,0:T(8,128)(2,1)S(1)}, bf16[384,256]{1,0:T(8,128)(2,1)S(1)}, u32[]{:S(2)}, u32[]{:S(2)}) %collective-permute-start.9) | collective-permute-done | bytes 196640 | tf_op jit(solution)/shard_map/ppermute | solution.py:397
  60.8 2.3 %attend_far.1 = bf16[3,8,128,128]{3,2,1,0:T(8,128)(2,1)} custom-call(s32[1]{0:T(128)} %bitcast.place, s32[896]{0:T(1024)S(1)} %prepare.1.table, bf16[3,8,128,128]{3,2,1,0:T(8,128)(2,1)S(1)} %copy-done.1, f32[6,128,512]{2,1,0:T(8,128)S(1)} %get-tuple-element.28.state, f32[6,8,512]{2,1,0:T(8,128)S(1)} %get-tuple-element.29.sums, ...), custom_call_target="tpu_custom_call" | custom-call | tf_op jit(solution)/shard_map/attend_far/pallas_call | solution.py:343
  (24 shorter events, 0.6 us)
Async XLA Ops:
  0.6 13.2 %copy-start = (s32[3,64,16]{1,2,0:T(8,128)S(1)}, s32[3,64,16]{1,2,0:T(8,128)}, u32[]{:S(2)}) copy-start(s32[3,64,16]{1,2,0:T(8,128)} %param.13) | copy-start | bytes 36868
  0.6 13.3 %copy-start.2 = (bf16[3,1,128,256]{3,2,1,0:T(8,128)(2,1)S(1)}, bf16[3,1,128,256]{3,2,1,0:T(8,128)(2,1)}, u32[]{:S(2)}) copy-start(bf16[3,1,128,256]{3,2,1,0:T(8,128)(2,1)} %own.1) | copy-start | bytes 589828
  6.2 7.8 %copy-start.1 = (bf16[3,8,128,128]{3,2,1,0:T(8,128)(2,1)S(1)}, bf16[3,8,128,128]{3,2,1,0:T(8,128)(2,1)}, u32[]{:S(2)}) copy-start(bf16[3,8,128,128]{3,2,1,0:T(8,128)(2,1)} %q.5) | copy-start | bytes 2359300
  6.2 10.6 %copy-start.3 = (s32[4096]{0:T(1024)S(1)}, s32[4096]{0:T(1024)}, u32[]{:S(2)}) copy-start(s32[4096]{0:T(1024)} %param.12) | copy-start | bytes 49156
  6.2 19.7 %all-to-all-start = ((bf16[8,136,256]{2,1,0:T(8,128)(2,1)}), bf16[8,136,256]{2,1,0:T(8,128)(2,1)S(1)}, u32[]{:S(2)}, u32[]{:S(2)}) async-start(bf16[8,136,256]{2,1,0:T(8,128)(2,1)} %project.1), calls=%async_computation | async-start | bytes 1114112 | tf_op jit(solution)/shard_map/all_to_all | solution.py:367
  26.6 6.9 %collective-permute-start.1 = (bf16[128,256]{1,0:T(8,128)(2,1)S(1)}, bf16[128,256]{1,0:T(8,128)(2,1)S(1)}, u32[]{:S(2)}, u32[]{:S(2)}) collective-permute-start(bf16[128,256]{1,0:T(8,128)(2,1)S(1)} %get-tuple-element.21), channel_id=1, source_target_pairs={{0,28},{1,29},{2,30},{3,31},{4,0},{5,1},{6,2},{7,3},{8,4},{9,5},{1... | collective-permute-start | bytes 196616 | tf_op jit(solution)/shard_map/ppermute | solution.py:391
  32.2 4.3 %collective-permute-start = (bf16[128,256]{1,0:T(8,128)(2,1)S(1)}, bf16[128,256]{1,0:T(8,128)(2,1)S(1)}, u32[]{:S(2)}, u32[]{:S(2)}) collective-permute-start(bf16[128,256]{1,0:T(8,128)(2,1)S(1)} %get-tuple-element.21), channel_id=1, source_target_pairs={{0,4},{1,5},{2,6},{3,7},{4,8},{5,9},{6,10},{7,11},{8,12},{9,13},{1... | collective-permute-start | bytes 196616 | tf_op jit(solution)/shard_map/ppermute | solution.py:391
  36.5 7.4 %collective-permute-start.6 = (bf16[256,256]{1,0:T(8,128)(2,1)S(1)}, bf16[256,256]{1,0:T(8,128)(2,1)S(1)}, u32[]{:S(2)}, u32[]{:S(2)}) collective-permute-start(bf16[256,256]{1,0:T(8,128)(2,1)S(1)} %get-tuple-element.25), channel_id=1, source_target_pairs={{0,24},{1,25},{2,26},{3,27},{4,28},{5,29},{6,30},{7,31},{8,0},{9,1... | collective-permute-start | bytes 393224 | tf_op jit(solution)/shard_map/ppermute | solution.py:391
  36.9 7.5 %collective-permute-start.5 = (bf16[256,256]{1,0:T(8,128)(2,1)S(1)}, bf16[256,256]{1,0:T(8,128)(2,1)S(1)}, u32[]{:S(2)}, u32[]{:S(2)}) collective-permute-start(bf16[256,256]{1,0:T(8,128)(2,1)S(1)} %get-tuple-element.22), channel_id=1, source_target_pairs={{0,2},{1,3},{2,0},{3,1},{4,6},{5,7},{6,4},{7,5},{8,10},{9,11},{10,... | collective-permute-start | bytes 393224 | tf_op jit(solution)/shard_map/ppermute | solution.py:394
  37.3 7.1 %collective-permute-start.2 = (bf16[256,256]{1,0:T(8,128)(2,1)S(1)}, bf16[256,256]{1,0:T(8,128)(2,1)S(1)}, u32[]{:S(2)}, u32[]{:S(2)}) collective-permute-start(bf16[256,256]{1,0:T(8,128)(2,1)S(1)} %get-tuple-element.22), channel_id=1, source_target_pairs={{0,8},{1,9},{2,10},{3,11},{4,12},{5,13},{6,14},{7,15},{8,16},{9,17... | collective-permute-start | bytes 393224 | tf_op jit(solution)/shard_map/ppermute | solution.py:391
  39.4 8.4 %collective-permute-start.3 = (bf16[128,256]{1,0:T(8,128)(2,1)S(1)}, bf16[128,256]{1,0:T(8,128)(2,1)S(1)}, u32[]{:S(2)}, u32[]{:S(2)}) collective-permute-start(bf16[128,256]{1,0:T(8,128)(2,1)S(1)} %slice.3), channel_id=1, source_target_pairs={{0,16},{1,17},{2,18},{3,19},{4,20},{5,21},{6,22},{7,23},{8,24},{9,... | collective-permute-start | bytes 196616 | tf_op jit(solution)/shard_map/ppermute | solution.py:391
  44.0 4.1 %collective-permute-start.7 = (bf16[256,256]{1,0:T(8,128)(2,1)S(1)}, bf16[256,256]{1,0:T(8,128)(2,1)S(1)}, u32[]{:S(2)}, u32[]{:S(2)}) collective-permute-start(bf16[256,256]{1,0:T(8,128)(2,1)S(1)} %collective-permute-done.6), channel_id=1, source_target_pairs={{0,2},{1,3},{2,0},{3,1},{4,6},{5,7},{6,4},{7,5},{8,10},{9,11},{10,... | collective-permute-start | bytes 393224 | tf_op jit(solution)/shard_map/ppermute | solution.py:394
  48.1 5.8 %collective-permute-start.8 = (bf16[1408,256]{1,0:T(8,128)(2,1)S(1)}, bf16[1408,256]{1,0:T(8,128)(2,1)S(1)}, u32[]{:S(2)}, u32[]{:S(2)}) collective-permute-start(bf16[1408,256]{1,0:T(8,128)(2,1)S(1)} %constant_dynamic-update-slice_fusion.mine), channel_id=1, source_target_pairs={{0,1},{1,0},{2,3},{3,2},{4,5},{5,4},{6,7},{7,6},{8,9},{9,8},{10,11... | collective-permute-start | bytes 2162696 | tf_op jit(solution)/shard_map/ppermute | solution.py:397
  52.1 6.8 %collective-permute-start.4 = (bf16[384,256]{1,0:T(8,128)(2,1)S(1)}, bf16[384,256]{1,0:T(8,128)(2,1)S(1)}, u32[]{:S(2)}, u32[]{:S(2)}) collective-permute-start(bf16[384,256]{1,0:T(8,128)(2,1)S(1)} %pad_maximum_fusion), channel_id=1, source_target_pairs={{0,2},{1,3},{2,0},{3,1},{4,6},{5,7},{6,4},{7,5},{8,10},{9,11},{10,... | collective-permute-start | bytes 589832 | tf_op jit(solution)/shard_map/ppermute | solution.py:394
  58.9 1.9 %collective-permute-start.9 = (bf16[384,256]{1,0:T(8,128)(2,1)S(1)}, bf16[384,256]{1,0:T(8,128)(2,1)S(1)}, u32[]{:S(2)}, u32[]{:S(2)}) collective-permute-start(bf16[384,256]{1,0:T(8,128)(2,1)S(1)} %collective-permute-done.4.mine), channel_id=1, source_target_pairs={{0,1},{1,0},{2,3},{3,2},{4,5},{5,4},{6,7},{7,6},{8,9},{9,8},{10,11... | collective-permute-start | bytes 589832 | tf_op jit(solution)/shard_map/ppermute | solution.py:397

commit v4 on v3

--- a/solution.py
+++ b/solution.py
@@ -25,8 +25,6 @@
 COUNTS = 64
 NEAR_SIZES = (2, 4, 6, 8, 10, 12, 16)
 FAR_SIZES = (0, 2, 4, 6, 8, 16)
-
-VMEM_ALL = 60 << 20
 
 
 def project_kernel(feat_hbm, gain_hbm, weight_hbm, out, feat, gain, weight, sems):
@@ -67,7 +65,7 @@
 def project(features, norm_gain, kv_weight, heads):
     tokens, width = features.shape
     cols = kv_weight.shape[1] // heads
-    blocks = 8
+    blocks = 4
     anywhere = pl.BlockSpec(memory_space=pl.ANY)
     return pl.pallas_call(
         project_kernel,
@@ -80,7 +78,7 @@
             pltpu.VMEM((blocks, width, kv_weight.shape[1] // blocks), kv_weight.dtype),
             pltpu.SemaphoreType.DMA((blocks + 2,)),
         ],
-        compiler_params=pltpu.CompilerParams(vmem_limit_bytes=VMEM_ALL),
+        compiler_params=pltpu.CompilerParams(vmem_limit_bytes=60 << 20),
         name="project",
     )(features, norm_gain.reshape(1, width), kv_weight)
 
@@ -405,7 +403,7 @@
     down23 = along_z(high, -2)
     up23 = along_z(low, 2)
     low_y = along_y(low)
-    up4 = along_z(low[:tok_dev], 4)
+    up4 = along_z(high[tok_dev:], -3)
     falling = join(down23, along_y(down23))
     rising = join(up23, up4)
     far = along_y(rising)

time: 63.4 us -> 64.1 us (1.011)
  Pallas kernels: 19.1 us -> 17.9 us
  starting transfers between devices: 23.2 us -> 24.2 us
  waiting for transfers between devices: 19.7 us -> 20.7 us
    ppermute x2, starting transfers between devices: 4.79 us -> 6.85 us  [along_core(): return lax.ppermute(x, 'seq', [(i, i ^ 1) for i in every])]
    pallas_call x1, Pallas kernels: 5.49 us -> 3.97 us  [project(): pl.pallas_call(project_kernel, in_specs=[anywhere] * 3, out_specs=pl.Bloc...]
    ppermute x3, waiting for transfers between devices: 1.48 us -> 2.99 us  [along_y(): return lax.ppermute(x, 'seq', [(i, i ^ 2) for i in every])]
    ppermute x5, waiting for transfers between devices: 10.9 us -> 10.1 us  [along_z(): return lax.ppermute(x, 'seq', [(i, (i + 4 * levels) % seqs) for i in every])]
    ppermute x5, starting transfers between devices: 9.44 us -> 8.8 us  [along_z(): return lax.ppermute(x, 'seq', [(i, (i + 4 * levels) % seqs) for i in every])]
where the time goes in v4:
time: 64.1 us; the launch traced here: 64 us
  starting transfers between devices  24.2 us (38%)
  waiting for transfers between devices  20.7 us (32%)
  Pallas kernels  17.9 us (28%)
  between operations  0.94 us (1%)
    ppermute x5, waiting for transfers between devices, along_z(): return lax.ppermute(x, 'seq', [(i, (i + 4 * levels) % seqs) for i in every])  10.1 us
    ppermute x5, starting transfers between devices, along_z(): return lax.ppermute(x, 'seq', [(i, (i + 4 * levels) % seqs) for i in every])  8.8 us
    all_to_all x1, starting transfers between devices, per_device(): parts = lax.all_to_all(partial, 'section', 0, 0, tiled=True)  7.62 us
    ppermute x2, starting transfers between devices, along_core(): return lax.ppermute(x, 'seq', [(i, i ^ 1) for i in every])  6.85 us
    all_to_all x1, waiting for transfers between devices, per_device(): parts = lax.all_to_all(partial, 'section', 0, 0, tiled=True)  5.03 us
    pallas_call x1, Pallas kernels, attend_near(): pl.pallas_call(functools.partial(near_kernel, blocks_dev), in_specs=[SMEM...  4.02 us
    pallas_call x1, Pallas kernels, per_device(): pl.pallas_call(functools.partial(prepare_kernel, blocks_dev), in_specs=[S...  4.02 us
    pallas_call x1, Pallas kernels, project(): pl.pallas_call(project_kernel, in_specs=[anywhere] * 3, out_specs=pl.Bloc...  3.97 us
  transfers between devices with their start and end apart: 11, of which 9 were waited for; matrix products, arithmetic and copies ran while one was open for 0% of the time, Pallas kernels for 17%

profile of v4, /device:TPU:1, one launch (start us, length us, event | category | flops | bytes accessed | tf_op | source)
XLA Modules:
  0.0 64.0 jit_solution(9047675448057986921)
XLA Ops:
  0.7 4.0 %project.1 = bf16[8,136,256]{2,1,0:T(8,128)(2,1)} custom-call(bf16[128,1024]{1,0:T(8,128)(2,1)} %feat_hbm.1, f32[1,1024]{1,0:T(1,128)} %bitcast.5, bf16[1024,2048]{1,0:T(8,128)(2,1)} %weight_hbm.1), custom_call_target="tpu_custom_call" | custom-call | tf_op jit(solution)/shard_map/project/pallas_call | solution.py:70
  4.7 7.6 %all-to-all-start = ((bf16[8,136,256]{2,1,0:T(8,128)(2,1)}), bf16[8,136,256]{2,1,0:T(8,128)(2,1)S(1)}, u32[]{:S(2)}, u32[]{:S(2)}) async-start(bf16[8,136,256]{2,1,0:T(8,128)(2,1)} %project.1), calls=%async_computation | async-start | bytes 1114112 | tf_op jit(solution)/shard_map/all_to_all | solution.py:365
  12.5 2.8 %attend_own.1 = (f32[6,128,512]{2,1,0:T(8,128)S(1)}, f32[6,8,512]{2,1,0:T(8,128)S(1)}) custom-call(bf16[3,8,128,128]{3,2,1,0:T(8,128)(2,1)S(1)} %copy-done.1, bf16[3,1,128,256]{3,2,1,0:T(8,128)(2,1)S(1)} %copy-done.2), custom_call_target="tpu_custom_call" | custom-call | tf_op jit(solution)/shard_map/attend_own/pallas_call | solution.py:315
  15.3 4.0 %prepare.1.table = s32[896]{0:T(1024)S(1)} custom-call(s32[1]{0:T(128)} %bitcast.place, s32[6,16]{1,0:T(8,128)S(1)} %reshape.18.lists, s32[32,128]{1,0:T(8,128)S(1)} %bitcast.4), custom_call_target="tpu_custom_call" | custom-call | tf_op jit(solution)/shard_map/prepare/pallas_call | solution.py:367
  19.3 5.0 %all-to-all-done.parts = bf16[8,136,256]{2,1,0:T(8,128)(2,1)S(1)} async-done(((bf16[8,136,256]{2,1,0:T(8,128)(2,1)}), bf16[8,136,256]{2,1,0:T(8,128)(2,1)S(1)}, u32[]{:S(2)}, u32[]{:S(2)}) %all-to-all-start) | async-done | bytes 557088 | tf_op jit(solution)/shard_map/all_to_all | solution.py:365
  24.3 0.8 %reduce.1 = (bf16[128,256]{1,0:T(8,128)(2,1)}, bf16[128,256]{1,0:T(8,128)(2,1)S(1)}) custom-call(bf16[8,136,256]{2,1,0:T(8,128)(2,1)S(1)} %all-to-all-done.parts), custom_call_target="tpu_custom_call" | custom-call | tf_op jit(solution)/shard_map/reduce/pallas_call | solution.py:379
  25.1 5.6 %collective-permute-start.1 = (bf16[128,256]{1,0:T(8,128)(2,1)S(1)}, bf16[128,256]{1,0:T(8,128)(2,1)S(1)}, u32[]{:S(2)}, u32[]{:S(2)}) collective-permute-start(bf16[128,256]{1,0:T(8,128)(2,1)S(1)} %get-tuple-element.21), channel_id=1, source_target_pairs={{0,28},{1,29},{2,30},{3,31},{4,0},{5,1},{6,2},{7,3},{8,4},{9,5},{1... | collective-permute-start | bytes 196616 | tf_op jit(solution)/shard_map/ppermute | solution.py:389
  30.7 1.3 %collective-permute-done.1 = bf16[128,256]{1,0:T(8,128)(2,1)S(1)} collective-permute-done((bf16[128,256]{1,0:T(8,128)(2,1)S(1)}, bf16[128,256]{1,0:T(8,128)(2,1)S(1)}, u32[]{:S(2)}, u32[]{:S(2)}) %collective-permute-start.1) | collective-permute-done | bytes 65568 | tf_op jit(solution)/shard_map/ppermute | solution.py:389
  32.0 3.0 %collective-permute-done = bf16[128,256]{1,0:T(8,128)(2,1)S(1)} collective-permute-done((bf16[128,256]{1,0:T(8,128)(2,1)S(1)}, bf16[128,256]{1,0:T(8,128)(2,1)S(1)}, u32[]{:S(2)}, u32[]{:S(2)}) %collective-permute-start) | collective-permute-done | bytes 65568 | tf_op jit(solution)/shard_map/ppermute | solution.py:389
  35.0 0.3 collective-permute-start.6
  35.3 0.4 collective-permute-start.5
  35.7 2.1 %collective-permute-start.2 = (bf16[256,256]{1,0:T(8,128)(2,1)S(1)}, bf16[256,256]{1,0:T(8,128)(2,1)S(1)}, u32[]{:S(2)}, u32[]{:S(2)}) collective-permute-start(bf16[256,256]{1,0:T(8,128)(2,1)S(1)} %get-tuple-element.22), channel_id=1, source_target_pairs={{0,8},{1,9},{2,10},{3,11},{4,12},{5,13},{6,14},{7,15},{8,16},{9,17... | collective-permute-start | bytes 393224 | tf_op jit(solution)/shard_map/ppermute | solution.py:389
  37.9 0.8 %collective-permute-start.3 = (bf16[128,256]{1,0:T(8,128)(2,1)S(1)}, bf16[128,256]{1,0:T(8,128)(2,1)S(1)}, u32[]{:S(2)}, u32[]{:S(2)}) collective-permute-start(bf16[128,256]{1,0:T(8,128)(2,1)S(1)} %slice.3), channel_id=1, source_target_pairs={{0,20},{1,21},{2,22},{3,23},{4,24},{5,25},{6,26},{7,27},{8,28},{9,... | collective-permute-start | bytes 196616 | tf_op jit(solution)/shard_map/ppermute | solution.py:389
  38.7 4.0 %collective-permute-done.6 = bf16[256,256]{1,0:T(8,128)(2,1)S(1)} collective-permute-done((bf16[256,256]{1,0:T(8,128)(2,1)S(1)}, bf16[256,256]{1,0:T(8,128)(2,1)S(1)}, u32[]{:S(2)}, u32[]{:S(2)}) %collective-permute-start.6) | collective-permute-done | bytes 131104 | tf_op jit(solution)/shard_map/ppermute | solution.py:389
  42.9 1.8 %collective-permute-done.3 = bf16[128,256]{1,0:T(8,128)(2,1)S(1)} collective-permute-done((bf16[128,256]{1,0:T(8,128)(2,1)S(1)}, bf16[128,256]{1,0:T(8,128)(2,1)S(1)}, u32[]{:S(2)}, u32[]{:S(2)}) %collective-permute-start.3) | collective-permute-done | bytes 65568 | tf_op jit(solution)/shard_map/ppermute | solution.py:389
  44.7 2.0 %collective-permute-done.7 = bf16[256,256]{1,0:T(8,128)(2,1)S(1)} collective-permute-done((bf16[256,256]{1,0:T(8,128)(2,1)S(1)}, bf16[256,256]{1,0:T(8,128)(2,1)S(1)}, u32[]{:S(2)}, u32[]{:S(2)}) %collective-permute-start.7) | collective-permute-done | bytes 131104 | tf_op jit(solution)/shard_map/ppermute | solution.py:392
  46.8 6.1 %collective-permute-start.8 = (bf16[1408,256]{1,0:T(8,128)(2,1)S(1)}, bf16[1408,256]{1,0:T(8,128)(2,1)S(1)}, u32[]{:S(2)}, u32[]{:S(2)}) collective-permute-start(bf16[1408,256]{1,0:T(8,128)(2,1)S(1)} %constant_dynamic-update-slice_fusion.mine), channel_id=1, source_target_pairs={{0,1},{1,0},{2,3},{3,2},{4,5},{5,4},{6,7},{7,6},{8,9},{9,8},{10,11... | collective-permute-start | bytes 2162696 | tf_op jit(solution)/shard_map/ppermute | solution.py:395
  52.8 0.3 collective-permute-start.4
  53.1 1.5 %collective-permute-done.8.theirs = bf16[1408,256]{1,0:T(8,128)(2,1)S(1)} collective-permute-done((bf16[1408,256]{1,0:T(8,128)(2,1)S(1)}, bf16[1408,256]{1,0:T(8,128)(2,1)S(1)}, u32[]{:S(2)}, u32[]{:S(2)}) %collective-permute-start.8) | collective-permute-done | bytes 720928 | tf_op jit(solution)/shard_map/ppermute | solution.py:395
  54.6 4.0 %attend_near.1 = (f32[6,128,512]{2,1,0:T(8,128)S(1)}, f32[6,8,512]{2,1,0:T(8,128)S(1)}) custom-call(s32[1]{0:T(128)} %bitcast.place, s32[896]{0:T(1024)S(1)} %prepare.1.table, bf16[3,8,128,128]{3,2,1,0:T(8,128)(2,1)S(1)} %copy-done.1, f32[6,128,512]{2,1,0:T(8,128)S(1)} %get-tuple-element.24.old_state, ...), custom_call_target="tpu_custom_call", output_to_operand_aliasing={{0}: (3, {}), {1}: (4, {})} | custom-call | tf_op jit(solution)/shard_map/attend_near/pallas_call | solution.py:326
  58.7 0.9 %collective-permute-done.4.mine = bf16[384,256]{1,0:T(8,128)(2,1)S(1)} collective-permute-done((bf16[384,256]{1,0:T(8,128)(2,1)S(1)}, bf16[384,256]{1,0:T(8,128)(2,1)S(1)}, u32[]{:S(2)}, u32[]{:S(2)}) %collective-permute-start.4) | collective-permute-done | bytes 196640 | tf_op jit(solution)/shard_map/ppermute | solution.py:392
  59.6 0.8 %collective-permute-start.9 = (bf16[384,256]{1,0:T(8,128)(2,1)S(1)}, bf16[384,256]{1,0:T(8,128)(2,1)S(1)}, u32[]{:S(2)}, u32[]{:S(2)}) collective-permute-start(bf16[384,256]{1,0:T(8,128)(2,1)S(1)} %collective-permute-done.4.mine), channel_id=1, source_target_pairs={{0,1},{1,0},{2,3},{3,2},{4,5},{5,4},{6,7},{7,6},{8,9},{9,8},{10,11... | collective-permute-start | bytes 589832 | tf_op jit(solution)/shard_map/ppermute | solution.py:395
  60.4 1.1 %collective-permute-done.9.theirs = bf16[384,256]{1,0:T(8,128)(2,1)S(1)} collective-permute-done((bf16[384,256]{1,0:T(8,128)(2,1)S(1)}, bf16[384,256]{1,0:T(8,128)(2,1)S(1)}, u32[]{:S(2)}, u32[]{:S(2)}) %collective-permute-start.9) | collective-permute-done | bytes 196640 | tf_op jit(solution)/shard_map/ppermute | solution.py:395
  61.5 2.3 %attend_far.1 = bf16[3,8,128,128]{3,2,1,0:T(8,128)(2,1)} custom-call(s32[1]{0:T(128)} %bitcast.place, s32[896]{0:T(1024)S(1)} %prepare.1.table, bf16[3,8,128,128]{3,2,1,0:T(8,128)(2,1)S(1)} %copy-done.1, f32[6,128,512]{2,1,0:T(8,128)S(1)} %get-tuple-element.28.state, f32[6,8,512]{2,1,0:T(8,128)S(1)} %get-tuple-element.29.sums, ...), custom_call_target="tpu_custom_call" | custom-call | tf_op jit(solution)/shard_map/attend_far/pallas_call | solution.py:341
  (24 shorter events, 0.5 us)
Async XLA Ops:
  0.6 11.6 %copy-start = (s32[3,64,16]{1,2,0:T(8,128)S(1)}, s32[3,64,16]{1,2,0:T(8,128)}, u32[]{:S(2)}) copy-start(s32[3,64,16]{1,2,0:T(8,128)} %param.13) | copy-start | bytes 36868
  0.6 11.8 %copy-start.2 = (bf16[3,1,128,256]{3,2,1,0:T(8,128)(2,1)S(1)}, bf16[3,1,128,256]{3,2,1,0:T(8,128)(2,1)}, u32[]{:S(2)}) copy-start(bf16[3,1,128,256]{3,2,1,0:T(8,128)(2,1)} %own.1) | copy-start | bytes 589828
  4.6 7.8 %copy-start.1 = (bf16[3,8,128,128]{3,2,1,0:T(8,128)(2,1)S(1)}, bf16[3,8,128,128]{3,2,1,0:T(8,128)(2,1)}, u32[]{:S(2)}) copy-start(bf16[3,8,128,128]{3,2,1,0:T(8,128)(2,1)} %q.5) | copy-start | bytes 2359300
  4.6 10.6 %copy-start.3 = (s32[4096]{0:T(1024)S(1)}, s32[4096]{0:T(1024)}, u32[]{:S(2)}) copy-start(s32[4096]{0:T(1024)} %param.12) | copy-start | bytes 49156
  4.7 19.7 %all-to-all-start = ((bf16[8,136,256]{2,1,0:T(8,128)(2,1)}), bf16[8,136,256]{2,1,0:T(8,128)(2,1)S(1)}, u32[]{:S(2)}, u32[]{:S(2)}) async-start(bf16[8,136,256]{2,1,0:T(8,128)(2,1)} %project.1), calls=%async_computation | async-start | bytes 1114112 | tf_op jit(solution)/shard_map/all_to_all | solution.py:365
  25.1 6.9 %collective-permute-start.1 = (bf16[128,256]{1,0:T(8,128)(2,1)S(1)}, bf16[128,256]{1,0:T(8,128)(2,1)S(1)}, u32[]{:S(2)}, u32[]{:S(2)}) collective-permute-start(bf16[128,256]{1,0:T(8,128)(2,1)S(1)} %get-tuple-element.21), channel_id=1, source_target_pairs={{0,28},{1,29},{2,30},{3,31},{4,0},{5,1},{6,2},{7,3},{8,4},{9,5},{1... | collective-permute-start | bytes 196616 | tf_op jit(solution)/shard_map/ppermute | solution.py:389
  30.7 4.3 %collective-permute-start = (bf16[128,256]{1,0:T(8,128)(2,1)S(1)}, bf16[128,256]{1,0:T(8,128)(2,1)S(1)}, u32[]{:S(2)}, u32[]{:S(2)}) collective-permute-start(bf16[128,256]{1,0:T(8,128)(2,1)S(1)} %get-tuple-element.21), channel_id=1, source_target_pairs={{0,4},{1,5},{2,6},{3,7},{4,8},{5,9},{6,10},{7,11},{8,12},{9,13},{1... | collective-permute-start | bytes 196616 | tf_op jit(solution)/shard_map/ppermute | solution.py:389
  35.0 7.6 %collective-permute-start.6 = (bf16[256,256]{1,0:T(8,128)(2,1)S(1)}, bf16[256,256]{1,0:T(8,128)(2,1)S(1)}, u32[]{:S(2)}, u32[]{:S(2)}) collective-permute-start(bf16[256,256]{1,0:T(8,128)(2,1)S(1)} %get-tuple-element.23), channel_id=1, source_target_pairs={{0,24},{1,25},{2,26},{3,27},{4,28},{5,29},{6,30},{7,31},{8,0},{9,1... | collective-permute-start | bytes 393224 | tf_op jit(solution)/shard_map/ppermute | solution.py:389
  35.3 7.5 %collective-permute-start.5 = (bf16[256,256]{1,0:T(8,128)(2,1)S(1)}, bf16[256,256]{1,0:T(8,128)(2,1)S(1)}, u32[]{:S(2)}, u32[]{:S(2)}) collective-permute-start(bf16[256,256]{1,0:T(8,128)(2,1)S(1)} %get-tuple-element.22), channel_id=1, source_target_pairs={{0,2},{1,3},{2,0},{3,1},{4,6},{5,7},{6,4},{7,5},{8,10},{9,11},{10,... | collective-permute-start | bytes 393224 | tf_op jit(solution)/shard_map/ppermute | solution.py:392
  35.7 7.1 %collective-permute-start.2 = (bf16[256,256]{1,0:T(8,128)(2,1)S(1)}, bf16[256,256]{1,0:T(8,128)(2,1)S(1)}, u32[]{:S(2)}, u32[]{:S(2)}) collective-permute-start(bf16[256,256]{1,0:T(8,128)(2,1)S(1)} %get-tuple-element.22), channel_id=1, source_target_pairs={{0,8},{1,9},{2,10},{3,11},{4,12},{5,13},{6,14},{7,15},{8,16},{9,17... | collective-permute-start | bytes 393224 | tf_op jit(solution)/shard_map/ppermute | solution.py:389
  37.9 6.8 %collective-permute-start.3 = (bf16[128,256]{1,0:T(8,128)(2,1)S(1)}, bf16[128,256]{1,0:T(8,128)(2,1)S(1)}, u32[]{:S(2)}, u32[]{:S(2)}) collective-permute-start(bf16[128,256]{1,0:T(8,128)(2,1)S(1)} %slice.3), channel_id=1, source_target_pairs={{0,20},{1,21},{2,22},{3,23},{4,24},{5,25},{6,26},{7,27},{8,28},{9,... | collective-permute-start | bytes 196616 | tf_op jit(solution)/shard_map/ppermute | solution.py:389
  42.6 4.1 %collective-permute-start.7 = (bf16[256,256]{1,0:T(8,128)(2,1)S(1)}, bf16[256,256]{1,0:T(8,128)(2,1)S(1)}, u32[]{:S(2)}, u32[]{:S(2)}) collective-permute-start(bf16[256,256]{1,0:T(8,128)(2,1)S(1)} %collective-permute-done.6), channel_id=1, source_target_pairs={{0,2},{1,3},{2,0},{3,1},{4,6},{5,7},{6,4},{7,5},{8,10},{9,11},{10,... | collective-permute-start | bytes 393224 | tf_op jit(solution)/shard_map/ppermute | solution.py:392
  46.8 7.9 %collective-permute-start.8 = (bf16[1408,256]{1,0:T(8,128)(2,1)S(1)}, bf16[1408,256]{1,0:T(8,128)(2,1)S(1)}, u32[]{:S(2)}, u32[]{:S(2)}) collective-permute-start(bf16[1408,256]{1,0:T(8,128)(2,1)S(1)} %constant_dynamic-update-slice_fusion.mine), channel_id=1, source_target_pairs={{0,1},{1,0},{2,3},{3,2},{4,5},{5,4},{6,7},{7,6},{8,9},{9,8},{10,11... | collective-permute-start | bytes 2162696 | tf_op jit(solution)/shard_map/ppermute | solution.py:395
  52.8 6.8 %collective-permute-start.4 = (bf16[384,256]{1,0:T(8,128)(2,1)S(1)}, bf16[384,256]{1,0:T(8,128)(2,1)S(1)}, u32[]{:S(2)}, u32[]{:S(2)}) collective-permute-start(bf16[384,256]{1,0:T(8,128)(2,1)S(1)} %pad_maximum_fusion), channel_id=1, source_target_pairs={{0,2},{1,3},{2,0},{3,1},{4,6},{5,7},{6,4},{7,5},{8,10},{9,11},{10,... | collective-permute-start | bytes 589832 | tf_op jit(solution)/shard_map/ppermute | solution.py:392
  59.6 1.9 %collective-permute-start.9 = (bf16[384,256]{1,0:T(8,128)(2,1)S(1)}, bf16[384,256]{1,0:T(8,128)(2,1)S(1)}, u32[]{:S(2)}, u32[]{:S(2)}) collective-permute-start(bf16[384,256]{1,0:T(8,128)(2,1)S(1)} %collective-permute-done.4.mine), channel_id=1, source_target_pairs={{0,1},{1,0},{2,3},{3,2},{4,5},{5,4},{6,7},{7,6},{8,9},{9,8},{10,11... | collective-permute-start | bytes 589832 | tf_op jit(solution)/shard_map/ppermute | solution.py:395

commit v5 on v4

--- a/solution.py
+++ b/solution.py
@@ -397,9 +397,9 @@
     def join(*arrays):
         return jnp.concatenate(arrays, axis=0)
 
+    down1 = along_z(kv, -1)
     up1 = along_z(kv, 1)
-    down1 = along_z(kv, -1)
-    low, high = lax.optimization_barrier((join(kv, up1), join(kv, down1)))
+    high, low = lax.optimization_barrier((join(kv, down1), join(kv, up1)))
     down23 = along_z(high, -2)
     up23 = along_z(low, 2)
     low_y = along_y(low)

time: 64.1 us -> 64.1 us (level)
  the two profiles are of different devices: /device:TPU:1 before, /device:TPU:97 now
where the time goes in v5:
time: 64.1 us; the launch traced here: 64.2 us
  starting transfers between devices  22.8 us (36%)
  Pallas kernels  22.1 us (34%)
  waiting for transfers between devices  18 us (28%)
  between operations  0.95 us (1%)
    ppermute x5, waiting for transfers between devices, along_z(): return lax.ppermute(x, 'seq', [(i, (i + 4 * levels) % seqs) for i in every])  10.2 us
    ppermute x2, starting transfers between devices, along_core(): return lax.ppermute(x, 'seq', [(i, i ^ 1) for i in every])  7.82 us
    all_to_all x1, starting transfers between devices, per_device(): parts = lax.all_to_all(partial, 'section', 0, 0, tiled=True)  6.79 us
    ppermute x5, starting transfers between devices, along_z(): return lax.ppermute(x, 'seq', [(i, (i + 4 * levels) % seqs) for i in every])  6.49 us
    pallas_call x1, Pallas kernels, attend_far(): pl.pallas_call(functools.partial(far_kernel, blocks_dev), in_specs=[SMEM_...  5.47 us
    pallas_call x1, Pallas kernels, attend_near(): pl.pallas_call(functools.partial(near_kernel, blocks_dev), in_specs=[SMEM...  5.11 us
    all_to_all x1, waiting for transfers between devices, per_device(): parts = lax.all_to_all(partial, 'section', 0, 0, tiled=True)  5.03 us
    pallas_call x1, Pallas kernels, per_device(): pl.pallas_call(functools.partial(prepare_kernel, blocks_dev), in_specs=[S...  4.02 us
  transfers between devices with their start and end apart: 11, of which 8 were waited for; matrix products, arithmetic and copies ran while one was open for 0% of the time, Pallas kernels for 19%

profile of v5, /device:TPU:97, one launch (start us, length us, event | category | flops | bytes accessed | tf_op | source)
XLA Modules:
  0.0 64.2 jit_solution(16038762137351760691)
XLA Ops:
  0.7 4.0 %project.1 = bf16[8,136,256]{2,1,0:T(8,128)(2,1)} custom-call(bf16[128,1024]{1,0:T(8,128)(2,1)} %feat_hbm.1, f32[1,1024]{1,0:T(1,128)} %bitcast.5, bf16[1024,2048]{1,0:T(8,128)(2,1)} %weight_hbm.1), custom_call_target="tpu_custom_call" | custom-call | tf_op jit(solution)/shard_map/project/pallas_call | solution.py:70
  4.7 6.8 %all-to-all-start = ((bf16[8,136,256]{2,1,0:T(8,128)(2,1)}), bf16[8,136,256]{2,1,0:T(8,128)(2,1)S(1)}, u32[]{:S(2)}, u32[]{:S(2)}) async-start(bf16[8,136,256]{2,1,0:T(8,128)(2,1)} %project.1), calls=%async_computation | async-start | bytes 1114112 | tf_op jit(solution)/shard_map/all_to_all | solution.py:365
  11.5 0.1 copy.11
  11.6 2.8 %attend_own.1 = (f32[6,128,512]{2,1,0:T(8,128)S(1)}, f32[6,8,512]{2,1,0:T(8,128)S(1)}) custom-call(bf16[3,8,128,128]{3,2,1,0:T(8,128)(2,1)S(1)} %copy-done.1, bf16[3,1,128,256]{3,2,1,0:T(8,128)(2,1)S(1)} %copy-done.2), custom_call_target="tpu_custom_call" | custom-call | tf_op jit(solution)/shard_map/attend_own/pallas_call | solution.py:315
  14.4 4.0 %prepare.1.table = s32[896]{0:T(1024)S(1)} custom-call(s32[1]{0:T(128)} %bitcast.place, s32[6,16]{1,0:T(8,128)S(1)} %reshape.18.lists, s32[32,128]{1,0:T(8,128)S(1)} %bitcast.4), custom_call_target="tpu_custom_call" | custom-call | tf_op jit(solution)/shard_map/prepare/pallas_call | solution.py:367
  18.5 5.0 %all-to-all-done.parts = bf16[8,136,256]{2,1,0:T(8,128)(2,1)S(1)} async-done(((bf16[8,136,256]{2,1,0:T(8,128)(2,1)}), bf16[8,136,256]{2,1,0:T(8,128)(2,1)S(1)}, u32[]{:S(2)}, u32[]{:S(2)}) %all-to-all-start) | async-done | bytes 557088 | tf_op jit(solution)/shard_map/all_to_all | solution.py:365
  23.5 0.8 %reduce.1 = (bf16[128,256]{1,0:T(8,128)(2,1)}, bf16[128,256]{1,0:T(8,128)(2,1)S(1)}) custom-call(bf16[8,136,256]{2,1,0:T(8,128)(2,1)S(1)} %all-to-all-done.parts), custom_call_target="tpu_custom_call" | custom-call | tf_op jit(solution)/shard_map/reduce/pallas_call | solution.py:379
  24.2 2.9 %collective-permute-start.1 = (bf16[128,256]{1,0:T(8,128)(2,1)S(1)}, bf16[128,256]{1,0:T(8,128)(2,1)S(1)}, u32[]{:S(2)}, u32[]{:S(2)}) collective-permute-start(bf16[128,256]{1,0:T(8,128)(2,1)S(1)} %get-tuple-element.21), channel_id=1, source_target_pairs={{0,4},{1,5},{2,6},{3,7},{4,8},{5,9},{6,10},{7,11},{8,12},{9,13},{1... | collective-permute-start | bytes 196616 | tf_op jit(solution)/shard_map/ppermute | solution.py:389
  27.1 1.3 %collective-permute-done.1 = bf16[128,256]{1,0:T(8,128)(2,1)S(1)} collective-permute-done((bf16[128,256]{1,0:T(8,128)(2,1)S(1)}, bf16[128,256]{1,0:T(8,128)(2,1)S(1)}, u32[]{:S(2)}, u32[]{:S(2)}) %collective-permute-start.1) | collective-permute-done | bytes 65568 | tf_op jit(solution)/shard_map/ppermute | solution.py:389
  28.4 3.0 %collective-permute-done = bf16[128,256]{1,0:T(8,128)(2,1)S(1)} collective-permute-done((bf16[128,256]{1,0:T(8,128)(2,1)S(1)}, bf16[128,256]{1,0:T(8,128)(2,1)S(1)}, u32[]{:S(2)}, u32[]{:S(2)}) %collective-permute-start) | collective-permute-done | bytes 65568 | tf_op jit(solution)/shard_map/ppermute | solution.py:389
  31.4 0.1 collective-permute-start.6
  31.5 0.5 collective-permute-start.5
  32.0 3.5 %collective-permute-start.2 = (bf16[256,256]{1,0:T(8,128)(2,1)S(1)}, bf16[256,256]{1,0:T(8,128)(2,1)S(1)}, u32[]{:S(2)}, u32[]{:S(2)}) collective-permute-start(bf16[256,256]{1,0:T(8,128)(2,1)S(1)} %get-tuple-element.22), channel_id=1, source_target_pairs={{0,8},{1,9},{2,10},{3,11},{4,12},{5,13},{6,14},{7,15},{8,16},{9,17... | collective-permute-start | bytes 393224 | tf_op jit(solution)/shard_map/ppermute | solution.py:389
  35.6 3.0 %collective-permute-done.6 = bf16[256,256]{1,0:T(8,128)(2,1)S(1)} collective-permute-done((bf16[256,256]{1,0:T(8,128)(2,1)S(1)}, bf16[256,256]{1,0:T(8,128)(2,1)S(1)}, u32[]{:S(2)}, u32[]{:S(2)}) %collective-permute-start.6) | collective-permute-done | bytes 131104 | tf_op jit(solution)/shard_map/ppermute | solution.py:389
  38.6 0.3 collective-permute-start.7
  38.9 2.9 %collective-permute-done.3 = bf16[128,256]{1,0:T(8,128)(2,1)S(1)} collective-permute-done((bf16[128,256]{1,0:T(8,128)(2,1)S(1)}, bf16[128,256]{1,0:T(8,128)(2,1)S(1)}, u32[]{:S(2)}, u32[]{:S(2)}) %collective-permute-start.3) | collective-permute-done | bytes 65568 | tf_op jit(solution)/shard_map/ppermute | solution.py:389
  41.8 0.9 %collective-permute-done.7 = bf16[256,256]{1,0:T(8,128)(2,1)S(1)} collective-permute-done((bf16[256,256]{1,0:T(8,128)(2,1)S(1)}, bf16[256,256]{1,0:T(8,128)(2,1)S(1)}, u32[]{:S(2)}, u32[]{:S(2)}) %collective-permute-start.7) | collective-permute-done | bytes 131104 | tf_op jit(solution)/shard_map/ppermute | solution.py:392
  42.7 7.2 %collective-permute-start.8 = (bf16[1408,256]{1,0:T(8,128)(2,1)S(1)}, bf16[1408,256]{1,0:T(8,128)(2,1)S(1)}, u32[]{:S(2)}, u32[]{:S(2)}) collective-permute-start(bf16[1408,256]{1,0:T(8,128)(2,1)S(1)} %constant_dynamic-update-slice_fusion.mine), channel_id=1, source_target_pairs={{0,1},{1,0},{2,3},{3,2},{4,5},{5,4},{6,7},{7,6},{8,9},{9,8},{10,11... | collective-permute-start | bytes 2162696 | tf_op jit(solution)/shard_map/ppermute | solution.py:395
  49.9 0.9 %collective-permute-start.4 = (bf16[384,256]{1,0:T(8,128)(2,1)S(1)}, bf16[384,256]{1,0:T(8,128)(2,1)S(1)}, u32[]{:S(2)}, u32[]{:S(2)}) collective-permute-start(bf16[384,256]{1,0:T(8,128)(2,1)S(1)} %pad_maximum_fusion), channel_id=1, source_target_pairs={{0,2},{1,3},{2,0},{3,1},{4,6},{5,7},{6,4},{7,5},{8,10},{9,11},{10,... | collective-permute-start | bytes 589832 | tf_op jit(solution)/shard_map/ppermute | solution.py:392
  50.8 0.9 %collective-permute-done.8.theirs = bf16[1408,256]{1,0:T(8,128)(2,1)S(1)} collective-permute-done((bf16[1408,256]{1,0:T(8,128)(2,1)S(1)}, bf16[1408,256]{1,0:T(8,128)(2,1)S(1)}, u32[]{:S(2)}, u32[]{:S(2)}) %collective-permute-start.8) | collective-permute-done | bytes 720928 | tf_op jit(solution)/shard_map/ppermute | solution.py:395
  51.7 5.1 %attend_near.1 = (f32[6,128,512]{2,1,0:T(8,128)S(1)}, f32[6,8,512]{2,1,0:T(8,128)S(1)}) custom-call(s32[1]{0:T(128)} %bitcast.place, s32[896]{0:T(1024)S(1)} %prepare.1.table, bf16[3,8,128,128]{3,2,1,0:T(8,128)(2,1)S(1)} %copy-done.1, f32[6,128,512]{2,1,0:T(8,128)S(1)} %get-tuple-element.24.old_state, ...), custom_call_target="tpu_custom_call", output_to_operand_aliasing={{0}: (3, {}), {1}: (4, {})} | custom-call | tf_op jit(solution)/shard_map/attend_near/pallas_call | solution.py:326
  56.8 0.7 %collective-permute-start.9 = (bf16[384,256]{1,0:T(8,128)(2,1)S(1)}, bf16[384,256]{1,0:T(8,128)(2,1)S(1)}, u32[]{:S(2)}, u32[]{:S(2)}) collective-permute-start(bf16[384,256]{1,0:T(8,128)(2,1)S(1)} %collective-permute-done.4.mine), channel_id=1, source_target_pairs={{0,1},{1,0},{2,3},{3,2},{4,5},{5,4},{6,7},{7,6},{8,9},{9,8},{10,11... | collective-permute-start | bytes 589832 | tf_op jit(solution)/shard_map/ppermute | solution.py:395
  57.5 1.1 %collective-permute-done.9.theirs = bf16[384,256]{1,0:T(8,128)(2,1)S(1)} collective-permute-done((bf16[384,256]{1,0:T(8,128)(2,1)S(1)}, bf16[384,256]{1,0:T(8,128)(2,1)S(1)}, u32[]{:S(2)}, u32[]{:S(2)}) %collective-permute-start.9) | collective-permute-done | bytes 196640 | tf_op jit(solution)/shard_map/ppermute | solution.py:395
  58.6 5.5 %attend_far.1 = bf16[3,8,128,128]{3,2,1,0:T(8,128)(2,1)} custom-call(s32[1]{0:T(128)} %bitcast.place, s32[896]{0:T(1024)S(1)} %prepare.1.table, bf16[3,8,128,128]{3,2,1,0:T(8,128)(2,1)S(1)} %copy-done.1, f32[6,128,512]{2,1,0:T(8,128)S(1)} %get-tuple-element.28.state, f32[6,8,512]{2,1,0:T(8,128)S(1)} %get-tuple-element.29.sums, ...), custom_call_target="tpu_custom_call" | custom-call | tf_op jit(solution)/shard_map/attend_far/pallas_call | solution.py:341
  (24 shorter events, 0.3 us)
Async XLA Ops:
  0.6 10.8 %copy-start = (s32[3,64,16]{1,2,0:T(8,128)S(1)}, s32[3,64,16]{1,2,0:T(8,128)}, u32[]{:S(2)}) copy-start(s32[3,64,16]{1,2,0:T(8,128)} %param.13) | copy-start | bytes 36868
  0.6 11.0 %copy-start.2 = (bf16[3,1,128,256]{3,2,1,0:T(8,128)(2,1)S(1)}, bf16[3,1,128,256]{3,2,1,0:T(8,128)(2,1)}, u32[]{:S(2)}) copy-start(bf16[3,1,128,256]{3,2,1,0:T(8,128)(2,1)} %own.1) | copy-start | bytes 589828
  4.6 7.0 %copy-start.1 = (bf16[3,8,128,128]{3,2,1,0:T(8,128)(2,1)S(1)}, bf16[3,8,128,128]{3,2,1,0:T(8,128)(2,1)}, u32[]{:S(2)}) copy-start(bf16[3,8,128,128]{3,2,1,0:T(8,128)(2,1)} %q.5) | copy-start | bytes 2359300
  4.6 9.8 %copy-start.3 = (s32[4096]{0:T(1024)S(1)}, s32[4096]{0:T(1024)}, u32[]{:S(2)}) copy-start(s32[4096]{0:T(1024)} %param.12) | copy-start | bytes 49156
  4.7 18.8 %all-to-all-start = ((bf16[8,136,256]{2,1,0:T(8,128)(2,1)}), bf16[8,136,256]{2,1,0:T(8,128)(2,1)S(1)}, u32[]{:S(2)}, u32[]{:S(2)}) async-start(bf16[8,136,256]{2,1,0:T(8,128)(2,1)} %project.1), calls=%async_computation | async-start | bytes 1114112 | tf_op jit(solution)/shard_map/all_to_all | solution.py:365
  24.2 4.2 %collective-permute-start.1 = (bf16[128,256]{1,0:T(8,128)(2,1)S(1)}, bf16[128,256]{1,0:T(8,128)(2,1)S(1)}, u32[]{:S(2)}, u32[]{:S(2)}) collective-permute-start(bf16[128,256]{1,0:T(8,128)(2,1)S(1)} %get-tuple-element.21), channel_id=1, source_target_pairs={{0,4},{1,5},{2,6},{3,7},{4,8},{5,9},{6,10},{7,11},{8,12},{9,13},{1... | collective-permute-start | bytes 196616 | tf_op jit(solution)/shard_map/ppermute | solution.py:389
  27.1 4.3 %collective-permute-start = (bf16[128,256]{1,0:T(8,128)(2,1)S(1)}, bf16[128,256]{1,0:T(8,128)(2,1)S(1)}, u32[]{:S(2)}, u32[]{:S(2)}) collective-permute-start(bf16[128,256]{1,0:T(8,128)(2,1)S(1)} %get-tuple-element.21), channel_id=1, source_target_pairs={{0,28},{1,29},{2,30},{3,31},{4,0},{5,1},{6,2},{7,3},{8,4},{9,5},{1... | collective-permute-start | bytes 196616 | tf_op jit(solution)/shard_map/ppermute | solution.py:389
  31.4 7.1 %collective-permute-start.6 = (bf16[256,256]{1,0:T(8,128)(2,1)S(1)}, bf16[256,256]{1,0:T(8,128)(2,1)S(1)}, u32[]{:S(2)}, u32[]{:S(2)}) collective-permute-start(bf16[256,256]{1,0:T(8,128)(2,1)S(1)} %get-tuple-element.23), channel_id=1, source_target_pairs={{0,24},{1,25},{2,26},{3,27},{4,28},{5,29},{6,30},{7,31},{8,0},{9,1... | collective-permute-start | bytes 393224 | tf_op jit(solution)/shard_map/ppermute | solution.py:389
  31.5 7.4 %collective-permute-start.5 = (bf16[256,256]{1,0:T(8,128)(2,1)S(1)}, bf16[256,256]{1,0:T(8,128)(2,1)S(1)}, u32[]{:S(2)}, u32[]{:S(2)}) collective-permute-start(bf16[256,256]{1,0:T(8,128)(2,1)S(1)} %get-tuple-element.22), channel_id=1, source_target_pairs={{0,2},{1,3},{2,0},{3,1},{4,6},{5,7},{6,4},{7,5},{8,10},{9,11},{10,... | collective-permute-start | bytes 393224 | tf_op jit(solution)/shard_map/ppermute | solution.py:392
  32.0 6.9 %collective-permute-start.2 = (bf16[256,256]{1,0:T(8,128)(2,1)S(1)}, bf16[256,256]{1,0:T(8,128)(2,1)S(1)}, u32[]{:S(2)}, u32[]{:S(2)}) collective-permute-start(bf16[256,256]{1,0:T(8,128)(2,1)S(1)} %get-tuple-element.22), channel_id=1, source_target_pairs={{0,8},{1,9},{2,10},{3,11},{4,12},{5,13},{6,14},{7,15},{8,16},{9,17... | collective-permute-start | bytes 393224 | tf_op jit(solution)/shard_map/ppermute | solution.py:389
  35.5 6.3 %collective-permute-start.3 = (bf16[128,256]{1,0:T(8,128)(2,1)S(1)}, bf16[128,256]{1,0:T(8,128)(2,1)S(1)}, u32[]{:S(2)}, u32[]{:S(2)}) collective-permute-start(bf16[128,256]{1,0:T(8,128)(2,1)S(1)} %slice.3), channel_id=1, source_target_pairs={{0,20},{1,21},{2,22},{3,23},{4,24},{5,25},{6,26},{7,27},{8,28},{9,... | collective-permute-start | bytes 196616 | tf_op jit(solution)/shard_map/ppermute | solution.py:389
  38.6 4.1 %collective-permute-start.7 = (bf16[256,256]{1,0:T(8,128)(2,1)S(1)}, bf16[256,256]{1,0:T(8,128)(2,1)S(1)}, u32[]{:S(2)}, u32[]{:S(2)}) collective-permute-start(bf16[256,256]{1,0:T(8,128)(2,1)S(1)} %collective-permute-done.6), channel_id=1, source_target_pairs={{0,2},{1,3},{2,0},{3,1},{4,6},{5,7},{6,4},{7,5},{8,10},{9,11},{10,... | collective-permute-start | bytes 393224 | tf_op jit(solution)/shard_map/ppermute | solution.py:392
  42.7 9.0 %collective-permute-start.8 = (bf16[1408,256]{1,0:T(8,128)(2,1)S(1)}, bf16[1408,256]{1,0:T(8,128)(2,1)S(1)}, u32[]{:S(2)}, u32[]{:S(2)}) collective-permute-start(bf16[1408,256]{1,0:T(8,128)(2,1)S(1)} %constant_dynamic-update-slice_fusion.mine), channel_id=1, source_target_pairs={{0,1},{1,0},{2,3},{3,2},{4,5},{5,4},{6,7},{7,6},{8,9},{9,8},{10,11... | collective-permute-start | bytes 2162696 | tf_op jit(solution)/shard_map/ppermute | solution.py:395
  49.9 6.9 %collective-permute-start.4 = (bf16[384,256]{1,0:T(8,128)(2,1)S(1)}, bf16[384,256]{1,0:T(8,128)(2,1)S(1)}, u32[]{:S(2)}, u32[]{:S(2)}) collective-permute-start(bf16[384,256]{1,0:T(8,128)(2,1)S(1)} %pad_maximum_fusion), channel_id=1, source_target_pairs={{0,2},{1,3},{2,0},{3,1},{4,6},{5,7},{6,4},{7,5},{8,10},{9,11},{10,... | collective-permute-start | bytes 589832 | tf_op jit(solution)/shard_map/ppermute | solution.py:392
  56.8 1.7 %collective-permute-start.9 = (bf16[384,256]{1,0:T(8,128)(2,1)S(1)}, bf16[384,256]{1,0:T(8,128)(2,1)S(1)}, u32[]{:S(2)}, u32[]{:S(2)}) collective-permute-start(bf16[384,256]{1,0:T(8,128)(2,1)S(1)} %collective-permute-done.4.mine), channel_id=1, source_target_pairs={{0,1},{1,0},{2,3},{3,2},{4,5},{5,4},{6,7},{7,6},{8,9},{9,8},{10,11... | collective-permute-start | bytes 589832 | tf_op jit(solution)/shard_map/ppermute | solution.py:395

commit v6 on v5

--- a/solution.py
+++ b/solution.py
@@ -385,8 +385,11 @@
 
     every = range(seqs)
 
-    def along_z(x, levels):
-        return lax.ppermute(x, "seq", [(i, (i + 4 * levels) % seqs) for i in every])
+    levels = range(seqs // 4)
+
+    def along_z(x, moves):
+        pairs = [(4 * source + i, 4 * goal + i) for source, goal in moves for i in range(4)]
+        return lax.ppermute(x, "seq", sorted(pairs))
 
     def along_y(x):
         return lax.ppermute(x, "seq", [(i, i ^ 2) for i in every])
@@ -397,13 +400,13 @@
     def join(*arrays):
         return jnp.concatenate(arrays, axis=0)
 
-    down1 = along_z(kv, -1)
-    up1 = along_z(kv, 1)
+    down1 = along_z(kv, [(3, 2), (2, 1), (1, 0), (0, 7)])
+    up1 = along_z(kv, [(z, z + 1) for z in levels[:-1]])
     high, low = lax.optimization_barrier((join(kv, down1), join(kv, up1)))
-    down23 = along_z(high, -2)
-    up23 = along_z(low, 2)
+    down23 = along_z(high, [(1, 7), (0, 6), (7, 5)])
+    up23 = along_z(low, [(z, z + 2) for z in levels[:-2]])
     low_y = along_y(low)
-    up4 = along_z(high[tok_dev:], -3)
+    up4 = along_z(high[tok_dev:], [(7, 4), (0, 5), (1, 6), (2, 7)])
     falling = join(down23, along_y(down23))
     rising = join(up23, up4)
     far = along_y(rising)

time: 64.1 us -> 65.6 us (1.023)
  the two profiles are of different devices: /device:TPU:97 before, /device:TPU:1 now
where the time goes in v6:
time: 65.6 us; the launch traced here: 65.4 us
  starting transfers between devices  34.9 us (53%)
  Pallas kernels  17.6 us (27%)
  waiting for transfers between devices  11.8 us (18%)
  between operations  0.83 us (1%)
    ppermute x5, starting transfers between devices, along_z(): return lax.ppermute(x, 'seq', sorted(pairs))  19.6 us
    all_to_all x1, starting transfers between devices, per_device(): parts = lax.all_to_all(partial, 'section', 0, 0, tiled=True)  7.62 us
    all_to_all x1, waiting for transfers between devices, per_device(): parts = lax.all_to_all(partial, 'section', 0, 0, tiled=True)  5.03 us
    ppermute x2, starting transfers between devices, along_core(): return lax.ppermute(x, 'seq', [(i, i ^ 1) for i in every])  4.87 us
    pallas_call x1, Pallas kernels, per_device(): pl.pallas_call(functools.partial(prepare_kernel, blocks_dev), in_specs=[S...  4.02 us
    pallas_call x1, Pallas kernels, project(): pl.pallas_call(project_kernel, in_specs=[anywhere] * 3, out_specs=pl.Bloc...  3.97 us
    pallas_call x1, Pallas kernels, attend_near(): pl.pallas_call(functools.partial(near_kernel, blocks_dev), in_specs=[SMEM...  3.76 us
    ppermute x3, waiting for transfers between devices, along_y(): return lax.ppermute(x, 'seq', [(i, i ^ 2) for i in every])  3.04 us
  transfers between devices with their start and end apart: 11, of which 7 were waited for; matrix products, arithmetic and copies ran while one was open for 0% of the time, Pallas kernels for 16%

profile of v6, /device:TPU:1, one launch (start us, length us, event | category | flops | bytes accessed | tf_op | source)
XLA Modules:
  0.0 65.4 jit_solution(16295453213395164023)
XLA Ops:
  0.7 4.0 %project.1 = bf16[8,136,256]{2,1,0:T(8,128)(2,1)} custom-call(bf16[128,1024]{1,0:T(8,128)(2,1)} %feat_hbm.1, f32[1,1024]{1,0:T(1,128)} %bitcast.5, bf16[1024,2048]{1,0:T(8,128)(2,1)} %weight_hbm.1), custom_call_target="tpu_custom_call" | custom-call | tf_op jit(solution)/shard_map/project/pallas_call | solution.py:70
  4.7 7.6 %all-to-all-start = ((bf16[8,136,256]{2,1,0:T(8,128)(2,1)}), bf16[8,136,256]{2,1,0:T(8,128)(2,1)S(1)}, u32[]{:S(2)}, u32[]{:S(2)}) async-start(bf16[8,136,256]{2,1,0:T(8,128)(2,1)} %project.1), calls=%async_computation | async-start | bytes 1114112 | tf_op jit(solution)/shard_map/all_to_all | solution.py:365
  12.5 2.8 %attend_own.1 = (f32[6,128,512]{2,1,0:T(8,128)S(1)}, f32[6,8,512]{2,1,0:T(8,128)S(1)}) custom-call(bf16[3,8,128,128]{3,2,1,0:T(8,128)(2,1)S(1)} %copy-done.1, bf16[3,1,128,256]{3,2,1,0:T(8,128)(2,1)S(1)} %copy-done.2), custom_call_target="tpu_custom_call" | custom-call | tf_op jit(solution)/shard_map/attend_own/pallas_call | solution.py:315
  15.3 4.0 %prepare.1.table = s32[896]{0:T(1024)S(1)} custom-call(s32[1]{0:T(128)} %bitcast.place, s32[6,16]{1,0:T(8,128)S(1)} %reshape.18.lists, s32[32,128]{1,0:T(8,128)S(1)} %bitcast.4), custom_call_target="tpu_custom_call" | custom-call | tf_op jit(solution)/shard_map/prepare/pallas_call | solution.py:367
  19.3 5.0 %all-to-all-done.parts = bf16[8,136,256]{2,1,0:T(8,128)(2,1)S(1)} async-done(((bf16[8,136,256]{2,1,0:T(8,128)(2,1)}), bf16[8,136,256]{2,1,0:T(8,128)(2,1)S(1)}, u32[]{:S(2)}, u32[]{:S(2)}) %all-to-all-start) | async-done | bytes 557088 | tf_op jit(solution)/shard_map/all_to_all | solution.py:365
  24.3 0.8 %reduce.1 = (bf16[128,256]{1,0:T(8,128)(2,1)}, bf16[128,256]{1,0:T(8,128)(2,1)S(1)}) custom-call(bf16[8,136,256]{2,1,0:T(8,128)(2,1)S(1)} %all-to-all-done.parts), custom_call_target="tpu_custom_call" | custom-call | tf_op jit(solution)/shard_map/reduce/pallas_call | solution.py:379
  25.1 3.5 %collective-permute-start.1 = (bf16[128,256]{1,0:T(8,128)(2,1)S(1)}, bf16[128,256]{1,0:T(8,128)(2,1)S(1)}, u32[]{:S(2)}, u32[]{:S(2)}) collective-permute-start(bf16[128,256]{1,0:T(8,128)(2,1)S(1)} %get-tuple-element.21), channel_id=1, source_target_pairs={{0,4},{1,5},{2,6},{3,7},{4,8},{5,9},{6,10},{7,11},{8,12},{9,13},{1... | collective-permute-start | bytes 196616 | tf_op jit(solution)/shard_map/ppermute | solution.py:392
  28.6 5.2 %collective-permute-start = (bf16[128,256]{1,0:T(8,128)(2,1)S(1)}, bf16[128,256]{1,0:T(8,128)(2,1)S(1)}, u32[]{:S(2)}, u32[]{:S(2)}) collective-permute-start(bf16[128,256]{1,0:T(8,128)(2,1)S(1)} %get-tuple-element.21), channel_id=1, source_target_pairs={{0,28},{1,29},{2,30},{3,31},{4,0},{5,1},{6,2},{7,3},{8,4},{9,5},{1... | collective-permute-start | bytes 196616 | tf_op jit(solution)/shard_map/ppermute | solution.py:392
  33.9 1.3 %collective-permute-done = bf16[128,256]{1,0:T(8,128)(2,1)S(1)} collective-permute-done((bf16[128,256]{1,0:T(8,128)(2,1)S(1)}, bf16[128,256]{1,0:T(8,128)(2,1)S(1)}, u32[]{:S(2)}, u32[]{:S(2)}) %collective-permute-start) | collective-permute-done | bytes 65568 | tf_op jit(solution)/shard_map/ppermute | solution.py:392
  35.2 2.8 %collective-permute-start.6 = (bf16[256,256]{1,0:T(8,128)(2,1)S(1)}, bf16[256,256]{1,0:T(8,128)(2,1)S(1)}, u32[]{:S(2)}, u32[]{:S(2)}) collective-permute-start(bf16[256,256]{1,0:T(8,128)(2,1)S(1)} %get-tuple-element.23), channel_id=1, source_target_pairs={{0,24},{1,25},{2,26},{3,27},{4,28},{5,29},{6,30},{7,31},{28,20},{2... | collective-permute-start | bytes 393224 | tf_op jit(solution)/shard_map/ppermute | solution.py:392
  38.0 0.5 collective-permute-start.5
  38.5 1.9 %collective-permute-start.2 = (bf16[256,256]{1,0:T(8,128)(2,1)S(1)}, bf16[256,256]{1,0:T(8,128)(2,1)S(1)}, u32[]{:S(2)}, u32[]{:S(2)}) collective-permute-start(bf16[256,256]{1,0:T(8,128)(2,1)S(1)} %get-tuple-element.22), channel_id=1, source_target_pairs={{0,8},{1,9},{2,10},{3,11},{4,12},{5,13},{6,14},{7,15},{8,16},{9,17... | collective-permute-start | bytes 393224 | tf_op jit(solution)/shard_map/ppermute | solution.py:392
  40.5 6.0 %collective-permute-start.3 = (bf16[128,256]{1,0:T(8,128)(2,1)S(1)}, bf16[128,256]{1,0:T(8,128)(2,1)S(1)}, u32[]{:S(2)}, u32[]{:S(2)}) collective-permute-start(bf16[128,256]{1,0:T(8,128)(2,1)S(1)} %slice.3), channel_id=1, source_target_pairs={{0,20},{1,21},{2,22},{3,23},{4,24},{5,25},{6,26},{7,27},{8,28},{9,... | collective-permute-start | bytes 196616 | tf_op jit(solution)/shard_map/ppermute | solution.py:392
  46.5 1.2 %collective-permute-start.7 = (bf16[256,256]{1,0:T(8,128)(2,1)S(1)}, bf16[256,256]{1,0:T(8,128)(2,1)S(1)}, u32[]{:S(2)}, u32[]{:S(2)}) collective-permute-start(bf16[256,256]{1,0:T(8,128)(2,1)S(1)} %collective-permute-done.6), channel_id=1, source_target_pairs={{0,2},{1,3},{2,0},{3,1},{4,6},{5,7},{6,4},{7,5},{8,10},{9,11},{10,... | collective-permute-start | bytes 393224 | tf_op jit(solution)/shard_map/ppermute | solution.py:395
  47.7 0.7 %collective-permute-done.3 = bf16[128,256]{1,0:T(8,128)(2,1)S(1)} collective-permute-done((bf16[128,256]{1,0:T(8,128)(2,1)S(1)}, bf16[128,256]{1,0:T(8,128)(2,1)S(1)}, u32[]{:S(2)}, u32[]{:S(2)}) %collective-permute-start.3) | collective-permute-done | bytes 65568 | tf_op jit(solution)/shard_map/ppermute | solution.py:392
  48.4 2.0 %collective-permute-done.7 = bf16[256,256]{1,0:T(8,128)(2,1)S(1)} collective-permute-done((bf16[256,256]{1,0:T(8,128)(2,1)S(1)}, bf16[256,256]{1,0:T(8,128)(2,1)S(1)}, u32[]{:S(2)}, u32[]{:S(2)}) %collective-permute-start.7) | collective-permute-done | bytes 131104 | tf_op jit(solution)/shard_map/ppermute | solution.py:395
  50.5 4.1 %collective-permute-start.8 = (bf16[1408,256]{1,0:T(8,128)(2,1)S(1)}, bf16[1408,256]{1,0:T(8,128)(2,1)S(1)}, u32[]{:S(2)}, u32[]{:S(2)}) collective-permute-start(bf16[1408,256]{1,0:T(8,128)(2,1)S(1)} %constant_dynamic-update-slice_fusion.mine), channel_id=1, source_target_pairs={{0,1},{1,0},{2,3},{3,2},{4,5},{5,4},{6,7},{7,6},{8,9},{9,8},{10,11... | collective-permute-start | bytes 2162696 | tf_op jit(solution)/shard_map/ppermute | solution.py:398
  54.5 1.2 %collective-permute-start.4 = (bf16[384,256]{1,0:T(8,128)(2,1)S(1)}, bf16[384,256]{1,0:T(8,128)(2,1)S(1)}, u32[]{:S(2)}, u32[]{:S(2)}) collective-permute-start(bf16[384,256]{1,0:T(8,128)(2,1)S(1)} %pad_maximum_fusion), channel_id=1, source_target_pairs={{0,2},{1,3},{2,0},{3,1},{4,6},{5,7},{6,4},{7,5},{8,10},{9,11},{10,... | collective-permute-start | bytes 589832 | tf_op jit(solution)/shard_map/ppermute | solution.py:395
  55.7 0.6 collective-permute-done.8.theirs
  56.4 3.8 %attend_near.1 = (f32[6,128,512]{2,1,0:T(8,128)S(1)}, f32[6,8,512]{2,1,0:T(8,128)S(1)}) custom-call(s32[1]{0:T(128)} %bitcast.place, s32[896]{0:T(1024)S(1)} %prepare.1.table, bf16[3,8,128,128]{3,2,1,0:T(8,128)(2,1)S(1)} %copy-done.1, f32[6,128,512]{2,1,0:T(8,128)S(1)} %get-tuple-element.24.old_state, ...), custom_call_target="tpu_custom_call", output_to_operand_aliasing={{0}: (3, {}), {1}: (4, {})} | custom-call | tf_op jit(solution)/shard_map/attend_near/pallas_call | solution.py:326
  60.1 1.0 %collective-permute-done.4.mine = bf16[384,256]{1,0:T(8,128)(2,1)S(1)} collective-permute-done((bf16[384,256]{1,0:T(8,128)(2,1)S(1)}, bf16[384,256]{1,0:T(8,128)(2,1)S(1)}, u32[]{:S(2)}, u32[]{:S(2)}) %collective-permute-start.4) | collective-permute-done | bytes 196640 | tf_op jit(solution)/shard_map/ppermute | solution.py:395
  61.2 0.8 %collective-permute-start.9 = (bf16[384,256]{1,0:T(8,128)(2,1)S(1)}, bf16[384,256]{1,0:T(8,128)(2,1)S(1)}, u32[]{:S(2)}, u32[]{:S(2)}) collective-permute-start(bf16[384,256]{1,0:T(8,128)(2,1)S(1)} %collective-permute-done.4.mine), channel_id=1, source_target_pairs={{0,1},{1,0},{2,3},{3,2},{4,5},{5,4},{6,7},{7,6},{8,9},{9,8},{10,11... | collective-permute-start | bytes 589832 | tf_op jit(solution)/shard_map/ppermute | solution.py:398
  62.0 1.1 %collective-permute-done.9.theirs = bf16[384,256]{1,0:T(8,128)(2,1)S(1)} collective-permute-done((bf16[384,256]{1,0:T(8,128)(2,1)S(1)}, bf16[384,256]{1,0:T(8,128)(2,1)S(1)}, u32[]{:S(2)}, u32[]{:S(2)}) %collective-permute-start.9) | collective-permute-done | bytes 196640 | tf_op jit(solution)/shard_map/ppermute | solution.py:398
  63.0 2.3 %attend_far.1 = bf16[3,8,128,128]{3,2,1,0:T(8,128)(2,1)} custom-call(s32[1]{0:T(128)} %bitcast.place, s32[896]{0:T(1024)S(1)} %prepare.1.table, bf16[3,8,128,128]{3,2,1,0:T(8,128)(2,1)S(1)} %copy-done.1, f32[6,128,512]{2,1,0:T(8,128)S(1)} %get-tuple-element.28.state, f32[6,8,512]{2,1,0:T(8,128)S(1)} %get-tuple-element.29.sums, ...), custom_call_target="tpu_custom_call" | custom-call | tf_op jit(solution)/shard_map/attend_far/pallas_call | solution.py:341
  (24 shorter events, 0.3 us)
Async XLA Ops:
  0.6 11.7 %copy-start = (s32[3,64,16]{1,2,0:T(8,128)S(1)}, s32[3,64,16]{1,2,0:T(8,128)}, u32[]{:S(2)}) copy-start(s32[3,64,16]{1,2,0:T(8,128)} %param.13) | copy-start | bytes 36868
  0.6 11.8 %copy-start.2 = (bf16[3,1,128,256]{3,2,1,0:T(8,128)(2,1)S(1)}, bf16[3,1,128,256]{3,2,1,0:T(8,128)(2,1)}, u32[]{:S(2)}) copy-start(bf16[3,1,128,256]{3,2,1,0:T(8,128)(2,1)} %own.1) | copy-start | bytes 589828
  4.6 7.8 %copy-start.1 = (bf16[3,8,128,128]{3,2,1,0:T(8,128)(2,1)S(1)}, bf16[3,8,128,128]{3,2,1,0:T(8,128)(2,1)}, u32[]{:S(2)}) copy-start(bf16[3,8,128,128]{3,2,1,0:T(8,128)(2,1)} %q.5) | copy-start | bytes 2359300
  4.6 10.6 %copy-start.3 = (s32[4096]{0:T(1024)S(1)}, s32[4096]{0:T(1024)}, u32[]{:S(2)}) copy-start(s32[4096]{0:T(1024)} %param.12) | copy-start | bytes 49156
  4.7 19.7 %all-to-all-start = ((bf16[8,136,256]{2,1,0:T(8,128)(2,1)}), bf16[8,136,256]{2,1,0:T(8,128)(2,1)S(1)}, u32[]{:S(2)}, u32[]{:S(2)}) async-start(bf16[8,136,256]{2,1,0:T(8,128)(2,1)} %project.1), calls=%async_computation | async-start | bytes 1114112 | tf_op jit(solution)/shard_map/all_to_all | solution.py:365
  25.1 8.8 %collective-permute-start.1 = (bf16[128,256]{1,0:T(8,128)(2,1)S(1)}, bf16[128,256]{1,0:T(8,128)(2,1)S(1)}, u32[]{:S(2)}, u32[]{:S(2)}) collective-permute-start(bf16[128,256]{1,0:T(8,128)(2,1)S(1)} %get-tuple-element.21), channel_id=1, source_target_pairs={{0,4},{1,5},{2,6},{3,7},{4,8},{5,9},{6,10},{7,11},{8,12},{9,13},{1... | collective-permute-start | bytes 196616 | tf_op jit(solution)/shard_map/ppermute | solution.py:392
  28.6 6.5 %collective-permute-start = (bf16[128,256]{1,0:T(8,128)(2,1)S(1)}, bf16[128,256]{1,0:T(8,128)(2,1)S(1)}, u32[]{:S(2)}, u32[]{:S(2)}) collective-permute-start(bf16[128,256]{1,0:T(8,128)(2,1)S(1)} %get-tuple-element.21), channel_id=1, source_target_pairs={{0,28},{1,29},{2,30},{3,31},{4,0},{5,1},{6,2},{7,3},{8,4},{9,5},{1... | collective-permute-start | bytes 196616 | tf_op jit(solution)/shard_map/ppermute | solution.py:392
  35.2 11.3 %collective-permute-start.6 = (bf16[256,256]{1,0:T(8,128)(2,1)S(1)}, bf16[256,256]{1,0:T(8,128)(2,1)S(1)}, u32[]{:S(2)}, u32[]{:S(2)}) collective-permute-start(bf16[256,256]{1,0:T(8,128)(2,1)S(1)} %get-tuple-element.23), channel_id=1, source_target_pairs={{0,24},{1,25},{2,26},{3,27},{4,28},{5,29},{6,30},{7,31},{28,20},{2... | collective-permute-start | bytes 393224 | tf_op jit(solution)/shard_map/ppermute | solution.py:392
  38.0 9.7 %collective-permute-start.5 = (bf16[256,256]{1,0:T(8,128)(2,1)S(1)}, bf16[256,256]{1,0:T(8,128)(2,1)S(1)}, u32[]{:S(2)}, u32[]{:S(2)}) collective-permute-start(bf16[256,256]{1,0:T(8,128)(2,1)S(1)} %get-tuple-element.22), channel_id=1, source_target_pairs={{0,2},{1,3},{2,0},{3,1},{4,6},{5,7},{6,4},{7,5},{8,10},{9,11},{10,... | collective-permute-start | bytes 393224 | tf_op jit(solution)/shard_map/ppermute | solution.py:395
  38.5 9.2 %collective-permute-start.2 = (bf16[256,256]{1,0:T(8,128)(2,1)S(1)}, bf16[256,256]{1,0:T(8,128)(2,1)S(1)}, u32[]{:S(2)}, u32[]{:S(2)}) collective-permute-start(bf16[256,256]{1,0:T(8,128)(2,1)S(1)} %get-tuple-element.22), channel_id=1, source_target_pairs={{0,8},{1,9},{2,10},{3,11},{4,12},{5,13},{6,14},{7,15},{8,16},{9,17... | collective-permute-start | bytes 393224 | tf_op jit(solution)/shard_map/ppermute | solution.py:392
  40.5 7.9 %collective-permute-start.3 = (bf16[128,256]{1,0:T(8,128)(2,1)S(1)}, bf16[128,256]{1,0:T(8,128)(2,1)S(1)}, u32[]{:S(2)}, u32[]{:S(2)}) collective-permute-start(bf16[128,256]{1,0:T(8,128)(2,1)S(1)} %slice.3), channel_id=1, source_target_pairs={{0,20},{1,21},{2,22},{3,23},{4,24},{5,25},{6,26},{7,27},{8,28},{9,... | collective-permute-start | bytes 196616 | tf_op jit(solution)/shard_map/ppermute | solution.py:392
  46.5 3.9 %collective-permute-start.7 = (bf16[256,256]{1,0:T(8,128)(2,1)S(1)}, bf16[256,256]{1,0:T(8,128)(2,1)S(1)}, u32[]{:S(2)}, u32[]{:S(2)}) collective-permute-start(bf16[256,256]{1,0:T(8,128)(2,1)S(1)} %collective-permute-done.6), channel_id=1, source_target_pairs={{0,2},{1,3},{2,0},{3,1},{4,6},{5,7},{6,4},{7,5},{8,10},{9,11},{10,... | collective-permute-start | bytes 393224 | tf_op jit(solution)/shard_map/ppermute | solution.py:395
  50.5 5.9 %collective-permute-start.8 = (bf16[1408,256]{1,0:T(8,128)(2,1)S(1)}, bf16[1408,256]{1,0:T(8,128)(2,1)S(1)}, u32[]{:S(2)}, u32[]{:S(2)}) collective-permute-start(bf16[1408,256]{1,0:T(8,128)(2,1)S(1)} %constant_dynamic-update-slice_fusion.mine), channel_id=1, source_target_pairs={{0,1},{1,0},{2,3},{3,2},{4,5},{5,4},{6,7},{7,6},{8,9},{9,8},{10,11... | collective-permute-start | bytes 2162696 | tf_op jit(solution)/shard_map/ppermute | solution.py:398
  54.5 6.6 %collective-permute-start.4 = (bf16[384,256]{1,0:T(8,128)(2,1)S(1)}, bf16[384,256]{1,0:T(8,128)(2,1)S(1)}, u32[]{:S(2)}, u32[]{:S(2)}) collective-permute-start(bf16[384,256]{1,0:T(8,128)(2,1)S(1)} %pad_maximum_fusion), channel_id=1, source_target_pairs={{0,2},{1,3},{2,0},{3,1},{4,6},{5,7},{6,4},{7,5},{8,10},{9,11},{10,... | collective-permute-start | bytes 589832 | tf_op jit(solution)/shard_map/ppermute | solution.py:395
  61.2 1.9 %collective-permute-start.9 = (bf16[384,256]{1,0:T(8,128)(2,1)S(1)}, bf16[384,256]{1,0:T(8,128)(2,1)S(1)}, u32[]{:S(2)}, u32[]{:S(2)}) collective-permute-start(bf16[384,256]{1,0:T(8,128)(2,1)S(1)} %collective-permute-done.4.mine), channel_id=1, source_target_pairs={{0,1},{1,0},{2,3},{3,2},{4,5},{5,4},{6,7},{7,6},{8,9},{9,8},{10,11... | collective-permute-start | bytes 589832 | tf_op jit(solution)/shard_map/ppermute | solution.py:398

commit v7 on v5

--- a/solution.py
+++ b/solution.py
@@ -397,7 +397,8 @@
     def join(*arrays):
         return jnp.concatenate(arrays, axis=0)
 
-    down1 = along_z(kv, -1)
+    moves = [(4 * z + i, (4 * z - 4) % seqs + i) for z in range(4) for i in range(4)]
+    down1 = lax.ppermute(kv, "seq", moves)
     up1 = along_z(kv, 1)
     high, low = lax.optimization_barrier((join(kv, down1), join(kv, up1)))
     down23 = along_z(high, -2)

time: 64.1 us -> 62.3 us (0.972)
  the two profiles are of different devices: /device:TPU:97 before, /device:TPU:224 now
where the time goes in v7:
time: 62.3 us; the launch traced here: 62.2 us
  waiting for transfers between devices  25.1 us (40%)
  Pallas kernels  22.1 us (35%)
  starting transfers between devices  13.8 us (22%)
  between operations  0.99 us (2%)
    ppermute x4, waiting for transfers between devices, along_z(): return lax.ppermute(x, 'seq', [(i, (i + 4 * levels) % seqs) for i in every])  10.3 us
    all_to_all x1, starting transfers between devices, per_device(): parts = lax.all_to_all(partial, 'section', 0, 0, tiled=True)  7.08 us
    pallas_call x1, Pallas kernels, attend_near(): pl.pallas_call(functools.partial(near_kernel, blocks_dev), in_specs=[SMEM...  5.79 us
    all_to_all x1, waiting for transfers between devices, per_device(): parts = lax.all_to_all(partial, 'section', 0, 0, tiled=True)  4.92 us
    pallas_call x1, Pallas kernels, attend_far(): pl.pallas_call(functools.partial(far_kernel, blocks_dev), in_specs=[SMEM_...  4.81 us
    ppermute x4, starting transfers between devices, along_z(): return lax.ppermute(x, 'seq', [(i, (i + 4 * levels) % seqs) for i in every])  4.2 us
    pallas_call x1, Pallas kernels, per_device(): pl.pallas_call(functools.partial(prepare_kernel, blocks_dev), in_specs=[S...  4.02 us
    pallas_call x1, Pallas kernels, project(): pl.pallas_call(project_kernel, in_specs=[anywhere] * 3, out_specs=pl.Bloc...  3.97 us
  transfers between devices with their start and end apart: 11, of which 8 were waited for; matrix products, arithmetic and copies ran while one was open for 0% of the time, Pallas kernels for 20%

profile of v7, /device:TPU:224, one launch (start us, length us, event | category | flops | bytes accessed | tf_op | source)
XLA Modules:
  0.0 62.2 jit_solution(11127545993084033268)
XLA Ops:
  0.7 4.0 %project.1 = bf16[8,136,256]{2,1,0:T(8,128)(2,1)} custom-call(bf16[128,1024]{1,0:T(8,128)(2,1)} %feat_hbm.1, f32[1,1024]{1,0:T(1,128)} %bitcast.5, bf16[1024,2048]{1,0:T(8,128)(2,1)} %weight_hbm.1), custom_call_target="tpu_custom_call" | custom-call | tf_op jit(solution)/shard_map/project/pallas_call | solution.py:70
  4.7 7.1 %all-to-all-start = ((bf16[8,136,256]{2,1,0:T(8,128)(2,1)}), bf16[8,136,256]{2,1,0:T(8,128)(2,1)S(1)}, u32[]{:S(2)}, u32[]{:S(2)}) async-start(bf16[8,136,256]{2,1,0:T(8,128)(2,1)} %project.1), calls=%async_computation | async-start | bytes 1114112 | tf_op jit(solution)/shard_map/all_to_all | solution.py:365
  11.8 0.1 copy.11
  11.9 2.8 %attend_own.1 = (f32[6,128,512]{2,1,0:T(8,128)S(1)}, f32[6,8,512]{2,1,0:T(8,128)S(1)}) custom-call(bf16[3,8,128,128]{3,2,1,0:T(8,128)(2,1)S(1)} %copy-done.1, bf16[3,1,128,256]{3,2,1,0:T(8,128)(2,1)S(1)} %copy-done.2), custom_call_target="tpu_custom_call" | custom-call | tf_op jit(solution)/shard_map/attend_own/pallas_call | solution.py:315
  14.7 4.0 %prepare.1.table = s32[896]{0:T(1024)S(1)} custom-call(s32[1]{0:T(128)} %bitcast.place, s32[6,16]{1,0:T(8,128)S(1)} %reshape.18.lists, s32[32,128]{1,0:T(8,128)S(1)} %bitcast.4), custom_call_target="tpu_custom_call" | custom-call | tf_op jit(solution)/shard_map/prepare/pallas_call | solution.py:367
  18.8 4.9 %all-to-all-done.parts = bf16[8,136,256]{2,1,0:T(8,128)(2,1)S(1)} async-done(((bf16[8,136,256]{2,1,0:T(8,128)(2,1)}), bf16[8,136,256]{2,1,0:T(8,128)(2,1)S(1)}, u32[]{:S(2)}, u32[]{:S(2)}) %all-to-all-start) | async-done | bytes 557088 | tf_op jit(solution)/shard_map/all_to_all | solution.py:365
  23.7 0.8 %reduce.1 = (bf16[128,256]{1,0:T(8,128)(2,1)}, bf16[128,256]{1,0:T(8,128)(2,1)S(1)}) custom-call(bf16[8,136,256]{2,1,0:T(8,128)(2,1)S(1)} %all-to-all-done.parts), custom_call_target="tpu_custom_call" | custom-call | tf_op jit(solution)/shard_map/reduce/pallas_call | solution.py:379
  24.4 1.3 %collective-permute-start = (bf16[128,256]{1,0:T(8,128)(2,1)S(1)}, bf16[128,256]{1,0:T(8,128)(2,1)S(1)}, u32[]{:S(2)}, u32[]{:S(2)}) collective-permute-start(bf16[128,256]{1,0:T(8,128)(2,1)S(1)} %get-tuple-element.21), channel_id=1, source_target_pairs={{0,28},{1,29},{2,30},{3,31},{4,0},{5,1},{6,2},{7,3},{8,4},{9,5},{1... | collective-permute-start | bytes 196616 | tf_op jit(solution)/shard_map/ppermute | solution.py:401
  25.7 3.0 %collective-permute-done.1 = bf16[128,256]{1,0:T(8,128)(2,1)S(1)} collective-permute-done((bf16[128,256]{1,0:T(8,128)(2,1)S(1)}, bf16[128,256]{1,0:T(8,128)(2,1)S(1)}, u32[]{:S(2)}, u32[]{:S(2)}) %collective-permute-start.1) | collective-permute-done | bytes 65568 | tf_op jit(solution)/shard_map/ppermute | solution.py:389
  28.7 3.4 %collective-permute-done = bf16[128,256]{1,0:T(8,128)(2,1)S(1)} collective-permute-done((bf16[128,256]{1,0:T(8,128)(2,1)S(1)}, bf16[128,256]{1,0:T(8,128)(2,1)S(1)}, u32[]{:S(2)}, u32[]{:S(2)}) %collective-permute-start) | collective-permute-done | bytes 65568 | tf_op jit(solution)/shard_map/ppermute | solution.py:401
  32.1 0.1 collective-permute-start.6
  32.2 0.8 %collective-permute-start.5 = (bf16[256,256]{1,0:T(8,128)(2,1)S(1)}, bf16[256,256]{1,0:T(8,128)(2,1)S(1)}, u32[]{:S(2)}, u32[]{:S(2)}) collective-permute-start(bf16[256,256]{1,0:T(8,128)(2,1)S(1)} %get-tuple-element.22), channel_id=1, source_target_pairs={{0,2},{1,3},{2,0},{3,1},{4,6},{5,7},{6,4},{7,5},{8,10},{9,11},{10,... | collective-permute-start | bytes 393224 | tf_op jit(solution)/shard_map/ppermute | solution.py:392
  33.0 4.0 %collective-permute-start.2 = (bf16[256,256]{1,0:T(8,128)(2,1)S(1)}, bf16[256,256]{1,0:T(8,128)(2,1)S(1)}, u32[]{:S(2)}, u32[]{:S(2)}) collective-permute-start(bf16[256,256]{1,0:T(8,128)(2,1)S(1)} %get-tuple-element.22), channel_id=1, source_target_pairs={{0,8},{1,9},{2,10},{3,11},{4,12},{5,13},{6,14},{7,15},{8,16},{9,17... | collective-permute-start | bytes 393224 | tf_op jit(solution)/shard_map/ppermute | solution.py:389
  37.0 0.1 collective-permute-start.3
  37.1 5.4 %collective-permute-done.6 = bf16[256,256]{1,0:T(8,128)(2,1)S(1)} collective-permute-done((bf16[256,256]{1,0:T(8,128)(2,1)S(1)}, bf16[256,256]{1,0:T(8,128)(2,1)S(1)}, u32[]{:S(2)}, u32[]{:S(2)}) %collective-permute-start.6) | collective-permute-done | bytes 131104 | tf_op jit(solution)/shard_map/ppermute | solution.py:389
  42.5 2.0 %collective-permute-done.3 = bf16[128,256]{1,0:T(8,128)(2,1)S(1)} collective-permute-done((bf16[128,256]{1,0:T(8,128)(2,1)S(1)}, bf16[128,256]{1,0:T(8,128)(2,1)S(1)}, u32[]{:S(2)}, u32[]{:S(2)}) %collective-permute-start.3) | collective-permute-done | bytes 65568 | tf_op jit(solution)/shard_map/ppermute | solution.py:389
  44.5 2.9 %collective-permute-done.7 = bf16[256,256]{1,0:T(8,128)(2,1)S(1)} collective-permute-done((bf16[256,256]{1,0:T(8,128)(2,1)S(1)}, bf16[256,256]{1,0:T(8,128)(2,1)S(1)}, u32[]{:S(2)}, u32[]{:S(2)}) %collective-permute-start.7) | collective-permute-done | bytes 131104 | tf_op jit(solution)/shard_map/ppermute | solution.py:392
  47.5 0.1 collective-permute-start.8
  47.6 0.1 collective-permute-start.4
  47.7 2.1 %collective-permute-done.8.theirs = bf16[1408,256]{1,0:T(8,128)(2,1)S(1)} collective-permute-done((bf16[1408,256]{1,0:T(8,128)(2,1)S(1)}, bf16[1408,256]{1,0:T(8,128)(2,1)S(1)}, u32[]{:S(2)}, u32[]{:S(2)}) %collective-permute-start.8) | collective-permute-done | bytes 720928 | tf_op jit(solution)/shard_map/ppermute | solution.py:395
  49.8 5.8 %attend_near.1 = (f32[6,128,512]{2,1,0:T(8,128)S(1)}, f32[6,8,512]{2,1,0:T(8,128)S(1)}) custom-call(s32[1]{0:T(128)} %bitcast.place, s32[896]{0:T(1024)S(1)} %prepare.1.table, bf16[3,8,128,128]{3,2,1,0:T(8,128)(2,1)S(1)} %copy-done.1, f32[6,128,512]{2,1,0:T(8,128)S(1)} %get-tuple-element.24.old_state, ...), custom_call_target="tpu_custom_call", output_to_operand_aliasing={{0}: (3, {}), {1}: (4, {})} | custom-call | tf_op jit(solution)/shard_map/attend_near/pallas_call | solution.py:326
  55.6 0.3 collective-permute-start.9
  55.8 1.4 %collective-permute-done.9.theirs = bf16[384,256]{1,0:T(8,128)(2,1)S(1)} collective-permute-done((bf16[384,256]{1,0:T(8,128)(2,1)S(1)}, bf16[384,256]{1,0:T(8,128)(2,1)S(1)}, u32[]{:S(2)}, u32[]{:S(2)}) %collective-permute-start.9) | collective-permute-done | bytes 196640 | tf_op jit(solution)/shard_map/ppermute | solution.py:395
  57.3 4.8 %attend_far.1 = bf16[3,8,128,128]{3,2,1,0:T(8,128)(2,1)} custom-call(s32[1]{0:T(128)} %bitcast.place, s32[896]{0:T(1024)S(1)} %prepare.1.table, bf16[3,8,128,128]{3,2,1,0:T(8,128)(2,1)S(1)} %copy-done.1, f32[6,128,512]{2,1,0:T(8,128)S(1)} %get-tuple-element.28.state, f32[6,8,512]{2,1,0:T(8,128)S(1)} %get-tuple-element.29.sums, ...), custom_call_target="tpu_custom_call" | custom-call | tf_op jit(solution)/shard_map/attend_far/pallas_call | solution.py:341
  (24 shorter events, 0.2 us)
Async XLA Ops:
  0.6 11.1 %copy-start = (s32[3,64,16]{1,2,0:T(8,128)S(1)}, s32[3,64,16]{1,2,0:T(8,128)}, u32[]{:S(2)}) copy-start(s32[3,64,16]{1,2,0:T(8,128)} %param.13) | copy-start | bytes 36868
  0.6 11.3 %copy-start.2 = (bf16[3,1,128,256]{3,2,1,0:T(8,128)(2,1)S(1)}, bf16[3,1,128,256]{3,2,1,0:T(8,128)(2,1)}, u32[]{:S(2)}) copy-start(bf16[3,1,128,256]{3,2,1,0:T(8,128)(2,1)} %own.1) | copy-start | bytes 589828
  4.6 7.3 %copy-start.1 = (bf16[3,8,128,128]{3,2,1,0:T(8,128)(2,1)S(1)}, bf16[3,8,128,128]{3,2,1,0:T(8,128)(2,1)}, u32[]{:S(2)}) copy-start(bf16[3,8,128,128]{3,2,1,0:T(8,128)(2,1)} %q.5) | copy-start | bytes 2359300
  4.6 10.1 %copy-start.3 = (s32[4096]{0:T(1024)S(1)}, s32[4096]{0:T(1024)}, u32[]{:S(2)}) copy-start(s32[4096]{0:T(1024)} %param.12) | copy-start | bytes 49156
  4.7 19.0 %all-to-all-start = ((bf16[8,136,256]{2,1,0:T(8,128)(2,1)}), bf16[8,136,256]{2,1,0:T(8,128)(2,1)S(1)}, u32[]{:S(2)}, u32[]{:S(2)}) async-start(bf16[8,136,256]{2,1,0:T(8,128)(2,1)} %project.1), calls=%async_computation | async-start | bytes 1114112 | tf_op jit(solution)/shard_map/all_to_all | solution.py:365
  24.4 4.3 %collective-permute-start.1 = (bf16[128,256]{1,0:T(8,128)(2,1)S(1)}, bf16[128,256]{1,0:T(8,128)(2,1)S(1)}, u32[]{:S(2)}, u32[]{:S(2)}) collective-permute-start(bf16[128,256]{1,0:T(8,128)(2,1)S(1)} %get-tuple-element.21), channel_id=1, source_target_pairs={{0,4},{1,5},{2,6},{3,7},{4,8},{5,9},{6,10},{7,11},{8,12},{9,13},{1... | collective-permute-start | bytes 196616 | tf_op jit(solution)/shard_map/ppermute | solution.py:389
  24.4 7.7 %collective-permute-start = (bf16[128,256]{1,0:T(8,128)(2,1)S(1)}, bf16[128,256]{1,0:T(8,128)(2,1)S(1)}, u32[]{:S(2)}, u32[]{:S(2)}) collective-permute-start(bf16[128,256]{1,0:T(8,128)(2,1)S(1)} %get-tuple-element.21), channel_id=1, source_target_pairs={{0,28},{1,29},{2,30},{3,31},{4,0},{5,1},{6,2},{7,3},{8,4},{9,5},{1... | collective-permute-start | bytes 196616 | tf_op jit(solution)/shard_map/ppermute | solution.py:401
  32.1 10.4 %collective-permute-start.6 = (bf16[256,256]{1,0:T(8,128)(2,1)S(1)}, bf16[256,256]{1,0:T(8,128)(2,1)S(1)}, u32[]{:S(2)}, u32[]{:S(2)}) collective-permute-start(bf16[256,256]{1,0:T(8,128)(2,1)S(1)} %get-tuple-element.23), channel_id=1, source_target_pairs={{0,24},{1,25},{2,26},{3,27},{4,28},{5,29},{6,30},{7,31},{8,0},{9,1... | collective-permute-start | bytes 393224 | tf_op jit(solution)/shard_map/ppermute | solution.py:389
  32.2 10.3 %collective-permute-start.5 = (bf16[256,256]{1,0:T(8,128)(2,1)S(1)}, bf16[256,256]{1,0:T(8,128)(2,1)S(1)}, u32[]{:S(2)}, u32[]{:S(2)}) collective-permute-start(bf16[256,256]{1,0:T(8,128)(2,1)S(1)} %get-tuple-element.22), channel_id=1, source_target_pairs={{0,2},{1,3},{2,0},{3,1},{4,6},{5,7},{6,4},{7,5},{8,10},{9,11},{10,... | collective-permute-start | bytes 393224 | tf_op jit(solution)/shard_map/ppermute | solution.py:392
  33.0 9.6 %collective-permute-start.2 = (bf16[256,256]{1,0:T(8,128)(2,1)S(1)}, bf16[256,256]{1,0:T(8,128)(2,1)S(1)}, u32[]{:S(2)}, u32[]{:S(2)}) collective-permute-start(bf16[256,256]{1,0:T(8,128)(2,1)S(1)} %get-tuple-element.22), channel_id=1, source_target_pairs={{0,8},{1,9},{2,10},{3,11},{4,12},{5,13},{6,14},{7,15},{8,16},{9,17... | collective-permute-start | bytes 393224 | tf_op jit(solution)/shard_map/ppermute | solution.py:389
  37.0 7.5 %collective-permute-start.3 = (bf16[128,256]{1,0:T(8,128)(2,1)S(1)}, bf16[128,256]{1,0:T(8,128)(2,1)S(1)}, u32[]{:S(2)}, u32[]{:S(2)}) collective-permute-start(bf16[128,256]{1,0:T(8,128)(2,1)S(1)} %slice.3), channel_id=1, source_target_pairs={{0,20},{1,21},{2,22},{3,23},{4,24},{5,25},{6,26},{7,27},{8,28},{9,... | collective-permute-start | bytes 196616 | tf_op jit(solution)/shard_map/ppermute | solution.py:389
  42.5 5.0 %collective-permute-start.7 = (bf16[256,256]{1,0:T(8,128)(2,1)S(1)}, bf16[256,256]{1,0:T(8,128)(2,1)S(1)}, u32[]{:S(2)}, u32[]{:S(2)}) collective-permute-start(bf16[256,256]{1,0:T(8,128)(2,1)S(1)} %collective-permute-done.6), channel_id=1, source_target_pairs={{0,2},{1,3},{2,0},{3,1},{4,6},{5,7},{6,4},{7,5},{8,10},{9,11},{10,... | collective-permute-start | bytes 393224 | tf_op jit(solution)/shard_map/ppermute | solution.py:392
  47.5 2.3 %collective-permute-start.8 = (bf16[1408,256]{1,0:T(8,128)(2,1)S(1)}, bf16[1408,256]{1,0:T(8,128)(2,1)S(1)}, u32[]{:S(2)}, u32[]{:S(2)}) collective-permute-start(bf16[1408,256]{1,0:T(8,128)(2,1)S(1)} %constant_dynamic-update-slice_fusion.mine), channel_id=1, source_target_pairs={{0,1},{1,0},{2,3},{3,2},{4,5},{5,4},{6,7},{7,6},{8,9},{9,8},{10,11... | collective-permute-start | bytes 2162696 | tf_op jit(solution)/shard_map/ppermute | solution.py:395
  47.6 8.0 %collective-permute-start.4 = (bf16[384,256]{1,0:T(8,128)(2,1)S(1)}, bf16[384,256]{1,0:T(8,128)(2,1)S(1)}, u32[]{:S(2)}, u32[]{:S(2)}) collective-permute-start(bf16[384,256]{1,0:T(8,128)(2,1)S(1)} %pad_maximum_fusion), channel_id=1, source_target_pairs={{0,2},{1,3},{2,0},{3,1},{4,6},{5,7},{6,4},{7,5},{8,10},{9,11},{10,... | collective-permute-start | bytes 589832 | tf_op jit(solution)/shard_map/ppermute | solution.py:392
  55.6 1.7 %collective-permute-start.9 = (bf16[384,256]{1,0:T(8,128)(2,1)S(1)}, bf16[384,256]{1,0:T(8,128)(2,1)S(1)}, u32[]{:S(2)}, u32[]{:S(2)}) collective-permute-start(bf16[384,256]{1,0:T(8,128)(2,1)S(1)} %collective-permute-done.4.mine), channel_id=1, source_target_pairs={{0,1},{1,0},{2,3},{3,2},{4,5},{5,4},{6,7},{7,6},{8,9},{9,8},{10,11... | collective-permute-start | bytes 589832 | tf_op jit(solution)/shard_map/ppermute | solution.py:395

commit v8 on v7

--- a/solution.py
+++ b/solution.py
@@ -397,14 +397,14 @@
     def join(*arrays):
         return jnp.concatenate(arrays, axis=0)
 
-    moves = [(4 * z + i, (4 * z - 4) % seqs + i) for z in range(4) for i in range(4)]
+    moves = [(4 * z + i, (4 * z - 4) % seqs + i) for z in range(3) for i in range(4)]
     down1 = lax.ppermute(kv, "seq", moves)
     up1 = along_z(kv, 1)
     high, low = lax.optimization_barrier((join(kv, down1), join(kv, up1)))
     down23 = along_z(high, -2)
     up23 = along_z(low, 2)
     low_y = along_y(low)
-    up4 = along_z(high[tok_dev:], -3)
+    up4 = along_z(low[:tok_dev], 4)
     falling = join(down23, along_y(down23))
     rising = join(up23, up4)
     far = along_y(rising)

time: 62.3 us -> 61.7 us (level)
  the two profiles are of different devices: /device:TPU:224 before, /device:TPU:105 now
where the time goes in v8:
time: 61.7 us; the launch traced here: 60.7 us
  starting transfers between devices  26.2 us (42%)
  Pallas kernels  21.4 us (35%)
  waiting for transfers between devices  11.9 us (19%)
  between operations  0.93 us (2%)
    ppermute x4, starting transfers between devices, along_z(): return lax.ppermute(x, 'seq', [(i, (i + 4 * levels) % seqs) for i in every])  12.8 us
    all_to_all x1, starting transfers between devices, per_device(): parts = lax.all_to_all(partial, 'section', 0, 0, tiled=True)  5.89 us
    pallas_call x1, Pallas kernels, attend_near(): pl.pallas_call(functools.partial(near_kernel, blocks_dev), in_specs=[SMEM...  5.69 us
    all_to_all x1, waiting for transfers between devices, per_device(): parts = lax.all_to_all(partial, 'section', 0, 0, tiled=True)  5.03 us
    ppermute x2, starting transfers between devices, along_core(): return lax.ppermute(x, 'seq', [(i, i ^ 1) for i in every])  4.87 us
    pallas_call x1, Pallas kernels, attend_far(): pl.pallas_call(functools.partial(far_kernel, blocks_dev), in_specs=[SMEM_...  4.17 us
    pallas_call x1, Pallas kernels, per_device(): pl.pallas_call(functools.partial(prepare_kernel, blocks_dev), in_specs=[S...  4.02 us
    pallas_call x1, Pallas kernels, project(): pl.pallas_call(project_kernel, in_specs=[anywhere] * 3, out_specs=pl.Bloc...  3.97 us
  transfers between devices with their start and end apart: 11, of which 7 were waited for; matrix products, arithmetic and copies ran while one was open for 0% of the time, Pallas kernels for 21%

profile of v8, /device:TPU:105, one launch (start us, length us, event | category | flops | bytes accessed | tf_op | source)
XLA Modules:
  0.0 60.7 jit_solution(4674834967269365781)
XLA Ops:
  0.7 4.0 %project.1 = bf16[8,136,256]{2,1,0:T(8,128)(2,1)} custom-call(bf16[128,1024]{1,0:T(8,128)(2,1)} %feat_hbm.1, f32[1,1024]{1,0:T(1,128)} %bitcast.5, bf16[1024,2048]{1,0:T(8,128)(2,1)} %weight_hbm.1), custom_call_target="tpu_custom_call" | custom-call | tf_op jit(solution)/shard_map/project/pallas_call | solution.py:70
  4.7 5.9 %all-to-all-start = ((bf16[8,136,256]{2,1,0:T(8,128)(2,1)}), bf16[8,136,256]{2,1,0:T(8,128)(2,1)S(1)}, u32[]{:S(2)}, u32[]{:S(2)}) async-start(bf16[8,136,256]{2,1,0:T(8,128)(2,1)} %project.1), calls=%async_computation | async-start | bytes 1114112 | tf_op jit(solution)/shard_map/all_to_all | solution.py:365
  10.7 2.8 %attend_own.1 = (f32[6,128,512]{2,1,0:T(8,128)S(1)}, f32[6,8,512]{2,1,0:T(8,128)S(1)}) custom-call(bf16[3,8,128,128]{3,2,1,0:T(8,128)(2,1)S(1)} %copy-done.1, bf16[3,1,128,256]{3,2,1,0:T(8,128)(2,1)S(1)} %copy-done.2), custom_call_target="tpu_custom_call" | custom-call | tf_op jit(solution)/shard_map/attend_own/pallas_call | solution.py:315
  13.5 4.0 %prepare.1.table = s32[896]{0:T(1024)S(1)} custom-call(s32[1]{0:T(128)} %bitcast.place, s32[6,16]{1,0:T(8,128)S(1)} %reshape.18.lists, s32[32,128]{1,0:T(8,128)S(1)} %bitcast.4), custom_call_target="tpu_custom_call" | custom-call | tf_op jit(solution)/shard_map/prepare/pallas_call | solution.py:367
  17.6 5.0 %all-to-all-done.parts = bf16[8,136,256]{2,1,0:T(8,128)(2,1)S(1)} async-done(((bf16[8,136,256]{2,1,0:T(8,128)(2,1)}), bf16[8,136,256]{2,1,0:T(8,128)(2,1)S(1)}, u32[]{:S(2)}, u32[]{:S(2)}) %all-to-all-start) | async-done | bytes 557088 | tf_op jit(solution)/shard_map/all_to_all | solution.py:365
  22.6 0.8 %reduce.1 = (bf16[128,256]{1,0:T(8,128)(2,1)}, bf16[128,256]{1,0:T(8,128)(2,1)S(1)}) custom-call(bf16[8,136,256]{2,1,0:T(8,128)(2,1)S(1)} %all-to-all-done.parts), custom_call_target="tpu_custom_call" | custom-call | tf_op jit(solution)/shard_map/reduce/pallas_call | solution.py:379
  23.3 2.9 %collective-permute-start.1 = (bf16[128,256]{1,0:T(8,128)(2,1)S(1)}, bf16[128,256]{1,0:T(8,128)(2,1)S(1)}, u32[]{:S(2)}, u32[]{:S(2)}) collective-permute-start(bf16[128,256]{1,0:T(8,128)(2,1)S(1)} %get-tuple-element.21), channel_id=1, source_target_pairs={{0,4},{1,5},{2,6},{3,7},{4,8},{5,9},{6,10},{7,11},{8,12},{9,13},{1... | collective-permute-start | bytes 196616 | tf_op jit(solution)/shard_map/ppermute | solution.py:389
  26.2 0.7 %collective-permute-start = (bf16[128,256]{1,0:T(8,128)(2,1)S(1)}, bf16[128,256]{1,0:T(8,128)(2,1)S(1)}, u32[]{:S(2)}, u32[]{:S(2)}) collective-permute-start(bf16[128,256]{1,0:T(8,128)(2,1)S(1)} %get-tuple-element.21), channel_id=1, source_target_pairs={{0,28},{1,29},{2,30},{3,31},{4,0},{5,1},{6,2},{7,3},{8,4},{9,5},{1... | collective-permute-start | bytes 196616 | tf_op jit(solution)/shard_map/ppermute | solution.py:401
  26.9 0.7 %collective-permute-done.1 = bf16[128,256]{1,0:T(8,128)(2,1)S(1)} collective-permute-done((bf16[128,256]{1,0:T(8,128)(2,1)S(1)}, bf16[128,256]{1,0:T(8,128)(2,1)S(1)}, u32[]{:S(2)}, u32[]{:S(2)}) %collective-permute-start.1) | collective-permute-done | bytes 65568 | tf_op jit(solution)/shard_map/ppermute | solution.py:389
  27.6 1.9 %collective-permute-start.6 = (bf16[256,256]{1,0:T(8,128)(2,1)S(1)}, bf16[256,256]{1,0:T(8,128)(2,1)S(1)}, u32[]{:S(2)}, u32[]{:S(2)}) collective-permute-start(bf16[256,256]{1,0:T(8,128)(2,1)S(1)} %get-tuple-element.25), channel_id=1, source_target_pairs={{0,24},{1,25},{2,26},{3,27},{4,28},{5,29},{6,30},{7,31},{8,0},{9,1... | collective-permute-start | bytes 393224 | tf_op jit(solution)/shard_map/ppermute | solution.py:389
  29.5 1.1 %collective-permute-start.5 = (bf16[256,256]{1,0:T(8,128)(2,1)S(1)}, bf16[256,256]{1,0:T(8,128)(2,1)S(1)}, u32[]{:S(2)}, u32[]{:S(2)}) collective-permute-start(bf16[256,256]{1,0:T(8,128)(2,1)S(1)} %get-tuple-element.22), channel_id=1, source_target_pairs={{0,2},{1,3},{2,0},{3,1},{4,6},{5,7},{6,4},{7,5},{8,10},{9,11},{10,... | collective-permute-start | bytes 393224 | tf_op jit(solution)/shard_map/ppermute | solution.py:392
  30.5 1.8 %collective-permute-start.2 = (bf16[256,256]{1,0:T(8,128)(2,1)S(1)}, bf16[256,256]{1,0:T(8,128)(2,1)S(1)}, u32[]{:S(2)}, u32[]{:S(2)}) collective-permute-start(bf16[256,256]{1,0:T(8,128)(2,1)S(1)} %get-tuple-element.22), channel_id=1, source_target_pairs={{0,8},{1,9},{2,10},{3,11},{4,12},{5,13},{6,14},{7,15},{8,16},{9,17... | collective-permute-start | bytes 393224 | tf_op jit(solution)/shard_map/ppermute | solution.py:389
  32.3 6.3 %collective-permute-start.3 = (bf16[128,256]{1,0:T(8,128)(2,1)S(1)}, bf16[128,256]{1,0:T(8,128)(2,1)S(1)}, u32[]{:S(2)}, u32[]{:S(2)}) collective-permute-start(bf16[128,256]{1,0:T(8,128)(2,1)S(1)} %slice.3), channel_id=1, source_target_pairs={{0,16},{1,17},{2,18},{3,19},{4,20},{5,21},{6,22},{7,23},{8,24},{9,... | collective-permute-start | bytes 196616 | tf_op jit(solution)/shard_map/ppermute | solution.py:389
  38.6 0.4 collective-permute-start.7
  39.1 1.5 %collective-permute-done.2 = bf16[256,256]{1,0:T(8,128)(2,1)S(1)} collective-permute-done((bf16[256,256]{1,0:T(8,128)(2,1)S(1)}, bf16[256,256]{1,0:T(8,128)(2,1)S(1)}, u32[]{:S(2)}, u32[]{:S(2)}) %collective-permute-start.2) | collective-permute-done | bytes 131104 | tf_op jit(solution)/shard_map/ppermute | solution.py:389
  40.6 0.4 collective-permute-done.3
  41.0 1.7 %collective-permute-done.7 = bf16[256,256]{1,0:T(8,128)(2,1)S(1)} collective-permute-done((bf16[256,256]{1,0:T(8,128)(2,1)S(1)}, bf16[256,256]{1,0:T(8,128)(2,1)S(1)}, u32[]{:S(2)}, u32[]{:S(2)}) %collective-permute-start.7) | collective-permute-done | bytes 131104 | tf_op jit(solution)/shard_map/ppermute | solution.py:392
  42.8 4.4 %collective-permute-start.8 = (bf16[1408,256]{1,0:T(8,128)(2,1)S(1)}, bf16[1408,256]{1,0:T(8,128)(2,1)S(1)}, u32[]{:S(2)}, u32[]{:S(2)}) collective-permute-start(bf16[1408,256]{1,0:T(8,128)(2,1)S(1)} %constant_dynamic-update-slice_fusion.mine), channel_id=1, source_target_pairs={{0,1},{1,0},{2,3},{3,2},{4,5},{5,4},{6,7},{7,6},{8,9},{9,8},{10,11... | collective-permute-start | bytes 2162696 | tf_op jit(solution)/shard_map/ppermute | solution.py:395
  47.1 0.5 collective-permute-start.4
  47.6 1.3 %collective-permute-done.8.theirs = bf16[1408,256]{1,0:T(8,128)(2,1)S(1)} collective-permute-done((bf16[1408,256]{1,0:T(8,128)(2,1)S(1)}, bf16[1408,256]{1,0:T(8,128)(2,1)S(1)}, u32[]{:S(2)}, u32[]{:S(2)}) %collective-permute-start.8) | collective-permute-done | bytes 720928 | tf_op jit(solution)/shard_map/ppermute | solution.py:395
  48.9 5.7 %attend_near.1 = (f32[6,128,512]{2,1,0:T(8,128)S(1)}, f32[6,8,512]{2,1,0:T(8,128)S(1)}) custom-call(s32[1]{0:T(128)} %bitcast.place, s32[896]{0:T(1024)S(1)} %prepare.1.table, bf16[3,8,128,128]{3,2,1,0:T(8,128)(2,1)S(1)} %copy-done.1, f32[6,128,512]{2,1,0:T(8,128)S(1)} %get-tuple-element.23.old_state, ...), custom_call_target="tpu_custom_call", output_to_operand_aliasing={{0}: (3, {}), {1}: (4, {})} | custom-call | tf_op jit(solution)/shard_map/attend_near/pallas_call | solution.py:326
  54.6 0.5 collective-permute-start.9
  55.2 1.2 %collective-permute-done.9.theirs = bf16[384,256]{1,0:T(8,128)(2,1)S(1)} collective-permute-done((bf16[384,256]{1,0:T(8,128)(2,1)S(1)}, bf16[384,256]{1,0:T(8,128)(2,1)S(1)}, u32[]{:S(2)}, u32[]{:S(2)}) %collective-permute-start.9) | collective-permute-done | bytes 196640 | tf_op jit(solution)/shard_map/ppermute | solution.py:395
  56.4 4.2 %attend_far.1 = bf16[3,8,128,128]{3,2,1,0:T(8,128)(2,1)} custom-call(s32[1]{0:T(128)} %bitcast.place, s32[896]{0:T(1024)S(1)} %prepare.1.table, bf16[3,8,128,128]{3,2,1,0:T(8,128)(2,1)S(1)} %copy-done.1, f32[6,128,512]{2,1,0:T(8,128)S(1)} %get-tuple-element.28.state, f32[6,8,512]{2,1,0:T(8,128)S(1)} %get-tuple-element.29.sums, ...), custom_call_target="tpu_custom_call" | custom-call | tf_op jit(solution)/shard_map/attend_far/pallas_call | solution.py:341
  (24 shorter events, 0.3 us)
Async XLA Ops:
  0.6 9.9 %copy-start = (s32[3,64,16]{1,2,0:T(8,128)S(1)}, s32[3,64,16]{1,2,0:T(8,128)}, u32[]{:S(2)}) copy-start(s32[3,64,16]{1,2,0:T(8,128)} %param.13) | copy-start | bytes 36868
  0.6 10.1 %copy-start.2 = (bf16[3,1,128,256]{3,2,1,0:T(8,128)(2,1)S(1)}, bf16[3,1,128,256]{3,2,1,0:T(8,128)(2,1)}, u32[]{:S(2)}) copy-start(bf16[3,1,128,256]{3,2,1,0:T(8,128)(2,1)} %own.1) | copy-start | bytes 589828
  4.6 6.1 %copy-start.1 = (bf16[3,8,128,128]{3,2,1,0:T(8,128)(2,1)S(1)}, bf16[3,8,128,128]{3,2,1,0:T(8,128)(2,1)}, u32[]{:S(2)}) copy-start(bf16[3,8,128,128]{3,2,1,0:T(8,128)(2,1)} %q.5) | copy-start | bytes 2359300
  4.6 8.9 %copy-start.3 = (s32[4096]{0:T(1024)S(1)}, s32[4096]{0:T(1024)}, u32[]{:S(2)}) copy-start(s32[4096]{0:T(1024)} %param.12) | copy-start | bytes 49156
  4.7 17.9 %all-to-all-start = ((bf16[8,136,256]{2,1,0:T(8,128)(2,1)}), bf16[8,136,256]{2,1,0:T(8,128)(2,1)S(1)}, u32[]{:S(2)}, u32[]{:S(2)}) async-start(bf16[8,136,256]{2,1,0:T(8,128)(2,1)} %project.1), calls=%async_computation | async-start | bytes 1114112 | tf_op jit(solution)/shard_map/all_to_all | solution.py:365
  23.3 4.2 %collective-permute-start.1 = (bf16[128,256]{1,0:T(8,128)(2,1)S(1)}, bf16[128,256]{1,0:T(8,128)(2,1)S(1)}, u32[]{:S(2)}, u32[]{:S(2)}) collective-permute-start(bf16[128,256]{1,0:T(8,128)(2,1)S(1)} %get-tuple-element.21), channel_id=1, source_target_pairs={{0,4},{1,5},{2,6},{3,7},{4,8},{5,9},{6,10},{7,11},{8,12},{9,13},{1... | collective-permute-start | bytes 196616 | tf_op jit(solution)/shard_map/ppermute | solution.py:389
  26.2 1.3 %collective-permute-start = (bf16[128,256]{1,0:T(8,128)(2,1)S(1)}, bf16[128,256]{1,0:T(8,128)(2,1)S(1)}, u32[]{:S(2)}, u32[]{:S(2)}) collective-permute-start(bf16[128,256]{1,0:T(8,128)(2,1)S(1)} %get-tuple-element.21), channel_id=1, source_target_pairs={{0,28},{1,29},{2,30},{3,31},{4,0},{5,1},{6,2},{7,3},{8,4},{9,5},{1... | collective-permute-start | bytes 196616 | tf_op jit(solution)/shard_map/ppermute | solution.py:401
  27.6 11.1 %collective-permute-start.6 = (bf16[256,256]{1,0:T(8,128)(2,1)S(1)}, bf16[256,256]{1,0:T(8,128)(2,1)S(1)}, u32[]{:S(2)}, u32[]{:S(2)}) collective-permute-start(bf16[256,256]{1,0:T(8,128)(2,1)S(1)} %get-tuple-element.25), channel_id=1, source_target_pairs={{0,24},{1,25},{2,26},{3,27},{4,28},{5,29},{6,30},{7,31},{8,0},{9,1... | collective-permute-start | bytes 393224 | tf_op jit(solution)/shard_map/ppermute | solution.py:389
  29.5 9.6 %collective-permute-start.5 = (bf16[256,256]{1,0:T(8,128)(2,1)S(1)}, bf16[256,256]{1,0:T(8,128)(2,1)S(1)}, u32[]{:S(2)}, u32[]{:S(2)}) collective-permute-start(bf16[256,256]{1,0:T(8,128)(2,1)S(1)} %get-tuple-element.22), channel_id=1, source_target_pairs={{0,2},{1,3},{2,0},{3,1},{4,6},{5,7},{6,4},{7,5},{8,10},{9,11},{10,... | collective-permute-start | bytes 393224 | tf_op jit(solution)/shard_map/ppermute | solution.py:392
  30.5 10.1 %collective-permute-start.2 = (bf16[256,256]{1,0:T(8,128)(2,1)S(1)}, bf16[256,256]{1,0:T(8,128)(2,1)S(1)}, u32[]{:S(2)}, u32[]{:S(2)}) collective-permute-start(bf16[256,256]{1,0:T(8,128)(2,1)S(1)} %get-tuple-element.22), channel_id=1, source_target_pairs={{0,8},{1,9},{2,10},{3,11},{4,12},{5,13},{6,14},{7,15},{8,16},{9,17... | collective-permute-start | bytes 393224 | tf_op jit(solution)/shard_map/ppermute | solution.py:389
  32.3 8.7 %collective-permute-start.3 = (bf16[128,256]{1,0:T(8,128)(2,1)S(1)}, bf16[128,256]{1,0:T(8,128)(2,1)S(1)}, u32[]{:S(2)}, u32[]{:S(2)}) collective-permute-start(bf16[128,256]{1,0:T(8,128)(2,1)S(1)} %slice.3), channel_id=1, source_target_pairs={{0,16},{1,17},{2,18},{3,19},{4,20},{5,21},{6,22},{7,23},{8,24},{9,... | collective-permute-start | bytes 196616 | tf_op jit(solution)/shard_map/ppermute | solution.py:389
  38.6 4.1 %collective-permute-start.7 = (bf16[256,256]{1,0:T(8,128)(2,1)S(1)}, bf16[256,256]{1,0:T(8,128)(2,1)S(1)}, u32[]{:S(2)}, u32[]{:S(2)}) collective-permute-start(bf16[256,256]{1,0:T(8,128)(2,1)S(1)} %collective-permute-done.6), channel_id=1, source_target_pairs={{0,2},{1,3},{2,0},{3,1},{4,6},{5,7},{6,4},{7,5},{8,10},{9,11},{10,... | collective-permute-start | bytes 393224 | tf_op jit(solution)/shard_map/ppermute | solution.py:392
  42.8 6.2 %collective-permute-start.8 = (bf16[1408,256]{1,0:T(8,128)(2,1)S(1)}, bf16[1408,256]{1,0:T(8,128)(2,1)S(1)}, u32[]{:S(2)}, u32[]{:S(2)}) collective-permute-start(bf16[1408,256]{1,0:T(8,128)(2,1)S(1)} %constant_dynamic-update-slice_fusion.mine), channel_id=1, source_target_pairs={{0,1},{1,0},{2,3},{3,2},{4,5},{5,4},{6,7},{7,6},{8,9},{9,8},{10,11... | collective-permute-start | bytes 2162696 | tf_op jit(solution)/shard_map/ppermute | solution.py:395
  47.1 7.5 %collective-permute-start.4 = (bf16[384,256]{1,0:T(8,128)(2,1)S(1)}, bf16[384,256]{1,0:T(8,128)(2,1)S(1)}, u32[]{:S(2)}, u32[]{:S(2)}) collective-permute-start(bf16[384,256]{1,0:T(8,128)(2,1)S(1)} %pad_maximum_fusion), channel_id=1, source_target_pairs={{0,2},{1,3},{2,0},{3,1},{4,6},{5,7},{6,4},{7,5},{8,10},{9,11},{10,... | collective-permute-start | bytes 589832 | tf_op jit(solution)/shard_map/ppermute | solution.py:392
  54.6 1.7 %collective-permute-start.9 = (bf16[384,256]{1,0:T(8,128)(2,1)S(1)}, bf16[384,256]{1,0:T(8,128)(2,1)S(1)}, u32[]{:S(2)}, u32[]{:S(2)}) collective-permute-start(bf16[384,256]{1,0:T(8,128)(2,1)S(1)} %collective-permute-done.4.mine), channel_id=1, source_target_pairs={{0,1},{1,0},{2,3},{3,2},{4,5},{5,4},{6,7},{7,6},{8,9},{9,8},{10,11... | collective-permute-start | bytes 589832 | tf_op jit(solution)/shard_map/ppermute | solution.py:395
